TPU v7x, 32 devices: a whole 2x2x4 slice. The times are simulated.
32 devices in a mesh: orb: 16 (over z, x, core), aux: 2 (over y).
Axes of the slice: x: 2, y: 2, z: 4, core: 2. Of those that a mesh axis runs over, the one named last changes fastest.
Arguments:
- three_index: float32 [56, 1024, 2048], P(None, 'aux', 'orb'), may hold values from -0.5 to 0.5
- pair_density: float32 [3136, 3136], P('orb'), as said below
- active_orbitals: int32 [56], replicated, may hold values from 200 to 2047, as said below
- screen_mask: int32 [64, 128], P('aux', 'orb'), may hold values from 0 to 1
- one_density: float32 [56, 56], replicated
- inactive_fock: float32 [2048, 256], P('orb'), may hold values from -6 to 6
- active_fock: float32 [2048, 200], P('orb'), may hold values from -6 to 6
Outputs:
- rotation_gradient: float32 [2048, 256], P(('orb', 'aux'))
Inputs may be any that keep to these rules, and one draw needn't show every extreme that they name: `active_orbitals`: 56 distinct orbital indices. pair_density is symmetric: its entry at (tu, vw) equals that at (vw, tu).
All inputs are finite; a program needn't handle non-finite values.
Results may differ from a plain program's by a relative error of at most 0.0001.
Values sent between devices are 32-bit elements; how exact they have to be, the bound alone decides.
No kernel may reach another device: no remote copies, remote signals or barrier semaphores. Data moves between devices by JAX's collectives and lax.ppermute only.
A program may use at most 128 MiB of HBM per device.

v0:
```python
import jax
import jax.numpy as jnp
from jax import lax
from jax.sharding import PartitionSpec as P


def shards(
    three_index, pair_density, active_orbitals, screen_mask, one_density, inactive_fock, active_fock
):
    highest = lax.Precision.HIGHEST
    act_count = three_index.shape[0]
    slab_count = three_index.shape[1]
    row_count = three_index.shape[2]
    inactive_count = active_fock.shape[1]
    orb_position = lax.axis_index("orb")
    kept_mask = jnp.repeat(
        jnp.repeat(screen_mask.astype(jnp.float32), slab_count // screen_mask.shape[0], axis=0),
        row_count // screen_mask.shape[1],
        axis=1,
    )
    screened = three_index * kept_mask[None]
    global_rows = orb_position * row_count + jnp.arange(row_count, dtype=jnp.int32)
    active_pick = (global_rows[:, None] == active_orbitals[None, :]).astype(jnp.float32)
    partial_pairs = jnp.einsum("wPp,pv->Pvw", screened, active_pick, precision=highest).reshape(
        slab_count, act_count * act_count
    )
    pairs = lax.psum(partial_pairs, "orb")
    column_block = jnp.dot(pairs, pair_density.T, precision=highest)
    half = lax.all_gather(column_block, "orb", axis=1, tiled=True)
    q_partial = jnp.einsum(
        "uPp,Ptu->pt", screened, half.reshape(slab_count, act_count, act_count), precision=highest
    )
    occ_index = jnp.concatenate([jnp.arange(inactive_count, dtype=jnp.int32), active_orbitals])
    row_share = row_count // lax.axis_size("aux")
    aux_offset = lax.axis_index("aux") * row_share
    qmatrix = lax.psum(q_partial, "aux")
    inactive_cols = 2.0 * (inactive_fock[:, :inactive_count] + active_fock)
    active_cols = (
        jnp.dot(inactive_fock[:, inactive_count:], one_density, precision=highest) + qmatrix
    )
    fock = jnp.concatenate([inactive_cols, active_cols], axis=1)
    occ_pick = (global_rows[:, None] == occ_index[None, :]).astype(jnp.float32)
    occupied = lax.psum(jnp.dot(occ_pick.T, fock, precision=highest), "orb")
    fock_mine = lax.dynamic_slice_in_dim(fock, aux_offset, row_share, 0)
    pick_mine = lax.dynamic_slice_in_dim(occ_pick, aux_offset, row_share, 0)
    transposed = jnp.dot(pick_mine, occupied.T, precision=highest)
    return 2.0 * (fock_mine - transposed)


def solution(mesh):
    in_specs = (
        P(None, "aux", "orb"),
        P("orb", None),
        P(),
        P("aux", "orb"),
        P(),
        P("orb", None),
        P("orb", None),
    )
    out_specs = P(("orb", "aux"), None)
    return jax.shard_map(shards, mesh=mesh, in_specs=in_specs, out_specs=out_specs, check_vma=False)
```

profile of v0, /device:TPU:0, one launch (start us, length us, event | category | flops | bytes accessed | tf_op | source)
XLA Modules:
  0.0 370.7 jit_solution(4190907556177980599)
XLA Ops:
  6.5 0.0 copy-start
  6.5 0.0 all-reduce.3.cloned.1.call-start
  6.5 0.8 convert_element_type.2
  7.4 0.1 broadcast_in_dim.4
  7.5 0.1 reshape.16
  7.6 0.1 copy.22
  7.8 13.4 %fusion.7 = f32[512,56,56]{0,1,2:T(8,128)S(1)} fusion(f32[56,512,128]{2,1,0:T(8,128)} %param.7, f32[512,128]{1,0:T(8,128)S(1)} %copy.22, s32[128]{0:T(128)S(1)} %iota_add_fusion, s32[56]{0:T(128)} %param.9), kind=kOutput, calls=%fused_computation.7 | convolution fusion | flops 2469927936 | bytes 21365472 | tf_op jit(solution)/shard_map/wPp,pv->Pvw/dot_general | solution.py:24
  21.2 6.4 %copy.23 = f32[512,56,56]{0,2,1:T(8,128)} copy(f32[512,56,56]{0,1,2:T(8,128)S(1)} %fusion.7) | data formatting | bytes 12845056 | tf_op jit(solution)/shard_map/wPp,pv->Pvw/transpose | solution.py:24
  27.6 0.0 all-reduce.3.cloned.1.call-update
  27.6 0.0 copy-start.2
  27.6 0.0 copy-start.4
  27.6 0.0 copy-start.1
  27.6 0.2 all-gather.3.cloned.1.call-start
  27.9 144.4 %all-reduce.3.cloned.1.call-done = f32[512,3136]{0,1:T(8,128)} async-done(((f32[512,3136]{0,1:T(8,128)}), f32[512,3136]{0,1:T(8,128)}) %all-reduce.3.cloned.1.call-update) | async-done | bytes 6422544 | tf_op jit(solution)/shard_map/psum | solution.py:27
  172.2 8.6 %convolution_bitcast_fusion = f32[1,196,512]{2,1,0:T(8,128)} fusion(f32[512,3136]{0,1:T(8,128)} %all-reduce.3.cloned.1.call-done, f32[196,3136]{1,0:T(8,128)S(1)} %copy-done), kind=kOutput, calls=%fused_computation.8 | convolution fusion | flops 3776446464 | bytes 9282560 | tf_op jit(solution)/shard_map/dot_general | solution.py:28
  180.8 0.0 all-gather.3.cloned.1.call-update
  180.9 0.0 all-reduce.5.cloned.1.call-start
  180.9 0.1 copy.21
  181.0 0.0 copy-done.4
  181.1 0.1 pad_add_fusion
  181.2 63.1 %all-gather.3.cloned.1.call-done = f32[16,196,512]{2,1,0:T(8,128)} async-done(((f32[1,196,512]{2,1,0:T(8,128)}), f32[16,196,512]{2,1,0:T(8,128)}) %all-gather.3.cloned.1.call-update) | async-done | bytes 6422544 | tf_op jit(solution)/shard_map/all_gather | solution.py:29
  244.2 6.1 %reshape.20 = f32[3136,512]{1,0:T(8,128)} reshape(f32[16,196,512]{2,1,0:T(8,128)} %all-gather.3.cloned.1.call-done) | data formatting | bytes 12845056
  250.3 15.4 %fusion.11 = f32[128,56]{0,1:T(8,128)S(1)} fusion(f32[512,56,56]{0,2,1:T(8,128)} %bitcast.23, f32[56,512,128]{2,1,0:T(8,128)} %param.7, f32[512,128]{1,0:T(8,128)S(1)} %copy.22), kind=kOutput, calls=%fused_computation.11 | convolution fusion | flops 2469920768 | bytes 21393408 | tf_op jit(solution)/shard_map/uPp,Ptu->pt/dot_general | solution.py:30
  265.7 8.3 %psum.22 = f32[128,56]{0,1:T(8,128)S(1)} all-reduce(f32[128,56]{0,1:T(8,128)S(1)} %fusion.11), channel_id=1, replica_groups=mesh['orb'=16,'aux'=2] {'aux'}, use_global_device_ids=true, to_apply=%region_1.0 | all-reduce | flops 7168 | bytes 57344 | tf_op jit(solution)/shard_map/psum | solution.py:36
  274.0 0.0 copy-done.3
  274.1 0.3 convolution_add_fusion
  274.4 0.1 copy.25
  274.5 1.1 fusion.16
  275.6 0.0 all-reduce.5.cloned.1.call-update
  275.6 0.1 broadcast_compare_fusion
  275.7 86.6 %all-reduce.5.cloned.1.call-done = f32[256,256]{1,0:T(8,128)} async-done(((f32[256,256]{1,0:T(8,128)}), f32[256,256]{1,0:T(8,128)}) %all-reduce.5.cloned.1.call-update) | async-done | bytes 262160 | tf_op jit(solution)/shard_map/psum | solution.py:43
  362.3 1.9 fusion.10
  (8 shorter events, 0.1 us)
Async XLA Ops:
  6.5 165.7 %copy-start = (f32[196,3136]{1,0:T(8,128)S(1)}, f32[196,3136]{1,0:T(8,128)}, u32[]{:S(2)}) copy-start(f32[196,3136]{1,0:T(8,128)} %param.8) | copy-start | bytes 7375876
  6.5 165.7 %all-reduce.3.cloned.1.call-start = ((), (), s32[]{:S(2)}) async-start(), calls=%async_computation | async-start | bytes 12845056 | tf_op jit(solution)/shard_map/psum | solution.py:27
  27.6 153.3 %copy-start.2 = (f32[128,200]{0,1:T(8,128)S(1)}, f32[128,200]{0,1:T(8,128)}, u32[]{:S(2)}) copy-start(f32[128,200]{0,1:T(8,128)} %param.13) | copy-start | bytes 307204
  27.6 153.4 %copy-start.4 = (s32[56]{0:T(128)S(1)}, s32[56]{0:T(128)}, u32[]{:S(2)}) copy-start(s32[56]{0:T(128)} %param.9) | copy-start | bytes 676
  27.6 153.5 %copy-start.1 = (f32[128,256]{1,0:T(8,128)S(1)}, f32[128,256]{1,0:T(8,128)}, u32[]{:S(2)}) copy-start(f32[128,256]{1,0:T(8,128)} %param.12) | copy-start | bytes 393220
  27.6 216.6 %all-gather.3.cloned.1.call-start = ((), (), s32[]{:S(2)}) async-start(), calls=%async_computation.2 | async-start | bytes 6963200 | tf_op jit(solution)/shard_map/all_gather | solution.py:29
  180.9 181.4 %all-reduce.5.cloned.1.call-start = ((), (), s32[]{:S(2)}) async-start(), calls=%async_computation.1 | async-start | bytes 524288 | tf_op jit(solution)/shard_map/psum | solution.py:43
  250.3 23.7 %copy-start.3 = (f32[56,56]{1,0:T(8,128)S(1)}, f32[56,56]{1,0:T(8,128)}, u32[]{:S(2)}) copy-start(f32[56,56]{1,0:T(8,128)} %param.11) | copy-start | bytes 37636
Sparse Core Ops, SparseCore 0:
  27.7 144.4 all-reduce.2
  181.0 63.1 all-gather.2
  275.7 86.5 all-reduce.4
where the time goes:
time: 371 us
  waiting for transfers between devices  294 us (79%)
  matrix products  40.7 us (11%)
  between operations  13.2 us (4%)
  local copies, waits for them, and re-layouts  13 us (4%)
  blocking collectives  8.33 us (2%)
    psum x1, waiting for transfers between devices, shards(): pairs = lax.psum(partial_pairs, 'orb')  144 us
    psum x1, waiting for transfers between devices, shards(): occupied = lax.psum(jnp.dot(occ_pick.T, fock, precision=highest), 'orb')  86.6 us
    all_gather x1, waiting for transfers between devices, shards(): half = lax.all_gather(column_block, 'orb', axis=1, tiled=True)  63.1 us
    dot_general x1, matrix products, shards(): jnp.einsum('uPp,Ptu->pt', screened, half.reshape(slab_count, act_count, a...  15.4 us
    dot_general x1, matrix products, shards(): jnp.einsum('wPp,pv->Pvw', screened, active_pick, precision=highest)  13.4 us
    dot_general x1, matrix products, shards(): column_block = jnp.dot(pairs, pair_density.T, precision=highest)  8.61 us
    psum x1, blocking collectives, shards(): qmatrix = lax.psum(q_partial, 'aux')  8.33 us
  transfers between devices with their start and end apart: 3, of which 3 were waited for; matrix products, arithmetic and copies ran while one was open for 0% of the time, Pallas kernels for 0%

commit v1 on v0

v1 whole, which is shorter than its diff:
```python
import functools

import jax
import jax.numpy as jnp
from jax import lax
from jax.experimental import pallas as pl
from jax.experimental.pallas import tpu as pltpu
from jax.sharding import PartitionSpec as P

HIGHEST = lax.Precision.HIGHEST
HIGH = lax.Precision.HIGH
LANES = 128
TILE = 8


def split(x):
    top = x.astype(jnp.bfloat16)
    return top, (x - top.astype(jnp.float32)).astype(jnp.bfloat16)


def mxu(a, b, contract):
    return lax.dot_general(a, b, (contract, ((), ())), preferred_element_type=jnp.float32)


def expand_mask(screen, quarter, chunk, rows):
    blocks, shells = screen.shape
    slab_rows = 4 * chunk // blocks
    row = lax.broadcasted_iota(jnp.int32, (chunk, blocks), 0) // slab_rows
    col = lax.broadcasted_iota(jnp.int32, (chunk, blocks), 1)
    down = (col == row + quarter * (blocks // 4)).astype(jnp.bfloat16)
    shell = lax.broadcasted_iota(jnp.int32, (shells, rows), 0)
    across = (shell == lax.broadcasted_iota(jnp.int32, (shells, rows), 1) // (rows // shells)).astype(jnp.bfloat16)
    nn = ((1,), (0,))
    tall = mxu(down, screen[...].astype(jnp.float32).astype(jnp.bfloat16), nn)
    return mxu(tall.astype(jnp.bfloat16), across, nn)


def extract_body(nb, info, active, three, screen, pairs, *refs):
    kept, pick, mask = refs[:-2], refs[-2], refs[-1]
    act, _, chunk = pairs.shape
    rows = three.shape[2]

    @pl.when(pl.program_id(0) == 0)
    def _():
        lane = lax.broadcasted_iota(jnp.int32, (1, rows), 1)
        for v in range(act):
            wanted = active[info[2 + v // nb] * nb + v % nb] - info[1]
            pick[v : v + 1, :rows] = (lane == wanted).astype(jnp.float32)
            pick[v : v + 1, rows:] = (lane == wanted).astype(jnp.float32)
        mask[...] = expand_mask(screen, info[0], chunk, rows)

    value = three[...] * mask[...][None]
    if kept:
        kept[0][...] = value
    top, low = split(value.reshape(TILE * chunk, rows))
    both = jnp.concatenate([top, low], axis=1)
    found = mxu(pick[...].astype(jnp.bfloat16), both, ((1,), (1,)))
    for w in range(TILE):
        pairs[:, w, :] = found[:, w * chunk : (w + 1) * chunk]


def extract(three_index, screen_mask, active, info, chunk, nb, keep):
    act, slab, rows = three_index.shape
    out_shape = [jax.ShapeDtypeStruct((act, act, chunk), jnp.float32)]
    out_specs = [pl.BlockSpec((act, TILE, chunk), lambda i, q, a: (0, i, 0))]
    if keep:
        out_shape.append(jax.ShapeDtypeStruct((act, chunk, rows), jnp.float32))
        out_specs.append(pl.BlockSpec((TILE, chunk, rows), lambda i, q, a: (i, 0, 0)))
    return pl.pallas_call(
        functools.partial(extract_body, nb),
        out_shape=out_shape,
        grid_spec=pltpu.PrefetchScalarGridSpec(
            num_scalar_prefetch=2,
            grid=(act // TILE,),
            in_specs=[
                pl.BlockSpec((TILE, chunk, rows), lambda i, q, a: (i, q[0], 0)),
                pl.BlockSpec(screen_mask.shape, lambda i, q, a: (0, 0)),
            ],
            out_specs=out_specs,
            scratch_shapes=[pltpu.VMEM((act, 2 * rows), jnp.float32), pltpu.VMEM((chunk, rows), jnp.float32)],
        ),
        cost_estimate=pl.CostEstimate(
            flops=4 * act * act * chunk * rows,
            transcendentals=0,
            bytes_accessed=4 * act * chunk * (act + rows * (2 if keep else 1)),
        ),
        name="extract",
    )(info, active, three_index, screen_mask)


def q_body(nb, info, three, screen, sib, *refs):
    blocks, out, lhs, acc, mask = refs[:-4], refs[-4], refs[-3], refs[-2], refs[-1]
    step = pl.program_id(0)
    rows = acc.shape[0]
    chunk = mask.shape[0]

    @pl.when(step == 0)
    def _():
        lhs[...] = jnp.zeros_like(lhs)
        acc[...] = jnp.zeros_like(acc)
        mask[...] = expand_mask(screen, info[0], chunk, mask.shape[1])

    for j, block in enumerate(blocks):
        for t in range(nb):
            lhs[pl.ds(j * TILE + t, TILE, stride=rows), :] = block[t]
    total = acc[...]
    for m in range(TILE // 2):
        pieces = [lhs[u * rows : (u + 1) * rows, :] for u in (2 * m, 2 * m + 1)]
        left, left_low = split(jnp.concatenate(pieces, axis=1))
        right = [jnp.concatenate([three[u] * mask[...], sib[u]], axis=1) for u in (2 * m, 2 * m + 1)]
        top, low = split(jnp.concatenate(right, axis=0))
        nn = ((1,), (0,))
        both = mxu(jnp.concatenate([left, left_low], axis=0), top, nn)
        total = total + (both[:rows] + both[rows:] + mxu(left, low, nn))
    acc[...] = total

    @pl.when(step == pl.num_programs(0) - 1)
    def _():
        for j in range(len(blocks)):
            where = pl.multiple_of(info[2 + j] * TILE, TILE)
            out[pl.ds(where, TILE), :] = acc[j * TILE : (j + 1) * TILE, :]


def q_partial(three_index, screen_mask, sib, blocks, info, chunk):
    act, slab, rows = three_index.shape
    count = len(blocks)
    nb = act // count
    in_specs = [
        pl.BlockSpec((TILE, chunk, rows), lambda i, q: (i, q[0], 0)),
        pl.BlockSpec(screen_mask.shape, lambda i, q: (0, 0)),
        pl.BlockSpec((TILE, chunk, rows), lambda i, q: (i, 0, 0)),
    ] + [pl.BlockSpec((nb, TILE, chunk), lambda i, q: (0, i, 0))] * count
    return pl.pallas_call(
        functools.partial(q_body, nb),
        out_shape=jax.ShapeDtypeStruct((count * TILE, 2 * rows), jnp.float32),
        grid_spec=pltpu.PrefetchScalarGridSpec(
            num_scalar_prefetch=1,
            grid=(act // TILE,),
            in_specs=in_specs,
            out_specs=pl.BlockSpec((count * TILE, 2 * rows), lambda i, q: (0, 0)),
            scratch_shapes=[
                pltpu.VMEM((TILE * count * TILE, chunk), jnp.float32),
                pltpu.VMEM((count * TILE, 2 * rows), jnp.float32),
                pltpu.VMEM((chunk, rows), jnp.float32),
            ],
        ),
        cost_estimate=pl.CostEstimate(
            flops=12 * act * act * chunk * rows,
            transcendentals=0,
            bytes_accessed=4 * act * chunk * (act + 2 * rows),
        ),
        name="qpartial",
    )(info, three_index, screen_mask, sib, *[b.reshape(nb, act, chunk) for b in blocks])


def fast(orb, aux, three_index, pair_density, active_orbitals, screen_mask, one_density, inactive_fock, active_fock):
    act, slab, rows = three_index.shape
    inactive = active_fock.shape[1]
    chips = orb // 2
    nb = act // chips
    blk = nb * act
    chunk = slab // 4
    me = lax.axis_index("orb")
    chip, core = me // 2, me % 2
    sign = 1 - 2 * core
    first_row = me * rows

    order = list(range(0, chips, 2)) + list(range(chips - 1, 0, -2))
    position = jnp.where(chip % 2 == 0, chip // 2, (2 * chips - 1 - chip) // 2)

    def info_of(sgn, half, k):
        place = (position + sgn * jnp.arange(chips, dtype=jnp.int32) + chips) % chips
        by_hops = jnp.where(place < chips // 2, 2 * place, 2 * chips - 1 - 2 * place)
        return jnp.concatenate([(2 * half + k).reshape(1), first_row.reshape(1), by_hops]).astype(jnp.int32)

    near = [(order[k], order[(k + 1) % chips]) for k in range(chips)]
    ahead = [(2 * a, 2 * b) for a, b in near] + [(2 * b + 1, 2 * a + 1) for a, b in near]
    behind = [(b, a) for a, b in ahead]
    twin = [(i, i ^ 1) for i in range(orb)]

    def hop(x, pairs):
        return lax.ppermute(x, "orb", pairs)

    local_rows = jnp.arange(rows, dtype=jnp.int32)
    mine = [info_of(sign, core, k) for k in range(2)]
    theirs = [info_of(-sign, 1 - core, k) for k in range(2)]

    contributions, sib_three = [], []
    for k in range(2):
        given, kept = extract(three_index, screen_mask, active_orbitals, theirs[k], chunk, nb, True)
        (own,) = extract(three_index, screen_mask, active_orbitals, mine[k], chunk, nb, False)
        got = hop(given.reshape(act * act, chunk), twin)
        own = own.reshape(act * act, chunk)
        contributions.append([own[j * blk : (j + 1) * blk] + got[j * blk : (j + 1) * blk] for j in range(chips)])
        sib_three.append(hop(kept, twin))
        if k == 0:
            inactive_fock, active_fock, pair_density, own = lax.optimization_barrier(
                (inactive_fock, active_fock, pair_density, own)
            )

    other = hop(pair_density, twin)
    density = jnp.concatenate(
        [jnp.where(core == 0, pair_density, other), jnp.where(core == 0, other, pair_density)], axis=0
    )
    density_rel = [lax.dynamic_slice_in_dim(density, mine[0][2 + j] * blk, blk, 1) for j in range(chips)]

    occ_index = jnp.concatenate([jnp.arange(inactive, dtype=jnp.int32), active_orbitals])
    occ_pick = ((first_row + local_rows)[:, None] == occ_index[None, :]).astype(jnp.float32)
    fixed = jnp.concatenate(
        [
            2.0 * (inactive_fock[:, :inactive] + active_fock),
            jnp.dot(inactive_fock[:, inactive:], one_density, precision=HIGHEST),
        ],
        axis=1,
    )
    occupied_fixed = lax.psum(jnp.dot(occ_pick.T, fixed, precision=HIGHEST), "orb")

    far = chips // 2
    totals = []
    for k in range(2):
        c = contributions[k]
        a = hop(c[far], ahead)
        b = hop(c[far + 1], behind) if chips - 1 - far > 0 else None
        for s in range(1, far):
            a = hop(a + c[far - s], ahead)
            if s < chips - 1 - far:
                b = hop(b + c[far + 1 + s], behind)
        totals.append(c[0] + a + b)

    def gather(x):
        blocks = [None] * chips
        blocks[0] = a = b = x
        for s in range(1, far + 1):
            a = hop(a, ahead)
            blocks[(chips - s) % chips] = a
            if s < chips - far:
                b = hop(b, behind)
                blocks[s] = b
        return blocks

    q = 0.0
    for k in range(2):
        pair_blocks = gather(totals[k])
        half = 0.0
        for j in [0] + [n for s in range(1, far + 1) for n in ((chips - s), s)][: chips - 1]:
            half = half + jnp.dot(density_rel[j], pair_blocks[j], precision=HIGH)
        if k == 0:
            half, occupied_fixed = lax.optimization_barrier((half, occupied_fixed))
        half_blocks = gather(half)
        q = q + q_partial(three_index, screen_mask, sib_three[k], half_blocks, mine[k], chunk)
    q = q.reshape(chips, TILE, 2 * rows)[:, :nb].reshape(act, 2 * rows)

    share = rows // aux
    aux_at = lax.axis_index("aux")

    def both(x, orb_bits, aux_bits):
        table = [(o * aux + y, (o ^ orb_bits) * aux + (y ^ aux_bits)) for o in range(orb) for y in range(aux)]
        return x + lax.ppermute(x, ("orb", "aux"), table)

    swapped = jnp.concatenate([q[:, rows:], q[:, :rows]], axis=1)
    q = q + lax.ppermute(swapped, "orb", twin)
    q = both(q, 0, 1)
    q_mine = q[:, :rows]
    q_rows = lax.dynamic_slice_in_dim(q_mine, aux_at * share, share, 1)

    other_row = (me ^ 1) * rows
    chip_rows = jnp.concatenate([first_row + local_rows, other_row + local_rows])
    chip_pick = (chip_rows[:, None] == occ_index[None, :]).astype(jnp.float32)
    occ_q = jnp.dot(q, chip_pick, precision=HIGHEST)
    for bit in (2, 4, 8):
        occ_q = both(occ_q, bit, 0)
    occupied = occupied_fixed + jnp.pad(occ_q.T, ((0, 0), (inactive, 0)))

    fixed_mine = lax.dynamic_slice_in_dim(fixed, aux_at * share, share, 0)
    pick_rows = lax.dynamic_slice_in_dim(occ_pick, aux_at * share, share, 0)
    fock_mine = fixed_mine + jnp.pad(q_rows.T, ((0, 0), (inactive, 0)))
    transposed = jnp.dot(pick_rows, occupied.T, precision=HIGHEST)
    return 2.0 * (fock_mine - transposed)


def plain(orb, aux, three_index, pair_density, active_orbitals, screen_mask, one_density, inactive_fock, active_fock):
    act_count = three_index.shape[0]
    slab_count = three_index.shape[1]
    row_count = three_index.shape[2]
    inactive_count = active_fock.shape[1]
    orb_position = lax.axis_index("orb")
    kept_mask = jnp.repeat(
        jnp.repeat(screen_mask.astype(jnp.float32), slab_count // screen_mask.shape[0], axis=0),
        row_count // screen_mask.shape[1],
        axis=1,
    )
    screened = three_index * kept_mask[None]
    global_rows = orb_position * row_count + jnp.arange(row_count, dtype=jnp.int32)
    active_pick = (global_rows[:, None] == active_orbitals[None, :]).astype(jnp.float32)
    partial_pairs = jnp.einsum("wPp,pv->Pvw", screened, active_pick, precision=HIGHEST).reshape(
        slab_count, act_count * act_count
    )
    pairs = lax.psum(partial_pairs, "orb")
    column_block = jnp.dot(pairs, pair_density.T, precision=HIGHEST)
    half = lax.all_gather(column_block, "orb", axis=1, tiled=True)
    q_partial = jnp.einsum(
        "uPp,Ptu->pt", screened, half.reshape(slab_count, act_count, act_count), precision=HIGHEST
    )
    occ_index = jnp.concatenate([jnp.arange(inactive_count, dtype=jnp.int32), active_orbitals])
    row_share = row_count // aux
    aux_offset = lax.axis_index("aux") * row_share
    qmatrix = lax.psum(q_partial, "aux")
    inactive_cols = 2.0 * (inactive_fock[:, :inactive_count] + active_fock)
    active_cols = jnp.dot(inactive_fock[:, inactive_count:], one_density, precision=HIGHEST) + qmatrix
    fock = jnp.concatenate([inactive_cols, active_cols], axis=1)
    occ_pick = (global_rows[:, None] == occ_index[None, :]).astype(jnp.float32)
    occupied = lax.psum(jnp.dot(occ_pick.T, fock, precision=HIGHEST), "orb")
    fock_mine = lax.dynamic_slice_in_dim(fock, aux_offset, row_share, 0)
    pick_mine = lax.dynamic_slice_in_dim(occ_pick, aux_offset, row_share, 0)
    transposed = jnp.dot(pick_mine, occupied.T, precision=HIGHEST)
    return 2.0 * (fock_mine - transposed)


def shards(orb, aux, *args):
    act, slab, rows = args[0].shape
    chips = orb // 2
    fits = orb == 16 and aux == 2 and act % chips == 0 and act % TILE == 0
    fits = fits and slab % (4 * LANES) == 0 and rows % LANES == 0
    return (fast if fits else plain)(orb, aux, *args)


def solution(mesh):
    in_specs = (
        P(None, "aux", "orb"),
        P("orb", None),
        P(),
        P("aux", "orb"),
        P(),
        P("orb", None),
        P("orb", None),
    )
    out_specs = P(("orb", "aux"), None)
    body = functools.partial(shards, mesh.shape["orb"], mesh.shape["aux"])
    return jax.shard_map(body, mesh=mesh, in_specs=in_specs, out_specs=out_specs, check_vma=False)
```

time: 371 us -> 226 us (0.61)
  waiting for transfers between devices: 294 us -> 65.7 us
  starting transfers between devices: 0.27 us -> 62.5 us
  Pallas kernels: 0 us -> 49.1 us
  matrix products: 40.7 us -> 11.6 us
  other arithmetic: 1.02 us -> 11.9 us
  blocking collectives: 8.33 us -> 0 us
  local copies, waits for them, and re-layouts: 13 us -> 5.35 us
  between operations: 13.2 us -> 19 us
    psum x2 -> x1, waiting for transfers between devices: 231 us -> 0.02 us  [fast(): lax.psum(jnp.dot(occ_pick.T, fixed, precision=HIGHEST), 'orb')]
    ppermute x0 -> x52, waiting for transfers between devices: none -> 65.7 us  [the longest x47 48.7 us: hop(): return lax.ppermute(x, 'orb', pairs)]
    all_gather x1 -> x0, waiting for transfers between devices: 63.1 us -> none  [shards(): half = lax.all_gather(column_block, 'orb', axis=1, tiled=True)]
    ppermute x0 -> x52, starting transfers between devices: none -> 62.5 us  [the longest x47 55.3 us: hop(): return lax.ppermute(x, 'orb', pairs)]
    pallas_call x0 -> x6, Pallas kernels: none -> 49.1 us  [the longest x4 32.1 us: extract(): pl.pallas_call(functools.partial(extract_body, nb), out_shape=out_shape,...]
    dot_general x6 -> x20, matrix products: 40.7 us -> 11.6 us  [the longest x16 8.78 us: fast(): half = half + jnp.dot(density_rel[j], pair_blocks[j], precision=HIGH)]
    psum x1 -> x0, blocking collectives: 8.33 us -> none  [shards(): qmatrix = lax.psum(q_partial, 'aux')]
    transpose x1, local copies, waits for them, and re-layouts: 6.37 us -> 0.01 us  [fast(): fock_mine = fixed_mine + jnp.pad(q_rows.T, ((0, 0), (inactive, 0)))]
  transfers between devices with their start and end apart: 3 -> 53, of which waited for: 3 -> 35; matrix products, arithmetic and copies ran while one was open for 0% -> 10% of each run, Pallas kernels for 0% -> 14%
where the time goes in v1:
time: 226 us; the launch traced here: 225 us
  waiting for transfers between devices  65.7 us (29%)
  starting transfers between devices  62.5 us (28%)
  Pallas kernels  49.1 us (22%)
  between operations  19 us (8%)
  other arithmetic  11.9 us (5%)
  matrix products  11.6 us (5%)
  local copies, waits for them, and re-layouts  5.35 us (2%)
    ppermute x47, starting transfers between devices, hop(): return lax.ppermute(x, 'orb', pairs)  55.3 us
    ppermute x47, waiting for transfers between devices, hop(): return lax.ppermute(x, 'orb', pairs)  48.7 us
    pallas_call x4, Pallas kernels, extract(): pl.pallas_call(functools.partial(extract_body, nb), out_shape=out_shape,...  32.1 us
    pallas_call x2, Pallas kernels, q_partial(): pl.pallas_call(functools.partial(q_body, nb), out_shape=jax.ShapeDtypeStr...  17 us
    ppermute x4, waiting for transfers between devices, both(): return x + lax.ppermute(x, ('orb', 'aux'), table)  15.8 us
    dot_general x16, matrix products, fast(): half = half + jnp.dot(density_rel[j], pair_blocks[j], precision=HIGH)  8.78 us
    ppermute x4, starting transfers between devices, both(): return x + lax.ppermute(x, ('orb', 'aux'), table)  7.13 us
  transfers between devices with their start and end apart: 53, of which 35 were waited for; matrix products, arithmetic and copies ran while one was open for 10% of the time, Pallas kernels for 14%

profile of v1, /device:TPU:0, one launch (start us, length us, event | category | flops | bytes accessed | tf_op | source)
XLA Modules:
  0.0 225.2 jit_solution(17385519134747575605)
XLA Ops:
  8.5 8.3 %extract.6 = (f32[56,56,128]{2,1,0:T(8,128)}, f32[56,128,128]{2,1,0:T(8,128)}) custom-call(s32[10]{0:T(128)} %get-tuple-element.59.info, s32[56]{0:T(128)} %active.7, f32[56,512,128]{2,1,0:T(8,128)} %three.11, s32[32,8]{1,0:T(8,128)} %copy.36.screen), custom_call_target="tpu_custom_call" | custom-call | flops 205520896 | bytes 8945664 | tf_op jit(solution)/shard_map/extract/pallas_call | solution.py:69
  17.9 8.4 %extract.4 = (f32[56,56,128]{2,1,0:T(8,128)}, f32[56,128,128]{2,1,0:T(8,128)}) custom-call(s32[10]{0:T(128)} %get-tuple-element.60.info, s32[56]{0:T(128)} %active.7, f32[56,512,128]{2,1,0:T(8,128)} %three.11, s32[32,8]{1,0:T(8,128)} %copy.36.screen), custom_call_target="tpu_custom_call" | custom-call | flops 205520896 | bytes 8945664 | tf_op jit(solution)/shard_map/extract/pallas_call | solution.py:69
  34.8 7.6 %extract.7 = f32[56,56,128]{2,1,0:T(8,128)} custom-call(s32[10]{0:T(128)} %get-tuple-element.61.info, s32[56]{0:T(128)} %active.7, f32[56,512,128]{2,1,0:T(8,128)} %three.11, s32[32,8]{1,0:T(8,128)} %copy.36.screen), custom_call_target="tpu_custom_call" | custom-call | flops 205520896 | bytes 5275648 | tf_op jit(solution)/shard_map/extract/pallas_call | solution.py:69
  42.5 7.7 %extract.5 = f32[56,56,128]{2,1,0:T(8,128)} custom-call(s32[10]{0:T(128)} %get-tuple-element.62.info, s32[56]{0:T(128)} %active.7, f32[56,512,128]{2,1,0:T(8,128)} %three.11, s32[32,8]{1,0:T(8,128)} %copy.36.screen), custom_call_target="tpu_custom_call" | custom-call | flops 205520896 | bytes 5275648 | tf_op jit(solution)/shard_map/extract/pallas_call | solution.py:69
  52.7 2.6 %collective-permute-start.26 = (f32[392,128]{1,0:T(8,128)S(1)}, f32[392,128]{1,0:T(8,128)S(1)}, u32[]{:S(2)}, u32[]{:S(2)}) collective-permute-start(f32[392,128]{1,0:T(8,128)S(1)} %slice_add_fusion.6), channel_id=1, source_target_pairs={{0,8},{8,16},{16,24},{24,28},{28,20},{20,12},{12,4},{4,0},{10,2},{... | collective-permute-start | bytes 602120 | tf_op jit(solution)/shard_map/ppermute | solution.py:182
  57.0 2.0 collective-permute-done.26
  60.0 2.1 collective-permute-start.27
  63.2 4.8 %collective-permute-done.27 = f32[392,128]{1,0:T(8,128)S(1)} collective-permute-done((f32[392,128]{1,0:T(8,128)S(1)}, f32[392,128]{1,0:T(8,128)S(1)}, u32[]{:S(2)}, u32[]{:S(2)}) %collective-permute-start.27) | collective-permute-done | bytes 200736 | tf_op jit(solution)/shard_map/ppermute | solution.py:182
  68.0 1.9 collective-permute-start.4
  71.2 4.1 %collective-permute-done.4 = f32[392,128]{1,0:T(8,128)S(1)} collective-permute-done((f32[392,128]{1,0:T(8,128)S(1)}, f32[392,128]{1,0:T(8,128)S(1)}, u32[]{:S(2)}, u32[]{:S(2)}) %collective-permute-start.4) | collective-permute-done | bytes 200736 | tf_op jit(solution)/shard_map/ppermute | solution.py:182
  77.7 4.1 %collective-permute-done.28 = f32[392,128]{1,0:T(8,128)S(1)} collective-permute-done((f32[392,128]{1,0:T(8,128)S(1)}, f32[392,128]{1,0:T(8,128)S(1)}, u32[]{:S(2)}, u32[]{:S(2)}) %collective-permute-start.28) | collective-permute-done | bytes 200736 | tf_op jit(solution)/shard_map/ppermute | solution.py:182
  88.5 2.2 collective-permute-done.8
  91.3 2.0 collective-permute-done.29
  97.9 2.1 collective-permute-done.6
  100.0 2.3 %collective-permute-start.33 = (f32[392,128]{1,0:T(8,128)S(1)}, f32[392,128]{1,0:T(8,128)S(1)}, u32[]{:S(2)}, u32[]{:S(2)}) collective-permute-start(f32[392,128]{1,0:T(8,128)S(1)} %fusion.25), channel_id=1, source_target_pairs={{0,8},{8,16},{16,24},{24,28},{28,20},{20,12},{12,4},{4,0},{10,2},{... | collective-permute-start | bytes 602120 | tf_op jit(solution)/shard_map/ppermute | solution.py:182
  105.6 2.8 %broadcast_select_fusion = (f32[196,3136]{1,0:T(8,128)S(1)}, f32[196,3136]{1,0:T(8,128)S(1)}) fusion(f32[196,3136]{1,0:T(8,128)} %collective-permute-done.1, f32[196,3136]{1,0:T(8,128)} %param.8, pred[]{:T(512)S(6)} %eq.42), kind=kLoop, calls=%fused_computation.16 | loop fusion | flops 1229312 | bytes 9834497 | tf_op jit(solution)/shard_map/jit(_where)/select_n | solution.py:203
  113.3 2.7 %collective-permute-done.11 = f32[392,128]{1,0:T(8,128)S(1)} collective-permute-done((f32[392,128]{1,0:T(8,128)S(1)}, f32[392,128]{1,0:T(8,128)S(1)}, u32[]{:S(2)}, u32[]{:S(2)}) %collective-permute-start.11) | collective-permute-done | bytes 200736 | tf_op jit(solution)/shard_map/ppermute | solution.py:182
  122.9 2.1 collective-permute-start.38
  130.9 1.9 collective-permute-start.15
  145.3 3.4 %collective-permute-done.43 = f32[392,128]{1,0:T(8,128)S(1)} collective-permute-done((f32[392,128]{1,0:T(8,128)S(1)}, f32[392,128]{1,0:T(8,128)S(1)}, u32[]{:S(2)}, u32[]{:S(2)}) %collective-permute-start.43) | collective-permute-done | bytes 200736 | tf_op jit(solution)/shard_map/ppermute | solution.py:182
  148.7 1.9 collective-permute-start.17
  154.3 2.0 collective-permute-done.17
  158.5 2.1 collective-permute-done.41
  163.2 2.5 %collective-permute-start.22 = (f32[392,128]{1,0:T(8,128)S(1)}, f32[392,128]{1,0:T(8,128)S(1)}, u32[]{:S(2)}, u32[]{:S(2)}) collective-permute-start(f32[392,128]{1,0:T(8,128)S(1)} %collective-permute-done.21), channel_id=1, source_target_pairs={{0,8},{8,16},{16,24},{24,28},{28,20},{20,12},{12,4},{4,0},{10,2},{... | collective-permute-start | bytes 602120 | tf_op jit(solution)/shard_map/ppermute | solution.py:182
  173.4 8.4 %qpartial.3 = f32[64,256]{1,0:T(8,128)} custom-call(s32[10]{0:T(128)} %get-tuple-element.61.info, f32[56,512,128]{2,1,0:T(8,128)} %three.11, s32[32,8]{1,0:T(8,128)} %copy.36.screen, f32[56,128,128]{2,1,0:T(8,128)} %collective-permute-done.24.sib, f32[7,56,128]{2,1,0:T(8,128)} %bitcast.97, f32[7,56,128]{2,1,0:T(8,128)} %bitcast.101, ...), custom_call_target="tpu_custom_call" | custom-call | flops 616562688 | bytes 8945664 | tf_op jit(solution)/shard_map/qpartial/pallas_call | solution.py:133
  182.7 8.6 %qpartial.2 = f32[64,256]{1,0:T(8,128)} custom-call(s32[10]{0:T(128)} %get-tuple-element.62.info, f32[56,512,128]{2,1,0:T(8,128)} %three.11, s32[32,8]{1,0:T(8,128)} %copy.36.screen, f32[56,128,128]{2,1,0:T(8,128)} %collective-permute-done.sib, f32[7,56,128]{2,1,0:T(8,128)} %bitcast.96, f32[7,56,128]{2,1,0:T(8,128)} %bitcast.102, f32[7,56,128]{2,1,0:T(8,128)} %bitcast.104, ...), custom_call_target="tpu_custom_call" | custom-call | flops 616562688 | bytes 8945664 | tf_op jit(solution)/shard_map/qpartial/pallas_call | solution.py:133
  195.6 3.8 %collective-permute-done.48 = f32[56,256]{0,1:T(8,128)S(1)} collective-permute-done((f32[56,256]{0,1:T(8,128)S(1)}, f32[56,256]{0,1:T(8,128)S(1)}, u32[]{:S(2)}, u32[]{:S(2)}) %collective-permute-start.48) | collective-permute-done | bytes 57376 | tf_op jit(solution)/shard_map/ppermute | solution.py:258
  199.9 1.9 collective-permute-start.49
  201.8 3.1 %collective-permute-done.49 = f32[56,256]{0,1:T(8,128)S(1)} collective-permute-done((f32[56,256]{0,1:T(8,128)S(1)}, f32[56,256]{0,1:T(8,128)S(1)}, u32[]{:S(2)}, u32[]{:S(2)}) %collective-permute-start.49) | collective-permute-done | bytes 57376 | tf_op jit(solution)/shard_map/ppermute | solution.py:258
  206.4 3.6 %collective-permute-done.50 = f32[56,256]{0,1:T(8,128)S(1)} collective-permute-done((f32[56,256]{0,1:T(8,128)S(1)}, f32[56,256]{0,1:T(8,128)S(1)}, u32[]{:S(2)}, u32[]{:S(2)}) %collective-permute-start.50) | collective-permute-done | bytes 57376 | tf_op jit(solution)/shard_map/ppermute | solution.py:258
  210.0 2.1 collective-permute-start.51
  212.1 5.2 %collective-permute-done.51 = f32[56,256]{0,1:T(8,128)S(1)} collective-permute-done((f32[56,256]{0,1:T(8,128)S(1)}, f32[56,256]{0,1:T(8,128)S(1)}, u32[]{:S(2)}, u32[]{:S(2)}) %collective-permute-start.51) | collective-permute-done | bytes 57376 | tf_op jit(solution)/shard_map/ppermute | solution.py:258
  (191 shorter events, 85.5 us)
Async XLA Ops:
  6.5 138.2 %all-reduce.4.cloned.1.call-start = ((), (), s32[]{:S(2)}) async-start(), calls=%async_computation | async-start | bytes 524288 | tf_op jit(solution)/shard_map/psum | solution.py:216
  16.9 34.8 %collective-permute-start.25 = (f32[3136,128]{1,0:T(8,128)}, f32[3136,128]{1,0:T(8,128)}, u32[]{:S(2)}, u32[]{:S(2)}) collective-permute-start(f32[3136,128]{1,0:T(8,128)} %bitcast.113), channel_id=1, source_target_pairs={{0,2},{2,0},{4,6},{6,4},{8,10},{10,8},{12,14},{14,12},{16,18},{18,... | collective-permute-start | bytes 4816904 | tf_op jit(solution)/shard_map/ppermute | solution.py:182
  17.3 87.3 %collective-permute-start.1 = (f32[196,3136]{1,0:T(8,128)}, f32[196,3136]{1,0:T(8,128)}, u32[]{:S(2)}, u32[]{:S(2)}) collective-permute-start(f32[196,3136]{1,0:T(8,128)} %param.8), channel_id=1, source_target_pairs={{0,2},{2,0},{4,6},{6,4},{8,10},{10,8},{12,14},{14,12},{16,18},{18,... | collective-permute-start | bytes 7375880 | tf_op jit(solution)/shard_map/ppermute | solution.py:182
  17.4 150.8 %collective-permute-start.24 = (f32[56,128,128]{2,1,0:T(8,128)}, f32[56,128,128]{2,1,0:T(8,128)}, u32[]{:S(2)}, u32[]{:S(2)}) collective-permute-start(f32[56,128,128]{2,1,0:T(8,128)} %get-tuple-element.20), channel_id=1, source_target_pairs={{0,2},{2,0},{4,6},{6,4},{8,10},{10,8},{12,14},{14,12},{16,18},{18,... | collective-permute-start | bytes 11010056 | tf_op jit(solution)/shard_map/ppermute | solution.py:182
  26.3 29.0 %collective-permute-start.2 = (f32[3136,128]{1,0:T(8,128)}, f32[3136,128]{1,0:T(8,128)S(1)}, u32[]{:S(2)}, u32[]{:S(2)}) collective-permute-start(f32[3136,128]{1,0:T(8,128)} %bitcast.114), channel_id=1, source_target_pairs={{0,2},{2,0},{4,6},{6,4},{8,10},{10,8},{12,14},{14,12},{16,18},{18,... | collective-permute-start | bytes 4816904 | tf_op jit(solution)/shard_map/ppermute | solution.py:182
  27.9 154.0 %collective-permute-start = (f32[56,128,128]{2,1,0:T(8,128)}, f32[56,128,128]{2,1,0:T(8,128)}, u32[]{:S(2)}, u32[]{:S(2)}) collective-permute-start(f32[56,128,128]{2,1,0:T(8,128)} %get-tuple-element.16), channel_id=1, source_target_pairs={{0,2},{2,0},{4,6},{6,4},{8,10},{10,8},{12,14},{14,12},{16,18},{18,... | collective-permute-start | bytes 11010056 | tf_op jit(solution)/shard_map/ppermute | solution.py:182
  60.0 8.0 %collective-permute-start.27 = (f32[392,128]{1,0:T(8,128)S(1)}, f32[392,128]{1,0:T(8,128)S(1)}, u32[]{:S(2)}, u32[]{:S(2)}) collective-permute-start(f32[392,128]{1,0:T(8,128)S(1)} %get-tuple-element.41), channel_id=1, source_target_pairs={{0,8},{8,16},{16,24},{24,28},{28,20},{20,12},{12,4},{4,0},{10,2},{... | collective-permute-start | bytes 602120 | tf_op jit(solution)/shard_map/ppermute | solution.py:182
  62.1 7.8 %collective-permute-start.30 = (f32[392,128]{1,0:T(8,128)S(1)}, f32[392,128]{1,0:T(8,128)S(1)}, u32[]{:S(2)}, u32[]{:S(2)}) collective-permute-start(f32[392,128]{1,0:T(8,128)S(1)} %get-tuple-element.42), channel_id=1, source_target_pairs={{8,0},{16,8},{24,16},{28,24},{20,28},{12,20},{4,12},{0,4},{2,10},{... | collective-permute-start | bytes 602120 | tf_op jit(solution)/shard_map/ppermute | solution.py:182
  68.0 7.4 %collective-permute-start.4 = (f32[392,128]{1,0:T(8,128)S(1)}, f32[392,128]{1,0:T(8,128)S(1)}, u32[]{:S(2)}, u32[]{:S(2)}) collective-permute-start(f32[392,128]{1,0:T(8,128)S(1)} %get-tuple-element.55), channel_id=1, source_target_pairs={{0,8},{8,16},{16,24},{24,28},{28,20},{20,12},{12,4},{4,0},{10,2},{... | collective-permute-start | bytes 602120 | tf_op jit(solution)/shard_map/ppermute | solution.py:182
  69.9 7.7 %collective-permute-start.7 = (f32[392,128]{1,0:T(8,128)S(1)}, f32[392,128]{1,0:T(8,128)S(1)}, u32[]{:S(2)}, u32[]{:S(2)}) collective-permute-start(f32[392,128]{1,0:T(8,128)S(1)} %get-tuple-element.56), channel_id=1, source_target_pairs={{8,0},{16,8},{24,16},{28,24},{20,28},{12,20},{4,12},{0,4},{2,10},{... | collective-permute-start | bytes 602120 | tf_op jit(solution)/shard_map/ppermute | solution.py:182
  77.6 6.9 %collective-permute-start.31 = (f32[392,128]{1,0:T(8,128)S(1)}, f32[392,128]{1,0:T(8,128)S(1)}, u32[]{:S(2)}, u32[]{:S(2)}) collective-permute-start(f32[392,128]{1,0:T(8,128)S(1)} %get-tuple-element.40), channel_id=1, source_target_pairs={{8,0},{16,8},{24,16},{28,24},{20,28},{12,20},{4,12},{0,4},{2,10},{... | collective-permute-start | bytes 602120 | tf_op jit(solution)/shard_map/ppermute | solution.py:182
  100.0 11.2 %collective-permute-start.33 = (f32[392,128]{1,0:T(8,128)S(1)}, f32[392,128]{1,0:T(8,128)S(1)}, u32[]{:S(2)}, u32[]{:S(2)}) collective-permute-start(f32[392,128]{1,0:T(8,128)S(1)} %fusion.25), channel_id=1, source_target_pairs={{0,8},{8,16},{16,24},{24,28},{28,20},{20,12},{12,4},{4,0},{10,2},{... | collective-permute-start | bytes 602120 | tf_op jit(solution)/shard_map/ppermute | solution.py:182
  104.6 14.2 %collective-permute-start.10 = (f32[392,128]{1,0:T(8,128)S(1)}, f32[392,128]{1,0:T(8,128)S(1)}, u32[]{:S(2)}, u32[]{:S(2)}) collective-permute-start(f32[392,128]{1,0:T(8,128)S(1)} %fusion.32), channel_id=1, source_target_pairs={{0,8},{8,16},{16,24},{24,28},{28,20},{20,12},{12,4},{4,0},{10,2},{... | collective-permute-start | bytes 602120 | tf_op jit(solution)/shard_map/ppermute | solution.py:182
  111.2 9.5 %collective-permute-start.36 = (f32[392,128]{1,0:T(8,128)S(1)}, f32[392,128]{1,0:T(8,128)S(1)}, u32[]{:S(2)}, u32[]{:S(2)}) collective-permute-start(f32[392,128]{1,0:T(8,128)S(1)} %collective-permute-done.34), channel_id=1, source_target_pairs={{8,0},{16,8},{24,16},{28,24},{20,28},{12,20},{4,12},{0,4},{2,10},{... | collective-permute-start | bytes 602120 | tf_op jit(solution)/shard_map/ppermute | solution.py:182
  116.1 6.9 %collective-permute-start.35 = (f32[392,128]{1,0:T(8,128)S(1)}, f32[392,128]{1,0:T(8,128)S(1)}, u32[]{:S(2)}, u32[]{:S(2)}) collective-permute-start(f32[392,128]{1,0:T(8,128)S(1)} %collective-permute-done.33), channel_id=1, source_target_pairs={{0,8},{8,16},{16,24},{24,28},{28,20},{20,12},{12,4},{4,0},{10,2},{... | collective-permute-start | bytes 602120 | tf_op jit(solution)/shard_map/ppermute | solution.py:182
  118.9 7.8 %collective-permute-start.13 = (f32[392,128]{1,0:T(8,128)S(1)}, f32[392,128]{1,0:T(8,128)S(1)}, u32[]{:S(2)}, u32[]{:S(2)}) collective-permute-start(f32[392,128]{1,0:T(8,128)S(1)} %collective-permute-done.11), channel_id=1, source_target_pairs={{8,0},{16,8},{24,16},{28,24},{20,28},{12,20},{4,12},{0,4},{2,10},{... | collective-permute-start | bytes 602120 | tf_op jit(solution)/shard_map/ppermute | solution.py:182
  120.7 7.5 %collective-permute-start.12 = (f32[392,128]{1,0:T(8,128)S(1)}, f32[392,128]{1,0:T(8,128)S(1)}, u32[]{:S(2)}, u32[]{:S(2)}) collective-permute-start(f32[392,128]{1,0:T(8,128)S(1)} %collective-permute-done.10), channel_id=1, source_target_pairs={{0,8},{8,16},{16,24},{24,28},{28,20},{20,12},{12,4},{4,0},{10,2},{... | collective-permute-start | bytes 602120 | tf_op jit(solution)/shard_map/ppermute | solution.py:182
  122.9 8.0 %collective-permute-start.38 = (f32[392,128]{1,0:T(8,128)S(1)}, f32[392,128]{1,0:T(8,128)S(1)}, u32[]{:S(2)}, u32[]{:S(2)}) collective-permute-start(f32[392,128]{1,0:T(8,128)S(1)} %collective-permute-done.36), channel_id=1, source_target_pairs={{8,0},{16,8},{24,16},{28,24},{20,28},{12,20},{4,12},{0,4},{2,10},{... | collective-permute-start | bytes 602120 | tf_op jit(solution)/shard_map/ppermute | solution.py:182
  130.9 7.5 %collective-permute-start.15 = (f32[392,128]{1,0:T(8,128)S(1)}, f32[392,128]{1,0:T(8,128)S(1)}, u32[]{:S(2)}, u32[]{:S(2)}) collective-permute-start(f32[392,128]{1,0:T(8,128)S(1)} %collective-permute-done.13), channel_id=1, source_target_pairs={{8,0},{16,8},{24,16},{28,24},{20,28},{12,20},{4,12},{0,4},{2,10},{... | collective-permute-start | bytes 602120 | tf_op jit(solution)/shard_map/ppermute | solution.py:182
  132.9 7.2 %collective-permute-start.39 = (f32[392,128]{1,0:T(8,128)S(1)}, f32[392,128]{1,0:T(8,128)S(1)}, u32[]{:S(2)}, u32[]{:S(2)}) collective-permute-start(f32[392,128]{1,0:T(8,128)S(1)} %collective-permute-done.37), channel_id=1, source_target_pairs={{0,8},{8,16},{16,24},{24,28},{28,20},{20,12},{12,4},{4,0},{10,2},{... | collective-permute-start | bytes 602120 | tf_op jit(solution)/shard_map/ppermute | solution.py:182
  134.5 9.5 %collective-permute-start.16 = (f32[392,128]{1,0:T(8,128)S(1)}, f32[392,128]{1,0:T(8,128)S(1)}, u32[]{:S(2)}, u32[]{:S(2)}) collective-permute-start(f32[392,128]{1,0:T(8,128)S(1)} %collective-permute-done.14), channel_id=1, source_target_pairs={{0,8},{8,16},{16,24},{24,28},{28,20},{20,12},{12,4},{4,0},{10,2},{... | collective-permute-start | bytes 602120 | tf_op jit(solution)/shard_map/ppermute | solution.py:182
  140.7 8.0 %collective-permute-start.43 = (f32[392,128]{1,0:T(8,128)S(1)}, f32[392,128]{1,0:T(8,128)S(1)}, u32[]{:S(2)}, u32[]{:S(2)}) collective-permute-start(f32[392,128]{1,0:T(8,128)S(1)} %convolution_add_fusion), channel_id=1, source_target_pairs={{0,8},{8,16},{16,24},{24,28},{28,20},{20,12},{12,4},{4,0},{10,2},{... | collective-permute-start | bytes 602120 | tf_op jit(solution)/shard_map/ppermute | solution.py:182
  142.4 8.3 %collective-permute-start.40 = (f32[392,128]{1,0:T(8,128)S(1)}, f32[392,128]{1,0:T(8,128)S(1)}, u32[]{:S(2)}, u32[]{:S(2)}) collective-permute-start(f32[392,128]{1,0:T(8,128)S(1)} %convolution_add_fusion), channel_id=1, source_target_pairs={{8,0},{16,8},{24,16},{28,24},{20,28},{12,20},{4,12},{0,4},{2,10},{... | collective-permute-start | bytes 602120 | tf_op jit(solution)/shard_map/ppermute | solution.py:182
  144.7 7.8 %collective-permute-start.20 = (f32[392,128]{1,0:T(8,128)S(1)}, f32[392,128]{1,0:T(8,128)S(1)}, u32[]{:S(2)}, u32[]{:S(2)}) collective-permute-start(f32[392,128]{1,0:T(8,128)S(1)} %convolution_add_fusion.4), channel_id=1, source_target_pairs={{0,8},{8,16},{16,24},{24,28},{28,20},{20,12},{12,4},{4,0},{10,2},{... | collective-permute-start | bytes 602120 | tf_op jit(solution)/shard_map/ppermute | solution.py:182
  148.7 7.6 %collective-permute-start.17 = (f32[392,128]{1,0:T(8,128)S(1)}, f32[392,128]{1,0:T(8,128)S(1)}, u32[]{:S(2)}, u32[]{:S(2)}) collective-permute-start(f32[392,128]{1,0:T(8,128)S(1)} %convolution_add_fusion.4), channel_id=1, source_target_pairs={{8,0},{16,8},{24,16},{28,24},{20,28},{12,20},{4,12},{0,4},{2,10},{... | collective-permute-start | bytes 602120 | tf_op jit(solution)/shard_map/ppermute | solution.py:182
  150.7 7.5 %collective-permute-start.44 = (f32[392,128]{1,0:T(8,128)S(1)}, f32[392,128]{1,0:T(8,128)S(1)}, u32[]{:S(2)}, u32[]{:S(2)}) collective-permute-start(f32[392,128]{1,0:T(8,128)S(1)} %collective-permute-done.43), channel_id=1, source_target_pairs={{0,8},{8,16},{16,24},{24,28},{28,20},{20,12},{12,4},{4,0},{10,2},{... | collective-permute-start | bytes 602120 | tf_op jit(solution)/shard_map/ppermute | solution.py:182
  152.4 8.1 %collective-permute-start.41 = (f32[392,128]{1,0:T(8,128)S(1)}, f32[392,128]{1,0:T(8,128)S(1)}, u32[]{:S(2)}, u32[]{:S(2)}) collective-permute-start(f32[392,128]{1,0:T(8,128)S(1)} %collective-permute-done.40), channel_id=1, source_target_pairs={{8,0},{16,8},{24,16},{28,24},{20,28},{12,20},{4,12},{0,4},{2,10},{... | collective-permute-start | bytes 602120 | tf_op jit(solution)/shard_map/ppermute | solution.py:182
  156.3 6.9 %collective-permute-start.21 = (f32[392,128]{1,0:T(8,128)S(1)}, f32[392,128]{1,0:T(8,128)S(1)}, u32[]{:S(2)}, u32[]{:S(2)}) collective-permute-start(f32[392,128]{1,0:T(8,128)S(1)} %collective-permute-done.20), channel_id=1, source_target_pairs={{0,8},{8,16},{16,24},{24,28},{28,20},{20,12},{12,4},{4,0},{10,2},{... | collective-permute-start | bytes 602120 | tf_op jit(solution)/shard_map/ppermute | solution.py:182
  158.2 7.9 %collective-permute-start.18 = (f32[392,128]{1,0:T(8,128)S(1)}, f32[392,128]{1,0:T(8,128)S(1)}, u32[]{:S(2)}, u32[]{:S(2)}) collective-permute-start(f32[392,128]{1,0:T(8,128)S(1)} %collective-permute-done.17), channel_id=1, source_target_pairs={{8,0},{16,8},{24,16},{28,24},{20,28},{12,20},{4,12},{0,4},{2,10},{... | collective-permute-start | bytes 602120 | tf_op jit(solution)/shard_map/ppermute | solution.py:182
  168.2 13.7 %collective-permute-start.19 = (f32[392,128]{1,0:T(8,128)S(1)}, f32[392,128]{1,0:T(8,128)S(1)}, u32[]{:S(2)}, u32[]{:S(2)}) collective-permute-start(f32[392,128]{1,0:T(8,128)S(1)} %collective-permute-done.18), channel_id=1, source_target_pairs={{8,0},{16,8},{24,16},{28,24},{20,28},{12,20},{4,12},{0,4},{2,10},{... | collective-permute-start | bytes 602120 | tf_op jit(solution)/shard_map/ppermute | solution.py:182
  169.7 12.3 %collective-permute-start.23 = (f32[392,128]{1,0:T(8,128)S(1)}, f32[392,128]{1,0:T(8,128)S(1)}, u32[]{:S(2)}, u32[]{:S(2)}) collective-permute-start(f32[392,128]{1,0:T(8,128)S(1)} %collective-permute-done.22), channel_id=1, source_target_pairs={{0,8},{8,16},{16,24},{24,28},{28,20},{20,12},{12,4},{4,0},{10,2},{... | collective-permute-start | bytes 602120 | tf_op jit(solution)/shard_map/ppermute | solution.py:182
  210.0 7.3 %collective-permute-start.51 = (f32[56,256]{0,1:T(8,128)S(1)}, f32[56,256]{0,1:T(8,128)S(1)}, u32[]{:S(2)}, u32[]{:S(2)}) collective-permute-start(f32[56,256]{0,1:T(8,128)S(1)} %add.338), channel_id=1, source_target_pairs={{0,16},{1,17},{2,18},{3,19},{4,20},{5,21},{6,22},{7,23},{8,24},{9,... | collective-permute-start | bytes 172040 | tf_op jit(solution)/shard_map/ppermute | solution.py:258
  (46 other events, 472.9 us)
Sparse Core Ops, SparseCore 0:
  28.1 92.8 all-reduce.3

commit v2 on v0

v2 whole, which is shorter than its diff:
```python
import functools

import jax
import jax.numpy as jnp
from jax import lax
from jax.experimental import pallas as pl
from jax.experimental.pallas import tpu as pltpu
from jax.sharding import PartitionSpec as P

HIGHEST = lax.Precision.HIGHEST
HIGH = lax.Precision.HIGH
LANES = 128
TILE = 8
MIB = 1024 * 1024


def split(x):
    top = x.astype(jnp.bfloat16)
    return top, (x - top.astype(jnp.float32)).astype(jnp.bfloat16)


def mxu(a, b, contract):
    return lax.dot_general(a, b, (contract, ((), ())), preferred_element_type=jnp.float32)


def places():
    return tuple(pl.BlockSpec(memory_space=m) for m in (pltpu.SMEM, pltpu.VMEM, pltpu.HBM, pl.ANY))


def expand_mask(screen, quarter, chunk, rows):
    shells, blocks = screen.shape
    slab_rows = 4 * chunk // blocks
    row = lax.broadcasted_iota(jnp.int32, (chunk, blocks), 0) // slab_rows
    col = lax.broadcasted_iota(jnp.int32, (chunk, blocks), 1)
    down = (col == row + quarter * (blocks // 4)).astype(jnp.bfloat16)
    shell = lax.broadcasted_iota(jnp.int32, (shells, rows), 0)
    across = (shell == lax.broadcasted_iota(jnp.int32, (shells, rows), 1) // (rows // shells)).astype(jnp.bfloat16)
    tall = mxu(down, screen[...].astype(jnp.float32).astype(jnp.bfloat16), ((1,), (1,)))
    return mxu(tall.astype(jnp.bfloat16), across, ((1,), (0,)))


def extract_body(nb, info, active, three, screen, pairs, *refs):
    kept = refs[0] if len(refs) == 8 else None
    value, turned, found, mask, sem_in, sem_out, sem_kept = refs[-7:]
    act = pairs.shape[0]
    _, chunk, rows = value.shape
    tiles = act // TILE
    start = pl.multiple_of(info[0] * chunk, chunk)

    def tile(i):
        return pl.ds(pl.multiple_of(i * TILE, TILE), TILE)

    def fetch(i):
        return pltpu.make_async_copy(three.at[tile(i), pl.ds(start, chunk), :], value.at[tile(i)], sem_in.at[i])

    def keep(i):
        return pltpu.make_async_copy(value.at[tile(i)], kept.at[tile(i)], sem_kept.at[i])

    for i in range(tiles):
        fetch(i).start()
    mask[...] = expand_mask(screen, info[0], chunk, rows)

    found[...] = jnp.zeros_like(found)

    @pl.loop(0, tiles)
    def _(i):
        fetch(i).wait()
        part = value[tile(i)] * mask[...][None]
        if kept is not None:
            value[tile(i)] = part
            keep(i).start()
        for w in range(TILE):
            turned[pl.ds(pl.multiple_of((i * TILE + w) * rows, rows), rows), :] = part[w].T

    for v in range(act):
        row = active[info[2 + v // nb] * nb + v % nb] - info[1]

        @pl.when(jnp.logical_and(row >= 0, row < rows))
        def _():
            for i in range(tiles):
                lines = turned[pl.ds(i * TILE * rows + row, TILE, stride=rows), :]
                found[v, i * TILE : (i + 1) * TILE, :] = lines

    give = pltpu.make_async_copy(found, pairs, sem_out)
    give.start()
    give.wait()
    if kept is not None:
        for i in range(tiles):
            keep(i).wait()


def extract(three_index, screen_mask, active, info, chunk, nb, keep):
    act, slab, rows = three_index.shape
    tiles = act // TILE
    out_shape = [jax.ShapeDtypeStruct((act, act, chunk), jnp.float32)]
    if keep:
        out_shape.append(jax.ShapeDtypeStruct((act, chunk, rows), jnp.float32))
    smem, vmem, hbm, anywhere = places()
    return pl.pallas_call(
        functools.partial(extract_body, nb),
        out_shape=out_shape,
        in_specs=[smem, smem, hbm, vmem],
        out_specs=[anywhere] * len(out_shape),
        scratch_shapes=[
            pltpu.VMEM((act, chunk, rows), jnp.float32),
            pltpu.VMEM((act * rows, chunk), jnp.float32),
            pltpu.VMEM((act, act, chunk), jnp.float32),
            pltpu.VMEM((chunk, rows), jnp.float32),
            pltpu.SemaphoreType.DMA((tiles,)),
            pltpu.SemaphoreType.DMA,
            pltpu.SemaphoreType.DMA((tiles,)),
        ],
        compiler_params=pltpu.CompilerParams(vmem_limit_bytes=52 * MIB),
        cost_estimate=pl.CostEstimate(
            flops=4 * act * act * chunk * rows,
            transcendentals=0,
            bytes_accessed=4 * act * chunk * (act + rows * (2 if keep else 1)),
        ),
        name="extract",
    )(info, active, three_index, screen_mask)


def q_body(nb, count, info, three, screen, sib, *refs):
    blocks = refs[:count]
    out, own_s, sib_s, held, lhs, acc, mask, sem_own, sem_sib, sem_block = refs[count:]
    act, chunk, rows = own_s.shape
    tiles = act // TILE
    height = acc.shape[0]
    start = pl.multiple_of(info[0] * chunk, chunk)

    def tile(i):
        return pl.ds(pl.multiple_of(i * TILE, TILE), TILE)

    def own(i):
        return pltpu.make_async_copy(three.at[tile(i), pl.ds(start, chunk), :], own_s.at[tile(i)], sem_own.at[i])

    def other(i):
        return pltpu.make_async_copy(sib.at[tile(i)], sib_s.at[tile(i)], sem_sib.at[i])

    def bring(j):
        return pltpu.make_async_copy(blocks[j], held.at[j], sem_block.at[j])

    for j in range(count):
        bring(j).start()
    for i in range(tiles):
        own(i).start()
        other(i).start()
    lhs[...] = jnp.zeros_like(lhs)
    mask[...] = expand_mask(screen, info[0], chunk, rows)
    for j in range(count):
        bring(j).wait()
    acc[...] = jnp.zeros_like(acc)
    nn = ((1,), (0,))

    @pl.loop(0, tiles)
    def _(i):
        for j in range(count):
            for t in range(nb):
                lhs[pl.ds(j * TILE + t, TILE, stride=height), :] = held[j, t, tile(i), :]
        own(i).wait()
        other(i).wait()
        total = acc[...]
        for m in range(0, TILE, 2):
            pieces = [lhs[n * height : (n + 1) * height, :] for n in (m, m + 1)]
            left, left_low = split(jnp.concatenate(pieces, axis=1))
            right = [jnp.concatenate([own_s[i * TILE + n] * mask[...], sib_s[i * TILE + n]], axis=1) for n in (m, m + 1)]
            top, low = split(jnp.concatenate(right, axis=0))
            both = mxu(jnp.concatenate([left, left_low], axis=0), top, nn)
            total = total + (both[:height] + both[height:] + mxu(left, low, nn))
        acc[...] = total

    for j in range(count):
        where = pl.multiple_of(info[2 + j] * TILE, TILE)
        out[pl.ds(where, TILE), :] = acc[j * TILE : (j + 1) * TILE, :]


def q_partial(three_index, screen_mask, sib, blocks, info, chunk):
    act, slab, rows = three_index.shape
    count = len(blocks)
    nb = act // count
    tiles = act // TILE
    smem, vmem, hbm, anywhere = places()
    return pl.pallas_call(
        functools.partial(q_body, nb, count),
        out_shape=jax.ShapeDtypeStruct((count * TILE, 2 * rows), jnp.float32),
        in_specs=[smem, hbm, vmem, anywhere] + [anywhere] * count,
        out_specs=vmem,
        scratch_shapes=[
            pltpu.VMEM((act, chunk, rows), jnp.float32),
            pltpu.VMEM((act, chunk, rows), jnp.float32),
            pltpu.VMEM((count, nb, act, chunk), jnp.float32),
            pltpu.VMEM((TILE * count * TILE, chunk), jnp.float32),
            pltpu.VMEM((count * TILE, 2 * rows), jnp.float32),
            pltpu.VMEM((chunk, rows), jnp.float32),
            pltpu.SemaphoreType.DMA((tiles,)),
            pltpu.SemaphoreType.DMA((tiles,)),
            pltpu.SemaphoreType.DMA((count,)),
        ],
        compiler_params=pltpu.CompilerParams(vmem_limit_bytes=52 * MIB),
        cost_estimate=pl.CostEstimate(
            flops=12 * act * act * chunk * rows,
            transcendentals=0,
            bytes_accessed=4 * act * chunk * (act + 2 * rows),
        ),
        name="qpartial",
    )(info, three_index, screen_mask, sib, *[b.reshape(nb, act, chunk) for b in blocks])


def half_body(chips, info, own, twin, *refs):
    count = 2 * (chips - 1)
    blocks, outs = refs[:count], refs[count : count + 2]
    density, held, acc, sem_own, sem_twin, sem_block = refs[count + 2 :]
    size, chunk = blocks[0].shape
    rows, depth = own.shape
    core = info[2 + chips]

    def bring(n):
        j, k = n // 2, n % 2
        hops = j if j < chips // 2 else j + 1
        where = pl.ds(pl.multiple_of(info[2 + hops] * size, TILE), size)
        return pltpu.make_async_copy(blocks[n], held.at[where, pl.ds(k * chunk, chunk)], sem_block.at[n])

    mine = pltpu.make_async_copy(own, density.at[core], sem_own)
    other = pltpu.make_async_copy(twin, density.at[1 - core], sem_twin)
    mine.start()
    other.start()
    for n in range(count):
        bring(n).start()
    missing = pl.ds(pl.multiple_of(info[2 + chips // 2] * size, TILE), size)
    held[missing, :] = jnp.zeros((size, 2 * chunk), jnp.float32)
    acc[...] = jnp.zeros_like(acc)
    mine.wait()
    other.wait()
    for n in range(count):
        bring(n).wait()
    nn = ((1,), (0,))
    step = 2 * LANES

    def add(start, length):
        top, low = split(held[pl.ds(start, length), :])
        for h in range(2):
            left, left_low = split(density[h, :, pl.ds(start, length)])
            acc[h] += mxu(left, top, nn) + mxu(left_low, top, nn) + mxu(left, low, nn)

    @pl.loop(0, depth // step)
    def _(i):
        add(pl.multiple_of(i * step, step), step)

    if depth % step:
        add(depth - depth % step, depth % step)
    for k in range(2):
        for h in range(2):
            outs[k][h * rows : (h + 1) * rows, :] = acc[h, :, k * chunk : (k + 1) * chunk]


def half_partial(own, twin, blocks, info, chips):
    size, chunk = blocks[0].shape
    rows, depth = own.shape
    smem, vmem, hbm, anywhere = places()
    return pl.pallas_call(
        functools.partial(half_body, chips),
        out_shape=[jax.ShapeDtypeStruct((2 * rows, chunk), jnp.float32)] * 2,
        in_specs=[smem, anywhere, anywhere] + [anywhere] * len(blocks),
        out_specs=[vmem, vmem],
        scratch_shapes=[
            pltpu.VMEM((2, rows, depth), jnp.float32),
            pltpu.VMEM((depth, 2 * chunk), jnp.float32),
            pltpu.VMEM((2, rows, 2 * chunk), jnp.float32),
            pltpu.SemaphoreType.DMA,
            pltpu.SemaphoreType.DMA,
            pltpu.SemaphoreType.DMA((len(blocks),)),
        ],
        compiler_params=pltpu.CompilerParams(vmem_limit_bytes=16 * MIB),
        cost_estimate=pl.CostEstimate(
            flops=24 * rows * depth * chunk,
            transcendentals=0,
            bytes_accessed=8 * rows * depth + 8 * depth * chunk,
        ),
        name="half",
    )(info, own, twin, *blocks)


def fast(orb, aux, three_index, pair_density, active_orbitals, screen_mask, one_density, inactive_fock, active_fock):
    act, slab, rows = three_index.shape
    inactive = active_fock.shape[1]
    chips = orb // 2
    nb = act // chips
    blk = nb * act
    chunk = slab // 4
    me = lax.axis_index("orb")
    chip, core = lax.shift_right_logical(me, 1), lax.bitwise_and(me, 1)
    half_chip = lax.shift_right_logical(chip, 1)
    sign = 1 - 2 * core
    first_row = me * rows

    order = list(range(0, chips, 2)) + list(range(chips - 1, 0, -2))
    position = jnp.where(lax.bitwise_and(chip, 1) == 0, half_chip, chips - 1 - half_chip)

    def chip_at(sgn, hops):
        place = lax.rem(position + sgn * hops + chips, chips)
        return jnp.where(place < chips // 2, 2 * place, 2 * chips - 1 - 2 * place)

    def info_of(sgn, half, k):
        by_hops = chip_at(sgn, jnp.arange(chips, dtype=jnp.int32))
        return jnp.concatenate([jnp.stack([2 * half + k, first_row]), by_hops, core.reshape(1)]).astype(jnp.int32)

    near = [(order[k], order[(k + 1) % chips]) for k in range(chips)]
    ahead = [(2 * a, 2 * b) for a, b in near] + [(2 * b + 1, 2 * a + 1) for a, b in near]
    behind = [(b, a) for a, b in ahead]
    twin = [(i, i ^ 1) for i in range(orb)]

    def hop(x, pairs):
        return lax.ppermute(x, "orb", pairs)

    local_rows = jnp.arange(rows, dtype=jnp.int32)
    mine = [info_of(sign, core, k) for k in range(2)]
    theirs = [info_of(-sign, 1 - core, k) for k in range(2)]

    shells = screen_mask.T
    contributions, sib_three = [], []
    for k in range(2):
        given, kept = extract(three_index, shells, active_orbitals, theirs[k], chunk, nb, True)
        (own,) = extract(three_index, shells, active_orbitals, mine[k], chunk, nb, False)
        got = hop(given.reshape(act * act, chunk), twin)
        own = own.reshape(act * act, chunk)
        sums = [own[j * blk : (j + 1) * blk] + got[j * blk : (j + 1) * blk] for j in range(chips)]
        sib_three.append(kept)
        if k == 0:
            theirs[1], mine[1], sums[chips // 2] = lax.optimization_barrier((theirs[1], mine[1], sums[chips // 2]))
        else:
            pair_density, inactive_fock, active_fock, sib_three, sums[chips // 2] = lax.optimization_barrier(
                (pair_density, inactive_fock, active_fock, sib_three, sums[chips // 2])
            )
        contributions.append(sums)

    other = hop(pair_density, twin)
    sib_three = [hop(x, twin) for x in sib_three]
    far = chips // 2
    first = [(hop(c[far], ahead), hop(c[far + 1], behind)) for c in contributions]
    first, other, sib_three = lax.optimization_barrier((first, other, sib_three))
    totals = []
    for c, (a, b) in zip(contributions, first):
        for s in range(1, far):
            a = hop(a + c[far - s], ahead)
            if s < chips - 1 - far:
                b = hop(b + c[far + 1 + s], behind)
        totals.append(c[0] + a + b)
    totals = lax.optimization_barrier(totals)

    far_at = chip_at(sign, far) * blk
    far_columns = [lax.dynamic_slice_in_dim(d, far_at, blk, 1) for d in (pair_density, other)]
    density_far = jnp.concatenate(
        [jnp.where(core == 0, far_columns[0], far_columns[1]), jnp.where(core == 0, far_columns[1], far_columns[0])],
        axis=0,
    )

    def gather(x):
        blocks = [None] * chips
        blocks[0] = a = b = x
        for s in range(1, far + 1):
            a = hop(a, ahead)
            blocks[(chips - s) % chips] = a
            if s < chips - far:
                b = hop(b, behind)
                blocks[s] = b
        return blocks

    gathered = [gather(x) for x in totals]
    near_blocks = [gathered[k][j] for j in range(chips) if j != far for k in range(2)]
    halves = half_partial(pair_density, other, near_blocks, mine[0], chips)
    halves = [h + jnp.dot(density_far, gathered[k][far], precision=HIGH) for k, h in enumerate(halves)]
    halves = lax.optimization_barrier(halves)
    q = 0.0
    for k, x in enumerate(halves):
        q = q + q_partial(three_index, shells, sib_three[k], gather(x), mine[k], chunk)
    q = q.reshape(chips, TILE, 2 * rows)[:, :nb].reshape(act, 2 * rows)

    share = rows // aux
    aux_at = lax.axis_index("aux")

    def across(x, orb_bits, aux_bits):
        table = [(o * aux + y, (o ^ orb_bits) * aux + (y ^ aux_bits)) for o in range(orb) for y in range(aux)]
        return lax.ppermute(x, ("orb", "aux"), table)

    closed = 2.0 * (inactive_fock[:, :inactive] + active_fock)
    opened = jnp.dot(inactive_fock[:, inactive:], one_density, precision=HIGHEST)
    closed_twin = hop(closed, twin)
    closed_chip = jnp.concatenate(
        [jnp.where(core == 0, closed, closed_twin), jnp.where(core == 0, closed_twin, closed)], axis=0
    )

    once = (aux_at == 0).astype(jnp.float32)
    own_q, twin_q = q[:, :rows] + once * opened.T, q[:, rows:]
    q_mine = own_q + hop(twin_q, twin)
    sent = lax.dynamic_slice_in_dim(q_mine, (1 - aux_at) * share, share, 1)
    q_rows = lax.dynamic_slice_in_dim(q_mine, aux_at * share, share, 1) + across(sent, 0, 1)

    occ_index = jnp.concatenate([jnp.arange(inactive, dtype=jnp.int32), active_orbitals])
    my_rows, twin_rows = first_row + local_rows, (me ^ 1) * rows + local_rows
    width = (inactive + act) // 2
    act_pick = (active_orbitals[:, None] == my_rows[None, :]).astype(jnp.float32) * once
    act_closed = jnp.pad(jnp.dot(act_pick, closed, precision=HIGHEST), ((0, 0), (0, act)))

    def picked(half):
        wanted = lax.dynamic_slice_in_dim(occ_index, half * width, width, 0)
        chosen = [(r[:, None] == wanted[None, :]).astype(jnp.float32) for r in (my_rows, twin_rows)]
        top = jnp.dot(jnp.concatenate([own_q, twin_q], axis=1), jnp.concatenate(chosen, axis=0), precision=HIGHEST)
        return jnp.concatenate([top, lax.dynamic_slice_in_dim(act_closed, half * width, width, 1)], axis=0)

    occ = picked(core) + hop(picked(1 - core), twin)
    occ = occ + across(occ, 2, 0) + across(occ, 0, 1) + across(occ, 2, 1)
    occ = occ + across(occ, 4, 0) + across(occ, 8, 0) + across(occ, 12, 0)
    occ_twin = hop(occ, twin)
    occ = jnp.concatenate([jnp.where(core == 0, occ, occ_twin), jnp.where(core == 0, occ_twin, occ)], axis=1)

    upper = jnp.concatenate([closed_chip[:inactive].T, occ[act:, :inactive].T], axis=1)
    occupied = jnp.concatenate([upper, occ[:act]], axis=0)

    mine_at = aux_at * share
    fock_mine = jnp.concatenate([lax.dynamic_slice_in_dim(closed, mine_at, share, 0), q_rows.T], axis=1)
    pick_rows = (first_row + mine_at + jnp.arange(share, dtype=jnp.int32))[:, None] == occ_index[None, :]
    transposed = jnp.dot(pick_rows.astype(jnp.float32), occupied, precision=HIGHEST)
    return 2.0 * (fock_mine - transposed)


def plain(orb, aux, three_index, pair_density, active_orbitals, screen_mask, one_density, inactive_fock, active_fock):
    act_count = three_index.shape[0]
    slab_count = three_index.shape[1]
    row_count = three_index.shape[2]
    inactive_count = active_fock.shape[1]
    orb_position = lax.axis_index("orb")
    kept_mask = jnp.repeat(
        jnp.repeat(screen_mask.astype(jnp.float32), slab_count // screen_mask.shape[0], axis=0),
        row_count // screen_mask.shape[1],
        axis=1,
    )
    screened = three_index * kept_mask[None]
    global_rows = orb_position * row_count + jnp.arange(row_count, dtype=jnp.int32)
    active_pick = (global_rows[:, None] == active_orbitals[None, :]).astype(jnp.float32)
    partial_pairs = jnp.einsum("wPp,pv->Pvw", screened, active_pick, precision=HIGHEST).reshape(
        slab_count, act_count * act_count
    )
    pairs = lax.psum(partial_pairs, "orb")
    column_block = jnp.dot(pairs, pair_density.T, precision=HIGHEST)
    half = lax.all_gather(column_block, "orb", axis=1, tiled=True)
    q_partial = jnp.einsum(
        "uPp,Ptu->pt", screened, half.reshape(slab_count, act_count, act_count), precision=HIGHEST
    )
    occ_index = jnp.concatenate([jnp.arange(inactive_count, dtype=jnp.int32), active_orbitals])
    row_share = row_count // aux
    aux_offset = lax.axis_index("aux") * row_share
    qmatrix = lax.psum(q_partial, "aux")
    inactive_cols = 2.0 * (inactive_fock[:, :inactive_count] + active_fock)
    active_cols = jnp.dot(inactive_fock[:, inactive_count:], one_density, precision=HIGHEST) + qmatrix
    fock = jnp.concatenate([inactive_cols, active_cols], axis=1)
    occ_pick = (global_rows[:, None] == occ_index[None, :]).astype(jnp.float32)
    occupied = lax.psum(jnp.dot(occ_pick.T, fock, precision=HIGHEST), "orb")
    fock_mine = lax.dynamic_slice_in_dim(fock, aux_offset, row_share, 0)
    pick_mine = lax.dynamic_slice_in_dim(occ_pick, aux_offset, row_share, 0)
    transposed = jnp.dot(pick_mine, occupied.T, precision=HIGHEST)
    return 2.0 * (fock_mine - transposed)


def shards(orb, aux, *args):
    act, slab, rows = args[0].shape
    chips = orb // 2
    fits = orb == 16 and aux == 2 and act % chips == 0 and act % TILE == 0
    fits = fits and args[6].shape[1] <= 2 * rows and (args[6].shape[1] + act) % 2 == 0
    fits = fits and slab % (4 * LANES) == 0 and rows % LANES == 0
    return (fast if fits else plain)(orb, aux, *args)


def solution(mesh):
    in_specs = (
        P(None, "aux", "orb"),
        P("orb", None),
        P(),
        P("aux", "orb"),
        P(),
        P("orb", None),
        P("orb", None),
    )
    out_specs = P(("orb", "aux"), None)
    body = functools.partial(shards, mesh.shape["orb"], mesh.shape["aux"])
    return jax.shard_map(body, mesh=mesh, in_specs=in_specs, out_specs=out_specs, check_vma=False)
```

time: 371 us -> 177 us (0.48)
  waiting for transfers between devices: 294 us -> 64.3 us
  starting transfers between devices: 0.27 us -> 57.9 us
  Pallas kernels: 0 us -> 38.7 us
  matrix products: 40.7 us -> 2.86 us
  between operations: 13.2 us -> 0.47 us
  blocking collectives: 8.33 us -> 0 us
    psum x2 -> x0, waiting for transfers between devices: 231 us -> none  [the longest x1 144 us: shards(): pairs = lax.psum(partial_pairs, 'orb')]
    ppermute x0 -> x58, waiting for transfers between devices: none -> 64.3 us  [the longest x51 56.7 us: hop(): return lax.ppermute(x, 'orb', pairs)]
    all_gather x1 -> x0, waiting for transfers between devices: 63.1 us -> none  [shards(): half = lax.all_gather(column_block, 'orb', axis=1, tiled=True)]
    ppermute x0 -> x58, starting transfers between devices: none -> 57.9 us  [the longest x51 49.3 us: hop(): return lax.ppermute(x, 'orb', pairs)]
    pallas_call x0 -> x7, Pallas kernels: none -> 38.7 us  [the longest x4 16.6 us: extract(): pl.pallas_call(functools.partial(extract_body, nb), out_shape=out_shape,...]
    dot_general x6 -> x7, matrix products: 40.7 us -> 2.86 us  [the longest x1 1 us: fast(): jnp.dot(pick_rows.astype(jnp.float32), occupied, precision=HIGHEST)]
    psum x1 -> x0, blocking collectives: 8.33 us -> none  [shards(): qmatrix = lax.psum(q_partial, 'aux')]
    transpose x1, local copies, waits for them, and re-layouts: 6.37 us -> 0.08 us  [fast(): fock_mine = jnp.concatenate([lax.dynamic_slice_in_dim(closed, mine_at, sh...]
  transfers between devices with their start and end apart: 3 -> 58, of which waited for: 3 -> 32; matrix products, arithmetic and copies ran while one was open for 0% -> 2% of each run, Pallas kernels for 0% -> 17%
where the time goes in v2:
time: 177 us
  waiting for transfers between devices  64.3 us (36%)
  starting transfers between devices  57.9 us (33%)
  Pallas kernels  38.7 us (22%)
  local copies, waits for them, and re-layouts  9.94 us (6%)
  matrix products  2.86 us (2%)
  other arithmetic  2.56 us (1%)
    ppermute x51, waiting for transfers between devices, hop(): return lax.ppermute(x, 'orb', pairs)  56.7 us
    ppermute x51, starting transfers between devices, hop(): return lax.ppermute(x, 'orb', pairs)  49.3 us
    pallas_call x4, Pallas kernels, extract(): pl.pallas_call(functools.partial(extract_body, nb), out_shape=out_shape,...  16.6 us
    pallas_call x2, Pallas kernels, q_partial(): pl.pallas_call(functools.partial(q_body, nb, count), out_shape=jax.ShapeD...  14.8 us
    unnamed x28, local copies, waits for them, and re-layouts  9.27 us
    ppermute x7, starting transfers between devices, across(): return lax.ppermute(x, ('orb', 'aux'), table)  8.52 us
    ppermute x7, waiting for transfers between devices, across(): return lax.ppermute(x, ('orb', 'aux'), table)  7.65 us
    pallas_call x1, Pallas kernels, half_partial(): pl.pallas_call(functools.partial(half_body, chips), out_shape=[jax.ShapeD...  7.29 us
  transfers between devices with their start and end apart: 58, of which 32 were waited for; matrix products, arithmetic and copies ran while one was open for 2% of the time, Pallas kernels for 17%

profile of v2, /device:TPU:0, one launch (start us, length us, event | category | flops | bytes accessed | tf_op | source)
XLA Modules:
  0.0 176.7 jit_solution(1650254253193533603)
XLA Ops:
  1.4 4.2 %extract.4 = (f32[56,56,128]{2,1,0:T(8,128)S(1)}, f32[56,128,128]{2,1,0:T(8,128)}) custom-call(s32[11]{0:T(128)S(1)} %get-tuple-element.102.info, s32[56]{0:T(128)S(1)} %copy-done.6, f32[56,512,128]{2,1,0:T(8,128)} %three.11, s32[8,32]{1,0:T(8,128)S(1)} %bitcast.90), custom_call_target="tpu_custom_call" | custom-call | flops 205520896 | bytes 8945664 | tf_op jit(solution)/shard_map/extract/pallas_call | solution.py:99
  6.2 4.1 %extract.5 = f32[56,56,128]{2,1,0:T(8,128)S(1)} custom-call(s32[11]{0:T(128)S(1)} %get-tuple-element.99.info, s32[56]{0:T(128)S(1)} %copy-done.7, f32[56,512,128]{2,1,0:T(8,128)} %three.11, s32[8,32]{1,0:T(8,128)S(1)} %bitcast.91), custom_call_target="tpu_custom_call" | custom-call | flops 205520896 | bytes 5275648 | tf_op jit(solution)/shard_map/extract/pallas_call | solution.py:99
  10.6 4.2 %extract.6 = (f32[56,56,128]{2,1,0:T(8,128)S(1)}, f32[56,128,128]{2,1,0:T(8,128)}) custom-call(s32[11]{0:T(128)S(1)} %get-tuple-element.33.info, s32[56]{0:T(128)S(1)} %copy-done.7, f32[56,512,128]{2,1,0:T(8,128)} %three.11, s32[8,32]{1,0:T(8,128)S(1)} %bitcast.92), custom_call_target="tpu_custom_call" | custom-call | flops 205520896 | bytes 8945664 | tf_op jit(solution)/shard_map/extract/pallas_call | solution.py:99
  14.9 4.1 %extract.7 = f32[56,56,128]{2,1,0:T(8,128)S(1)} custom-call(s32[11]{0:T(128)S(1)} %get-tuple-element.35.info, s32[56]{0:T(128)S(1)} %copy-done.7, f32[56,512,128]{2,1,0:T(8,128)} %three.11, s32[8,32]{1,0:T(8,128)S(1)} %bitcast.93), custom_call_target="tpu_custom_call" | custom-call | flops 205520896 | bytes 5275648 | tf_op jit(solution)/shard_map/extract/pallas_call | solution.py:99
  21.2 3.1 %collective-permute-start.2 = (f32[392,128]{1,0:T(8,128)S(1)}, f32[392,128]{1,0:T(8,128)S(1)}, u32[]{:S(2)}, u32[]{:S(2)}) collective-permute-start(f32[392,128]{1,0:T(8,128)S(1)} %get-tuple-element.39), channel_id=1, source_target_pairs={{0,8},{8,16},{16,24},{24,28},{28,20},{20,12},{12,4},{4,0},{10,2},{... | collective-permute-start | bytes 602120 | tf_op jit(solution)/shard_map/ppermute | solution.py:313
  24.3 4.9 %collective-permute-done.2 = f32[392,128]{1,0:T(8,128)S(1)} collective-permute-done((f32[392,128]{1,0:T(8,128)S(1)}, f32[392,128]{1,0:T(8,128)S(1)}, u32[]{:S(2)}, u32[]{:S(2)}) %collective-permute-start.2) | collective-permute-done | bytes 200736 | tf_op jit(solution)/shard_map/ppermute | solution.py:313
  29.2 2.5 %collective-permute-start.4 = (f32[392,128]{1,0:T(8,128)S(1)}, f32[392,128]{1,0:T(8,128)S(1)}, u32[]{:S(2)}, u32[]{:S(2)}) collective-permute-start(f32[392,128]{1,0:T(8,128)S(1)} %get-tuple-element.40), channel_id=1, source_target_pairs={{0,8},{8,16},{16,24},{24,28},{28,20},{20,12},{12,4},{4,0},{10,2},{... | collective-permute-start | bytes 602120 | tf_op jit(solution)/shard_map/ppermute | solution.py:313
  31.7 4.9 %collective-permute-done.4 = f32[392,128]{1,0:T(8,128)S(1)} collective-permute-done((f32[392,128]{1,0:T(8,128)S(1)}, f32[392,128]{1,0:T(8,128)S(1)}, u32[]{:S(2)}, u32[]{:S(2)}) %collective-permute-start.4) | collective-permute-done | bytes 200736 | tf_op jit(solution)/shard_map/ppermute | solution.py:313
  38.9 1.8 %copy-done.8 = f32[56,128,128]{2,1,0:T(8,128)} copy-done((f32[56,128,128]{2,1,0:T(8,128)}, f32[56,128,128]{2,1,0:T(8,128)S(1)}, u32[]{:S(2)}) %copy-start.8) | copy-done | bytes 3670040
  40.8 1.9 %copy-done.9 = f32[56,128,128]{2,1,0:T(8,128)} copy-done((f32[56,128,128]{2,1,0:T(8,128)}, f32[56,128,128]{2,1,0:T(8,128)S(1)}, u32[]{:S(2)}) %copy-start.9) | copy-done | bytes 3670040
  42.7 1.8 %collective-permute-start.14 = (f32[392,128]{1,0:T(8,128)S(1)}, f32[392,128]{1,0:T(8,128)S(1)}, u32[]{:S(2)}, u32[]{:S(2)}) collective-permute-start(f32[392,128]{1,0:T(8,128)S(1)} %fusion.13), channel_id=1, source_target_pairs={{0,8},{8,16},{16,24},{24,28},{28,20},{20,12},{12,4},{4,0},{10,2},{... | collective-permute-start | bytes 602120 | tf_op jit(solution)/shard_map/ppermute | solution.py:313
  46.1 2.3 %collective-permute-done.14 = f32[392,128]{1,0:T(8,128)S(1)} collective-permute-done((f32[392,128]{1,0:T(8,128)S(1)}, f32[392,128]{1,0:T(8,128)S(1)}, u32[]{:S(2)}, u32[]{:S(2)}) %collective-permute-start.14) | collective-permute-done | bytes 200736 | tf_op jit(solution)/shard_map/ppermute | solution.py:313
  48.5 1.8 %collective-permute-start.15 = (f32[392,128]{1,0:T(8,128)S(1)}, f32[392,128]{1,0:T(8,128)S(1)}, u32[]{:S(2)}, u32[]{:S(2)}) collective-permute-start(f32[392,128]{1,0:T(8,128)S(1)} %get-tuple-element.69), channel_id=1, source_target_pairs={{0,8},{8,16},{16,24},{24,28},{28,20},{20,12},{12,4},{4,0},{10,2},{... | collective-permute-start | bytes 602120 | tf_op jit(solution)/shard_map/ppermute | solution.py:313
  50.7 2.6 %collective-permute-start.10 = (f32[392,128]{1,0:T(8,128)S(1)}, f32[392,128]{1,0:T(8,128)S(1)}, u32[]{:S(2)}, u32[]{:S(2)}) collective-permute-start(f32[392,128]{1,0:T(8,128)S(1)} %get-tuple-element.81), channel_id=1, source_target_pairs={{0,8},{8,16},{16,24},{24,28},{28,20},{20,12},{12,4},{4,0},{10,2},{... | collective-permute-start | bytes 602120 | tf_op jit(solution)/shard_map/ppermute | solution.py:313
  53.4 3.0 %collective-permute-done.15 = f32[392,128]{1,0:T(8,128)S(1)} collective-permute-done((f32[392,128]{1,0:T(8,128)S(1)}, f32[392,128]{1,0:T(8,128)S(1)}, u32[]{:S(2)}, u32[]{:S(2)}) %collective-permute-start.15) | collective-permute-done | bytes 200736 | tf_op jit(solution)/shard_map/ppermute | solution.py:313
  62.8 2.1 %collective-permute-done.16 = f32[392,128]{1,0:T(8,128)S(1)} collective-permute-done((f32[392,128]{1,0:T(8,128)S(1)}, f32[392,128]{1,0:T(8,128)S(1)}, u32[]{:S(2)}, u32[]{:S(2)}) %collective-permute-start.16) | collective-permute-done | bytes 200736 | tf_op jit(solution)/shard_map/ppermute | solution.py:313
  65.5 3.4 %collective-permute-done.11 = f32[392,128]{1,0:T(8,128)S(1)} collective-permute-done((f32[392,128]{1,0:T(8,128)S(1)}, f32[392,128]{1,0:T(8,128)S(1)}, u32[]{:S(2)}, u32[]{:S(2)}) %collective-permute-start.11) | collective-permute-done | bytes 200736 | tf_op jit(solution)/shard_map/ppermute | solution.py:313
  73.1 3.8 %collective-permute-done.28.refs_13_ = f32[392,128]{1,0:T(8,128)S(1)} collective-permute-done((f32[392,128]{1,0:T(8,128)S(1)}, f32[392,128]{1,0:T(8,128)S(1)}, u32[]{:S(2)}, u32[]{:S(2)}) %collective-permute-start.28) | collective-permute-done | bytes 200736 | tf_op jit(solution)/shard_map/ppermute | solution.py:313
  79.0 3.3 %collective-permute-done.20.refs_3_ = f32[392,128]{1,0:T(8,128)} collective-permute-done((f32[392,128]{1,0:T(8,128)S(1)}, f32[392,128]{1,0:T(8,128)}, u32[]{:S(2)}, u32[]{:S(2)}) %collective-permute-start.20) | collective-permute-done | bytes 200736 | tf_op jit(solution)/shard_map/ppermute | solution.py:313
  87.6 2.8 %collective-permute-done.22.refs_5_ = f32[392,128]{1,0:T(8,128)S(1)} collective-permute-done((f32[392,128]{1,0:T(8,128)}, f32[392,128]{1,0:T(8,128)S(1)}, u32[]{:S(2)}, u32[]{:S(2)}) %collective-permute-start.22) | collective-permute-done | bytes 200736 | tf_op jit(solution)/shard_map/ppermute | solution.py:313
  92.5 3.3 %collective-permute-done.30.refs_9_ = f32[392,128]{1,0:T(8,128)S(1)} collective-permute-done((f32[392,128]{1,0:T(8,128)S(1)}, f32[392,128]{1,0:T(8,128)S(1)}, u32[]{:S(2)}, u32[]{:S(2)}) %collective-permute-start.30) | collective-permute-done | bytes 200736 | tf_op jit(solution)/shard_map/ppermute | solution.py:313
  100.7 7.3 %half.1 = (f32[392,128]{1,0:T(8,128)S(1)}, f32[392,128]{1,0:T(8,128)S(1)}) custom-call(s32[11]{0:T(128)S(1)} %get-tuple-element.99.info, f32[196,3136]{1,0:T(8,128)S(1)} %copy-done.1, f32[196,3136]{1,0:T(8,128)S(1)} %copy-done.3, f32[392,128]{1,0:T(8,128)S(1)} %fusion.22.refs_0_, f32[392,128]{1,0:T(8,128)S(1)} %fusion.15.refs_1_, ...), custom_call_target="tpu_custom_call" | custom-call | flops 1888223232 | bytes 8128512 | tf_op jit(solution)/shard_map/half/pallas_call | solution.py:260
  113.4 3.6 %collective-permute-done.43 = f32[392,128]{1,0:T(8,128)S(1)} collective-permute-done((f32[392,128]{1,0:T(8,128)S(1)}, f32[392,128]{1,0:T(8,128)S(1)}, u32[]{:S(2)}, u32[]{:S(2)}) %collective-permute-start.43) | collective-permute-done | bytes 200736 | tf_op jit(solution)/shard_map/ppermute | solution.py:313
  121.4 2.0 %collective-permute-done.33 = f32[392,128]{1,0:T(8,128)S(1)} collective-permute-done((f32[392,128]{1,0:T(8,128)S(1)}, f32[392,128]{1,0:T(8,128)S(1)}, u32[]{:S(2)}, u32[]{:S(2)}) %collective-permute-start.33) | collective-permute-done | bytes 200736 | tf_op jit(solution)/shard_map/ppermute | solution.py:313
  125.6 2.3 %collective-permute-start.38 = (f32[392,128]{1,0:T(8,128)S(1)}, f32[392,128]{1,0:T(8,128)S(1)}, u32[]{:S(2)}, u32[]{:S(2)}) collective-permute-start(f32[392,128]{1,0:T(8,128)S(1)} %collective-permute-done.37), channel_id=1, source_target_pairs={{0,8},{8,16},{16,24},{24,28},{28,20},{20,12},{12,4},{4,0},{10,2},{... | collective-permute-start | bytes 602120 | tf_op jit(solution)/shard_map/ppermute | solution.py:313
  128.3 4.0 %collective-permute-done.34 = f32[392,128]{1,0:T(8,128)S(1)} collective-permute-done((f32[392,128]{1,0:T(8,128)S(1)}, f32[392,128]{1,0:T(8,128)S(1)}, u32[]{:S(2)}, u32[]{:S(2)}) %collective-permute-start.34) | collective-permute-done | bytes 200736 | tf_op jit(solution)/shard_map/ppermute | solution.py:313
  132.3 2.2 %collective-permute-start.46 = (f32[392,128]{1,0:T(8,128)S(1)}, f32[392,128]{1,0:T(8,128)S(1)}, u32[]{:S(2)}, u32[]{:S(2)}) collective-permute-start(f32[392,128]{1,0:T(8,128)S(1)} %collective-permute-done.45), channel_id=1, source_target_pairs={{0,8},{8,16},{16,24},{24,28},{28,20},{20,12},{12,4},{4,0},{10,2},{... | collective-permute-start | bytes 602120 | tf_op jit(solution)/shard_map/ppermute | solution.py:313
  137.7 2.3 %collective-permute-done.46 = f32[392,128]{1,0:T(8,128)S(1)} collective-permute-done((f32[392,128]{1,0:T(8,128)S(1)}, f32[392,128]{1,0:T(8,128)S(1)}, u32[]{:S(2)}, u32[]{:S(2)}) %collective-permute-start.46) | collective-permute-done | bytes 200736 | tf_op jit(solution)/shard_map/ppermute | solution.py:313
  140.0 7.4 %qpartial.3 = f32[64,256]{1,0:T(8,128)S(1)} custom-call(s32[11]{0:T(128)S(1)} %get-tuple-element.35.info, f32[56,512,128]{2,1,0:T(8,128)} %three.11, s32[8,32]{1,0:T(8,128)S(1)} %bitcast.94, f32[56,128,128]{2,1,0:T(8,128)} %copy-done.9, f32[7,56,128]{2,1,0:T(8,128)S(1)} %bitcast.75, f32[7,56,128]{2,1,0:T(8,128)S(1)} %bitcast.79, f32[7,56,128]{2,1,0:T(8,128)S(1)} %bitcast.83, ...), custom_call_target="tpu_custom_call" | custom-call | flops 616562688 | bytes 8945664 | tf_op jit(solution)/shard_map/qpartial/pallas_call | solution.py:183
  147.4 7.4 %qpartial.2 = f32[64,256]{1,0:T(8,128)S(1)} custom-call(s32[11]{0:T(128)S(1)} %get-tuple-element.99.info, f32[56,512,128]{2,1,0:T(8,128)} %three.11, s32[8,32]{1,0:T(8,128)S(1)} %bitcast.95, f32[56,128,128]{2,1,0:T(8,128)} %copy-done.8, f32[7,56,128]{2,1,0:T(8,128)S(1)} %bitcast.74, f32[7,56,128]{2,1,0:T(8,128)S(1)} %bitcast.78, f32[7,56,128]{2,1,0:T(8,128)S(1)} %bitcast.82, ...), custom_call_target="tpu_custom_call" | custom-call | flops 616562688 | bytes 8945664 | tf_op jit(solution)/shard_map/qpartial/pallas_call | solution.py:183
  162.7 2.4 %collective-permute-done.53 = f32[112,128]{1,0:T(8,128)S(1)} collective-permute-done((f32[112,128]{1,0:T(8,128)S(1)}, f32[112,128]{1,0:T(8,128)S(1)}, u32[]{:S(2)}, u32[]{:S(2)}) %collective-permute-start.53) | collective-permute-done | bytes 57376 | tf_op jit(solution)/shard_map/ppermute | solution.py:383
  170.2 2.5 %collective-permute-done.55 = f32[112,128]{1,0:T(8,128)S(1)} collective-permute-done((f32[112,128]{1,0:T(8,128)S(1)}, f32[112,128]{1,0:T(8,128)S(1)}, u32[]{:S(2)}, u32[]{:S(2)}) %collective-permute-start.55) | collective-permute-done | bytes 57376 | tf_op jit(solution)/shard_map/ppermute | solution.py:383
  (168 shorter events, 66.8 us)
Async XLA Ops:
  19.3 19.7 %collective-permute-start.7 = (f32[56,128,128]{2,1,0:T(8,128)}, f32[56,128,128]{2,1,0:T(8,128)S(1)}, u32[]{:S(2)}, u32[]{:S(2)}) collective-permute-start(f32[56,128,128]{2,1,0:T(8,128)} %get-tuple-element.42), channel_id=1, source_target_pairs={{0,2},{2,0},{4,6},{6,4},{8,10},{10,8},{12,14},{14,12},{16,18},{18,... | collective-permute-start | bytes 11010056 | tf_op jit(solution)/shard_map/ppermute | solution.py:313
  19.8 21.0 %collective-permute-start.8 = (f32[56,128,128]{2,1,0:T(8,128)}, f32[56,128,128]{2,1,0:T(8,128)S(1)}, u32[]{:S(2)}, u32[]{:S(2)}) collective-permute-start(f32[56,128,128]{2,1,0:T(8,128)} %get-tuple-element.43), channel_id=1, source_target_pairs={{0,2},{2,0},{4,6},{6,4},{8,10},{10,8},{12,14},{14,12},{16,18},{18,... | collective-permute-start | bytes 11010056 | tf_op jit(solution)/shard_map/ppermute | solution.py:313
  20.8 16.6 %collective-permute-start.6 = (f32[196,3136]{1,0:T(8,128)S(1)}, f32[196,3136]{1,0:T(8,128)S(1)}, u32[]{:S(2)}, u32[]{:S(2)}) collective-permute-start(f32[196,3136]{1,0:T(8,128)S(1)} %copy-done.1), channel_id=1, source_target_pairs={{0,2},{2,0},{4,6},{6,4},{8,10},{10,8},{12,14},{14,12},{16,18},{18,... | collective-permute-start | bytes 7375880 | tf_op jit(solution)/shard_map/ppermute | solution.py:313
  21.2 7.9 %collective-permute-start.2 = (f32[392,128]{1,0:T(8,128)S(1)}, f32[392,128]{1,0:T(8,128)S(1)}, u32[]{:S(2)}, u32[]{:S(2)}) collective-permute-start(f32[392,128]{1,0:T(8,128)S(1)} %get-tuple-element.39), channel_id=1, source_target_pairs={{0,8},{8,16},{16,24},{24,28},{28,20},{20,12},{12,4},{4,0},{10,2},{... | collective-permute-start | bytes 602120 | tf_op jit(solution)/shard_map/ppermute | solution.py:313
  48.5 7.8 %collective-permute-start.15 = (f32[392,128]{1,0:T(8,128)S(1)}, f32[392,128]{1,0:T(8,128)S(1)}, u32[]{:S(2)}, u32[]{:S(2)}) collective-permute-start(f32[392,128]{1,0:T(8,128)S(1)} %get-tuple-element.69), channel_id=1, source_target_pairs={{0,8},{8,16},{16,24},{24,28},{28,20},{20,12},{12,4},{4,0},{10,2},{... | collective-permute-start | bytes 602120 | tf_op jit(solution)/shard_map/ppermute | solution.py:313
  50.7 10.0 %collective-permute-start.10 = (f32[392,128]{1,0:T(8,128)S(1)}, f32[392,128]{1,0:T(8,128)S(1)}, u32[]{:S(2)}, u32[]{:S(2)}) collective-permute-start(f32[392,128]{1,0:T(8,128)S(1)} %get-tuple-element.81), channel_id=1, source_target_pairs={{0,8},{8,16},{16,24},{24,28},{28,20},{20,12},{12,4},{4,0},{10,2},{... | collective-permute-start | bytes 602120 | tf_op jit(solution)/shard_map/ppermute | solution.py:313
  56.8 8.1 %collective-permute-start.16 = (f32[392,128]{1,0:T(8,128)S(1)}, f32[392,128]{1,0:T(8,128)S(1)}, u32[]{:S(2)}, u32[]{:S(2)}) collective-permute-start(f32[392,128]{1,0:T(8,128)S(1)} %get-tuple-element.67), channel_id=1, source_target_pairs={{0,8},{8,16},{16,24},{24,28},{28,20},{20,12},{12,4},{4,0},{10,2},{... | collective-permute-start | bytes 602120 | tf_op jit(solution)/shard_map/ppermute | solution.py:313
  60.8 8.2 %collective-permute-start.11 = (f32[392,128]{1,0:T(8,128)S(1)}, f32[392,128]{1,0:T(8,128)S(1)}, u32[]{:S(2)}, u32[]{:S(2)}) collective-permute-start(f32[392,128]{1,0:T(8,128)S(1)} %get-tuple-element.79), channel_id=1, source_target_pairs={{0,8},{8,16},{16,24},{24,28},{28,20},{20,12},{12,4},{4,0},{10,2},{... | collective-permute-start | bytes 602120 | tf_op jit(solution)/shard_map/ppermute | solution.py:313
  69.0 7.9 %collective-permute-start.28 = (f32[392,128]{1,0:T(8,128)S(1)}, f32[392,128]{1,0:T(8,128)S(1)}, u32[]{:S(2)}, u32[]{:S(2)}) collective-permute-start(f32[392,128]{1,0:T(8,128)S(1)} %fusion.15.refs_1_), channel_id=1, source_target_pairs={{0,8},{8,16},{16,24},{24,28},{28,20},{20,12},{12,4},{4,0},{10,2},{... | collective-permute-start | bytes 602120 | tf_op jit(solution)/shard_map/ppermute | solution.py:313
  70.1 7.9 %collective-permute-start.19 = (f32[392,128]{1,0:T(8,128)S(1)}, f32[392,128]{1,0:T(8,128)S(1)}, u32[]{:S(2)}, u32[]{:S(2)}) collective-permute-start(f32[392,128]{1,0:T(8,128)S(1)} %fusion.22.refs_0_), channel_id=1, source_target_pairs={{8,0},{16,8},{24,16},{28,24},{20,28},{12,20},{4,12},{0,4},{2,10},{... | collective-permute-start | bytes 602120 | tf_op jit(solution)/shard_map/ppermute | solution.py:313
  71.1 11.2 %collective-permute-start.20 = (f32[392,128]{1,0:T(8,128)S(1)}, f32[392,128]{1,0:T(8,128)}, u32[]{:S(2)}, u32[]{:S(2)}) collective-permute-start(f32[392,128]{1,0:T(8,128)S(1)} %fusion.15.refs_1_), channel_id=1, source_target_pairs={{8,0},{16,8},{24,16},{28,24},{20,28},{12,20},{4,12},{0,4},{2,10},{... | collective-permute-start | bytes 602120 | tf_op jit(solution)/shard_map/ppermute | solution.py:313
  72.6 10.8 %collective-permute-start.25 = (f32[392,128]{1,0:T(8,128)S(1)}, f32[392,128]{1,0:T(8,128)}, u32[]{:S(2)}, u32[]{:S(2)}) collective-permute-start(f32[392,128]{1,0:T(8,128)S(1)} %fusion.22.refs_0_), channel_id=1, source_target_pairs={{0,8},{8,16},{16,24},{24,28},{28,20},{20,12},{12,4},{4,0},{10,2},{... | collective-permute-start | bytes 602120 | tf_op jit(solution)/shard_map/ppermute | solution.py:313
  76.9 8.6 %collective-permute-start.29 = (f32[392,128]{1,0:T(8,128)S(1)}, f32[392,128]{1,0:T(8,128)S(1)}, u32[]{:S(2)}, u32[]{:S(2)}) collective-permute-start(f32[392,128]{1,0:T(8,128)S(1)} %collective-permute-done.28.refs_13_), channel_id=1, source_target_pairs={{0,8},{8,16},{16,24},{24,28},{28,20},{20,12},{12,4},{4,0},{10,2},{... | collective-permute-start | bytes 602120 | tf_op jit(solution)/shard_map/ppermute | solution.py:313
  78.0 8.5 %collective-permute-start.21 = (f32[392,128]{1,0:T(8,128)S(1)}, f32[392,128]{1,0:T(8,128)S(1)}, u32[]{:S(2)}, u32[]{:S(2)}) collective-permute-start(f32[392,128]{1,0:T(8,128)S(1)} %collective-permute-done.19.refs_2_), channel_id=1, source_target_pairs={{8,0},{16,8},{24,16},{28,24},{20,28},{12,20},{4,12},{0,4},{2,10},{... | collective-permute-start | bytes 602120 | tf_op jit(solution)/shard_map/ppermute | solution.py:313
  82.3 8.1 %collective-permute-start.22 = (f32[392,128]{1,0:T(8,128)}, f32[392,128]{1,0:T(8,128)S(1)}, u32[]{:S(2)}, u32[]{:S(2)}) collective-permute-start(f32[392,128]{1,0:T(8,128)} %collective-permute-done.20.refs_3_), channel_id=1, source_target_pairs={{8,0},{16,8},{24,16},{28,24},{20,28},{12,20},{4,12},{0,4},{2,10},{... | collective-permute-start | bytes 602120 | tf_op jit(solution)/shard_map/ppermute | solution.py:313
  83.4 8.1 %collective-permute-start.26 = (f32[392,128]{1,0:T(8,128)}, f32[392,128]{1,0:T(8,128)S(1)}, u32[]{:S(2)}, u32[]{:S(2)}) collective-permute-start(f32[392,128]{1,0:T(8,128)} %collective-permute-done.25.refs_12_), channel_id=1, source_target_pairs={{0,8},{8,16},{16,24},{24,28},{28,20},{20,12},{12,4},{4,0},{10,2},{... | collective-permute-start | bytes 602120 | tf_op jit(solution)/shard_map/ppermute | solution.py:313
  85.5 10.2 %collective-permute-start.30 = (f32[392,128]{1,0:T(8,128)S(1)}, f32[392,128]{1,0:T(8,128)S(1)}, u32[]{:S(2)}, u32[]{:S(2)}) collective-permute-start(f32[392,128]{1,0:T(8,128)S(1)} %collective-permute-done.29.refs_11_), channel_id=1, source_target_pairs={{0,8},{8,16},{16,24},{24,28},{28,20},{20,12},{12,4},{4,0},{10,2},{... | collective-permute-start | bytes 602120 | tf_op jit(solution)/shard_map/ppermute | solution.py:313
  86.6 12.4 %collective-permute-start.23 = (f32[392,128]{1,0:T(8,128)S(1)}, f32[392,128]{1,0:T(8,128)S(1)}, u32[]{:S(2)}, u32[]{:S(2)}) collective-permute-start(f32[392,128]{1,0:T(8,128)S(1)} %collective-permute-done.21.refs_4_), channel_id=1, source_target_pairs={{8,0},{16,8},{24,16},{28,24},{20,28},{12,20},{4,12},{0,4},{2,10},{... | collective-permute-start | bytes 602120 | tf_op jit(solution)/shard_map/ppermute | solution.py:313
  90.4 8.6 %collective-permute-start.24 = (f32[392,128]{1,0:T(8,128)S(1)}, f32[392,128]{1,0:T(8,128)S(1)}, u32[]{:S(2)}, u32[]{:S(2)}) collective-permute-start(f32[392,128]{1,0:T(8,128)S(1)} %collective-permute-done.22.refs_5_), channel_id=1, source_target_pairs={{8,0},{16,8},{24,16},{28,24},{20,28},{12,20},{4,12},{0,4},{2,10},{... | collective-permute-start | bytes 602120 | tf_op jit(solution)/shard_map/ppermute | solution.py:313
  95.8 12.3 %collective-permute-start.32 = (f32[392,128]{1,0:T(8,128)S(1)}, f32[392,128]{1,0:T(8,128)S(1)}, u32[]{:S(2)}, u32[]{:S(2)}) collective-permute-start(f32[392,128]{1,0:T(8,128)S(1)} %collective-permute-done.30.refs_9_), channel_id=1, source_target_pairs={{0,8},{8,16},{16,24},{24,28},{28,20},{20,12},{12,4},{4,0},{10,2},{... | collective-permute-start | bytes 602120 | tf_op jit(solution)/shard_map/ppermute | solution.py:313
  98.4 10.1 %collective-permute-start.31 = (f32[392,128]{1,0:T(8,128)S(1)}, f32[392,128]{1,0:T(8,128)S(1)}, u32[]{:S(2)}, u32[]{:S(2)}) collective-permute-start(f32[392,128]{1,0:T(8,128)S(1)} %collective-permute-done.27.refs_8_), channel_id=1, source_target_pairs={{0,8},{8,16},{16,24},{24,28},{28,20},{20,12},{12,4},{4,0},{10,2},{... | collective-permute-start | bytes 602120 | tf_op jit(solution)/shard_map/ppermute | solution.py:313
  109.0 8.0 %collective-permute-start.43 = (f32[392,128]{1,0:T(8,128)S(1)}, f32[392,128]{1,0:T(8,128)S(1)}, u32[]{:S(2)}, u32[]{:S(2)}) collective-permute-start(f32[392,128]{1,0:T(8,128)S(1)} %convolution_add_fusion), channel_id=1, source_target_pairs={{0,8},{8,16},{16,24},{24,28},{28,20},{20,12},{12,4},{4,0},{10,2},{... | collective-permute-start | bytes 602120 | tf_op jit(solution)/shard_map/ppermute | solution.py:313
  110.3 8.8 %collective-permute-start.36 = (f32[392,128]{1,0:T(8,128)S(1)}, f32[392,128]{1,0:T(8,128)S(1)}, u32[]{:S(2)}, u32[]{:S(2)}) collective-permute-start(f32[392,128]{1,0:T(8,128)S(1)} %convolution_add_fusion.1), channel_id=1, source_target_pairs={{0,8},{8,16},{16,24},{24,28},{28,20},{20,12},{12,4},{4,0},{10,2},{... | collective-permute-start | bytes 602120 | tf_op jit(solution)/shard_map/ppermute | solution.py:313
  111.8 9.2 %collective-permute-start.40 = (f32[392,128]{1,0:T(8,128)S(1)}, f32[392,128]{1,0:T(8,128)S(1)}, u32[]{:S(2)}, u32[]{:S(2)}) collective-permute-start(f32[392,128]{1,0:T(8,128)S(1)} %convolution_add_fusion), channel_id=1, source_target_pairs={{8,0},{16,8},{24,16},{28,24},{20,28},{12,20},{4,12},{0,4},{2,10},{... | collective-permute-start | bytes 602120 | tf_op jit(solution)/shard_map/ppermute | solution.py:313
  112.6 10.7 %collective-permute-start.33 = (f32[392,128]{1,0:T(8,128)S(1)}, f32[392,128]{1,0:T(8,128)S(1)}, u32[]{:S(2)}, u32[]{:S(2)}) collective-permute-start(f32[392,128]{1,0:T(8,128)S(1)} %convolution_add_fusion.1), channel_id=1, source_target_pairs={{8,0},{16,8},{24,16},{28,24},{20,28},{12,20},{4,12},{0,4},{2,10},{... | collective-permute-start | bytes 602120 | tf_op jit(solution)/shard_map/ppermute | solution.py:313
  120.9 34.0 %collective-permute-start.49 = (f32[128,200]{1,0:T(8,128)S(1)}, f32[128,200]{1,0:T(8,128)S(1)}, u32[]{:S(2)}, u32[]{:S(2)}) collective-permute-start(f32[128,200]{1,0:T(8,128)S(1)} %add_multiply_fusion), channel_id=1, source_target_pairs={{0,2},{2,0},{4,6},{6,4},{8,10},{10,8},{12,14},{14,12},{16,18},{18,... | collective-permute-start | bytes 307208 | tf_op jit(solution)/shard_map/ppermute | solution.py:313
  123.4 8.9 %collective-permute-start.34 = (f32[392,128]{1,0:T(8,128)S(1)}, f32[392,128]{1,0:T(8,128)S(1)}, u32[]{:S(2)}, u32[]{:S(2)}) collective-permute-start(f32[392,128]{1,0:T(8,128)S(1)} %collective-permute-done.33), channel_id=1, source_target_pairs={{8,0},{16,8},{24,16},{28,24},{20,28},{12,20},{4,12},{0,4},{2,10},{... | collective-permute-start | bytes 602120 | tf_op jit(solution)/shard_map/ppermute | solution.py:313
  123.7 8.6 %collective-permute-start.45 = (f32[392,128]{1,0:T(8,128)S(1)}, f32[392,128]{1,0:T(8,128)S(1)}, u32[]{:S(2)}, u32[]{:S(2)}) collective-permute-start(f32[392,128]{1,0:T(8,128)S(1)} %collective-permute-done.44), channel_id=1, source_target_pairs={{0,8},{8,16},{16,24},{24,28},{28,20},{20,12},{12,4},{4,0},{10,2},{... | collective-permute-start | bytes 602120 | tf_op jit(solution)/shard_map/ppermute | solution.py:313
  125.6 10.3 %collective-permute-start.38 = (f32[392,128]{1,0:T(8,128)S(1)}, f32[392,128]{1,0:T(8,128)S(1)}, u32[]{:S(2)}, u32[]{:S(2)}) collective-permute-start(f32[392,128]{1,0:T(8,128)S(1)} %collective-permute-done.37), channel_id=1, source_target_pairs={{0,8},{8,16},{16,24},{24,28},{28,20},{20,12},{12,4},{4,0},{10,2},{... | collective-permute-start | bytes 602120 | tf_op jit(solution)/shard_map/ppermute | solution.py:313
  128.2 9.4 %collective-permute-start.42 = (f32[392,128]{1,0:T(8,128)S(1)}, f32[392,128]{1,0:T(8,128)S(1)}, u32[]{:S(2)}, u32[]{:S(2)}) collective-permute-start(f32[392,128]{1,0:T(8,128)S(1)} %collective-permute-done.41), channel_id=1, source_target_pairs={{8,0},{16,8},{24,16},{28,24},{20,28},{12,20},{4,12},{0,4},{2,10},{... | collective-permute-start | bytes 602120 | tf_op jit(solution)/shard_map/ppermute | solution.py:313
  132.3 15.1 %collective-permute-start.35 = (f32[392,128]{1,0:T(8,128)S(1)}, f32[392,128]{1,0:T(8,128)S(1)}, u32[]{:S(2)}, u32[]{:S(2)}) collective-permute-start(f32[392,128]{1,0:T(8,128)S(1)} %collective-permute-done.34), channel_id=1, source_target_pairs={{8,0},{16,8},{24,16},{28,24},{20,28},{12,20},{4,12},{0,4},{2,10},{... | collective-permute-start | bytes 602120 | tf_op jit(solution)/shard_map/ppermute | solution.py:313
  135.9 11.5 %collective-permute-start.39 = (f32[392,128]{1,0:T(8,128)S(1)}, f32[392,128]{1,0:T(8,128)S(1)}, u32[]{:S(2)}, u32[]{:S(2)}) collective-permute-start(f32[392,128]{1,0:T(8,128)S(1)} %collective-permute-done.38), channel_id=1, source_target_pairs={{0,8},{8,16},{16,24},{24,28},{28,20},{20,12},{12,4},{4,0},{10,2},{... | collective-permute-start | bytes 602120 | tf_op jit(solution)/shard_map/ppermute | solution.py:313
  (40 other events, 365.1 us)

commit v3 on v2

--- a/solution.py
+++ b/solution.py
@@ -27,12 +27,12 @@
     return tuple(pl.BlockSpec(memory_space=m) for m in (pltpu.SMEM, pltpu.VMEM, pltpu.HBM, pl.ANY))
 
 
-def expand_mask(screen, quarter, chunk, rows):
+def expand_mask(screen, half, chunk, rows):
     shells, blocks = screen.shape
-    slab_rows = 4 * chunk // blocks
+    slab_rows = 2 * chunk // blocks
     row = lax.broadcasted_iota(jnp.int32, (chunk, blocks), 0) // slab_rows
     col = lax.broadcasted_iota(jnp.int32, (chunk, blocks), 1)
-    down = (col == row + quarter * (blocks // 4)).astype(jnp.bfloat16)
+    down = (col == row + half * (blocks // 2)).astype(jnp.bfloat16)
     shell = lax.broadcasted_iota(jnp.int32, (shells, rows), 0)
     across = (shell == lax.broadcasted_iota(jnp.int32, (shells, rows), 1) // (rows // shells)).astype(jnp.bfloat16)
     tall = mxu(down, screen[...].astype(jnp.float32).astype(jnp.bfloat16), ((1,), (1,)))
@@ -40,9 +40,9 @@
 
 
 def extract_body(nb, info, active, three, screen, pairs, *refs):
-    kept = refs[0] if len(refs) == 8 else None
+    kept = refs[0]
     value, turned, found, mask, sem_in, sem_out, sem_kept = refs[-7:]
-    act = pairs.shape[0]
+    act, parts, width = pairs.shape[1], pairs.shape[0], pairs.shape[3]
     _, chunk, rows = value.shape
     tiles = act // TILE
     start = pl.multiple_of(info[0] * chunk, chunk)
@@ -66,35 +66,39 @@
     def _(i):
         fetch(i).wait()
         part = value[tile(i)] * mask[...][None]
-        if kept is not None:
-            value[tile(i)] = part
-            keep(i).start()
+        value[tile(i)] = part
+        keep(i).start()
         for w in range(TILE):
-            turned[pl.ds(pl.multiple_of((i * TILE + w) * rows, rows), rows), :] = part[w].T
-
-    for v in range(act):
-        row = active[info[2 + v // nb] * nb + v % nb] - info[1]
-
-        @pl.when(jnp.logical_and(row >= 0, row < rows))
-        def _():
-            for i in range(tiles):
-                lines = turned[pl.ds(i * TILE * rows + row, TILE, stride=rows), :]
-                found[v, i * TILE : (i + 1) * TILE, :] = lines
+            at = pl.ds(pl.multiple_of((i * TILE + w) * rows, rows), rows)
+            for k in range(parts):
+                turned[k, at, :] = part[w, k * width : (k + 1) * width].T
+
+    @pl.loop(0, act // nb)
+    def _(j):
+        for t in range(nb):
+            row = active[info[2 + j] * nb + t] - info[1]
+
+            @pl.when(jnp.logical_and(row >= 0, row < rows))
+            def _():
+                for k in range(parts):
+                    for i in range(tiles):
+                        lines = turned[k, pl.ds(i * TILE * rows + row, TILE, stride=rows), :]
+                        found[k, j * nb + t, i * TILE : (i + 1) * TILE, :] = lines
 
     give = pltpu.make_async_copy(found, pairs, sem_out)
     give.start()
     give.wait()
-    if kept is not None:
-        for i in range(tiles):
-            keep(i).wait()
-
-
-def extract(three_index, screen_mask, active, info, chunk, nb, keep):
+    for i in range(tiles):
+        keep(i).wait()
+
+
+def extract(three_index, screen_mask, active, info, chunk, width, nb):
     act, slab, rows = three_index.shape
     tiles = act // TILE
-    out_shape = [jax.ShapeDtypeStruct((act, act, chunk), jnp.float32)]
-    if keep:
-        out_shape.append(jax.ShapeDtypeStruct((act, chunk, rows), jnp.float32))
+    out_shape = [
+        jax.ShapeDtypeStruct((chunk // width, act, act, width), jnp.float32),
+        jax.ShapeDtypeStruct((act, chunk, rows), jnp.float32),
+    ]
     smem, vmem, hbm, anywhere = places()
     return pl.pallas_call(
         functools.partial(extract_body, nb),
@@ -103,143 +107,106 @@
         out_specs=[anywhere] * len(out_shape),
         scratch_shapes=[
             pltpu.VMEM((act, chunk, rows), jnp.float32),
-            pltpu.VMEM((act * rows, chunk), jnp.float32),
-            pltpu.VMEM((act, act, chunk), jnp.float32),
+            pltpu.VMEM((chunk // width, act * rows, width), jnp.float32),
+            pltpu.VMEM((chunk // width, act, act, width), jnp.float32),
             pltpu.VMEM((chunk, rows), jnp.float32),
             pltpu.SemaphoreType.DMA((tiles,)),
             pltpu.SemaphoreType.DMA,
             pltpu.SemaphoreType.DMA((tiles,)),
         ],
-        compiler_params=pltpu.CompilerParams(vmem_limit_bytes=52 * MIB),
+        compiler_params=pltpu.CompilerParams(vmem_limit_bytes=50 * MIB),
         cost_estimate=pl.CostEstimate(
             flops=4 * act * act * chunk * rows,
             transcendentals=0,
-            bytes_accessed=4 * act * chunk * (act + rows * (2 if keep else 1)),
+            bytes_accessed=4 * act * chunk * (act + 2 * rows),
         ),
         name="extract",
     )(info, active, three_index, screen_mask)
 
 
-def q_body(nb, count, info, three, screen, sib, *refs):
-    blocks = refs[:count]
-    out, own_s, sib_s, held, lhs, acc, mask, sem_own, sem_sib, sem_block = refs[count:]
-    act, chunk, rows = own_s.shape
-    tiles = act // TILE
+def q_body(nb, count, info, kept, sib, *refs):
+    blocks, (out, own, lhs, acc, sems) = refs[: 2 * count], refs[2 * count :]
+    act, depth, rows = own.shape
+    chunk = depth // 2
     height = acc.shape[0]
-    start = pl.multiple_of(info[0] * chunk, chunk)
-
-    def tile(i):
-        return pl.ds(pl.multiple_of(i * TILE, TILE), TILE)
-
-    def own(i):
-        return pltpu.make_async_copy(three.at[tile(i), pl.ds(start, chunk), :], own_s.at[tile(i)], sem_own.at[i])
-
-    def other(i):
-        return pltpu.make_async_copy(sib.at[tile(i)], sib_s.at[tile(i)], sem_sib.at[i])
-
-    def bring(j):
-        return pltpu.make_async_copy(blocks[j], held.at[j], sem_block.at[j])
-
-    for j in range(count):
-        bring(j).start()
-    for i in range(tiles):
-        own(i).start()
-        other(i).start()
+
+    def bring(tile, i):
+        return pltpu.make_async_copy(kept.at[tile], own.at[tile], sems.at[i])
+
+    for i in range(act // TILE):
+        bring(pl.ds(i * TILE, TILE), i).start()
     lhs[...] = jnp.zeros_like(lhs)
-    mask[...] = expand_mask(screen, info[0], chunk, rows)
-    for j in range(count):
-        bring(j).wait()
     acc[...] = jnp.zeros_like(acc)
     nn = ((1,), (0,))
 
-    @pl.loop(0, tiles)
+    @pl.loop(0, act // TILE)
     def _(i):
-        for j in range(count):
-            for t in range(nb):
-                lhs[pl.ds(j * TILE + t, TILE, stride=height), :] = held[j, t, tile(i), :]
-        own(i).wait()
-        other(i).wait()
-        total = acc[...]
-        for m in range(0, TILE, 2):
-            pieces = [lhs[n * height : (n + 1) * height, :] for n in (m, m + 1)]
-            left, left_low = split(jnp.concatenate(pieces, axis=1))
-            right = [jnp.concatenate([own_s[i * TILE + n] * mask[...], sib_s[i * TILE + n]], axis=1) for n in (m, m + 1)]
-            top, low = split(jnp.concatenate(right, axis=0))
-            both = mxu(jnp.concatenate([left, left_low], axis=0), top, nn)
-            total = total + (both[:height] + both[height:] + mxu(left, low, nn))
-        acc[...] = total
+        tile = pl.ds(pl.multiple_of(i * TILE, TILE), TILE)
+        for k in range(2):
+            for j in range(count):
+                for t in range(nb):
+                    lhs[k, pl.ds(j * TILE + t, TILE, stride=height), :] = blocks[k * count + j][t, tile, :]
+        pieces = [lhs[k, n * height : (n + 1) * height, :] for n in range(TILE) for k in range(2)]
+        left, left_low = split(jnp.concatenate(pieces, axis=1))
+        bring(tile, i).wait()
+        right = [x[tile].reshape(TILE * depth, rows) for x in (own, sib)]
+        top, low = split(jnp.concatenate(right, axis=1))
+        both = mxu(jnp.concatenate([left, left_low], axis=0), top, nn)
+        acc[...] += both[:height] + both[height:] + mxu(left, low, nn)
 
     for j in range(count):
         where = pl.multiple_of(info[2 + j] * TILE, TILE)
         out[pl.ds(where, TILE), :] = acc[j * TILE : (j + 1) * TILE, :]
 
 
-def q_partial(three_index, screen_mask, sib, blocks, info, chunk):
-    act, slab, rows = three_index.shape
-    count = len(blocks)
+def q_partial(own, sib, blocks, info):
+    act, depth, rows = own.shape
+    count = len(blocks[0])
     nb = act // count
-    tiles = act // TILE
     smem, vmem, hbm, anywhere = places()
     return pl.pallas_call(
         functools.partial(q_body, nb, count),
         out_shape=jax.ShapeDtypeStruct((count * TILE, 2 * rows), jnp.float32),
-        in_specs=[smem, hbm, vmem, anywhere] + [anywhere] * count,
+        in_specs=[smem, hbm, vmem] + [vmem] * (2 * count),
         out_specs=vmem,
         scratch_shapes=[
-            pltpu.VMEM((act, chunk, rows), jnp.float32),
-            pltpu.VMEM((act, chunk, rows), jnp.float32),
-            pltpu.VMEM((count, nb, act, chunk), jnp.float32),
-            pltpu.VMEM((TILE * count * TILE, chunk), jnp.float32),
+            pltpu.VMEM((act, depth, rows), jnp.float32),
+            pltpu.VMEM((2, TILE * count * TILE, depth // 2), jnp.float32),
             pltpu.VMEM((count * TILE, 2 * rows), jnp.float32),
-            pltpu.VMEM((chunk, rows), jnp.float32),
-            pltpu.SemaphoreType.DMA((tiles,)),
-            pltpu.SemaphoreType.DMA((tiles,)),
-            pltpu.SemaphoreType.DMA((count,)),
+            pltpu.SemaphoreType.DMA((act // TILE,)),
         ],
-        compiler_params=pltpu.CompilerParams(vmem_limit_bytes=52 * MIB),
+        compiler_params=pltpu.CompilerParams(vmem_limit_bytes=49 * MIB),
         cost_estimate=pl.CostEstimate(
-            flops=12 * act * act * chunk * rows,
+            flops=12 * act * act * depth * rows,
             transcendentals=0,
-            bytes_accessed=4 * act * chunk * (act + 2 * rows),
+            bytes_accessed=4 * act * depth * (act + 2 * rows),
         ),
         name="qpartial",
-    )(info, three_index, screen_mask, sib, *[b.reshape(nb, act, chunk) for b in blocks])
+    )(info, own, sib, *[b.reshape(nb, act, depth // 2) for half in blocks for b in half])
 
 
 def half_body(chips, info, own, twin, *refs):
     count = 2 * (chips - 1)
     blocks, outs = refs[:count], refs[count : count + 2]
-    density, held, acc, sem_own, sem_twin, sem_block = refs[count + 2 :]
+    held, acc = refs[count + 2 :]
     size, chunk = blocks[0].shape
     rows, depth = own.shape
-    core = info[2 + chips]
-
-    def bring(n):
+
+    def place(hops):
+        return pl.ds(pl.multiple_of(info[2 + hops] * size, TILE), size)
+
+    for n in range(count):
         j, k = n // 2, n % 2
-        hops = j if j < chips // 2 else j + 1
-        where = pl.ds(pl.multiple_of(info[2 + hops] * size, TILE), size)
-        return pltpu.make_async_copy(blocks[n], held.at[where, pl.ds(k * chunk, chunk)], sem_block.at[n])
-
-    mine = pltpu.make_async_copy(own, density.at[core], sem_own)
-    other = pltpu.make_async_copy(twin, density.at[1 - core], sem_twin)
-    mine.start()
-    other.start()
-    for n in range(count):
-        bring(n).start()
-    missing = pl.ds(pl.multiple_of(info[2 + chips // 2] * size, TILE), size)
-    held[missing, :] = jnp.zeros((size, 2 * chunk), jnp.float32)
+        held[place(j if j < chips // 2 else j + 1), k * chunk : (k + 1) * chunk] = blocks[n][...]
+    held[place(chips // 2), :] = jnp.zeros((size, 2 * chunk), jnp.float32)
     acc[...] = jnp.zeros_like(acc)
-    mine.wait()
-    other.wait()
-    for n in range(count):
-        bring(n).wait()
     nn = ((1,), (0,))
-    step = 2 * LANES
+    step = 6 * LANES
 
     def add(start, length):
         top, low = split(held[pl.ds(start, length), :])
-        for h in range(2):
-            left, left_low = split(density[h, :, pl.ds(start, length)])
+        for h, density in enumerate((own, twin)):
+            left, left_low = split(density[:, pl.ds(start, length)])
             acc[h] += mxu(left, top, nn) + mxu(left_low, top, nn) + mxu(left, low, nn)
 
     @pl.loop(0, depth // step)
@@ -248,9 +215,15 @@
 
     if depth % step:
         add(depth - depth % step, depth % step)
-    for k in range(2):
-        for h in range(2):
-            outs[k][h * rows : (h + 1) * rows, :] = acc[h, :, k * chunk : (k + 1) * chunk]
+    core = info[2 + chips]
+    for first in range(2):
+
+        @pl.when(core == first)
+        def _():
+            for k in range(2):
+                for h in range(2):
+                    at = (h ^ first) * rows
+                    outs[k][at : at + rows, :] = acc[h, :, k * chunk : (k + 1) * chunk]
 
 
 def half_partial(own, twin, blocks, info, chips):
@@ -260,17 +233,13 @@
     return pl.pallas_call(
         functools.partial(half_body, chips),
         out_shape=[jax.ShapeDtypeStruct((2 * rows, chunk), jnp.float32)] * 2,
-        in_specs=[smem, anywhere, anywhere] + [anywhere] * len(blocks),
+        in_specs=[smem, vmem, vmem] + [vmem] * len(blocks),
         out_specs=[vmem, vmem],
         scratch_shapes=[
-            pltpu.VMEM((2, rows, depth), jnp.float32),
             pltpu.VMEM((depth, 2 * chunk), jnp.float32),
             pltpu.VMEM((2, rows, 2 * chunk), jnp.float32),
-            pltpu.SemaphoreType.DMA,
-            pltpu.SemaphoreType.DMA,
-            pltpu.SemaphoreType.DMA((len(blocks),)),
         ],
-        compiler_params=pltpu.CompilerParams(vmem_limit_bytes=16 * MIB),
+        compiler_params=pltpu.CompilerParams(vmem_limit_bytes=14 * MIB),
         cost_estimate=pl.CostEstimate(
             flops=24 * rows * depth * chunk,
             transcendentals=0,
@@ -286,7 +255,8 @@
     chips = orb // 2
     nb = act // chips
     blk = nb * act
-    chunk = slab // 4
+    depth = slab // 2
+    chunk = depth // 2
     me = lax.axis_index("orb")
     chip, core = lax.shift_right_logical(me, 1), lax.bitwise_and(me, 1)
     half_chip = lax.shift_right_logical(chip, 1)
@@ -300,9 +270,9 @@
         place = lax.rem(position + sgn * hops + chips, chips)
         return jnp.where(place < chips // 2, 2 * place, 2 * chips - 1 - 2 * place)
 
-    def info_of(sgn, half, k):
+    def info_of(sgn, half):
         by_hops = chip_at(sgn, jnp.arange(chips, dtype=jnp.int32))
-        return jnp.concatenate([jnp.stack([2 * half + k, first_row]), by_hops, core.reshape(1)]).astype(jnp.int32)
+        return jnp.concatenate([jnp.stack([half, first_row]), by_hops, core.reshape(1)]).astype(jnp.int32)
 
     near = [(order[k], order[(k + 1) % chips]) for k in range(chips)]
     ahead = [(2 * a, 2 * b) for a, b in near] + [(2 * b + 1, 2 * a + 1) for a, b in near]
@@ -313,31 +283,30 @@
         return lax.ppermute(x, "orb", pairs)
 
     local_rows = jnp.arange(rows, dtype=jnp.int32)
-    mine = [info_of(sign, core, k) for k in range(2)]
-    theirs = [info_of(-sign, 1 - core, k) for k in range(2)]
+    mine, theirs = info_of(sign, core), info_of(-sign, 1 - core)
 
     shells = screen_mask.T
-    contributions, sib_three = [], []
+    far = chips // 2
+    def pick(info):
+        found, kept = extract(three_index, shells, active_orbitals, info, depth, chunk, nb)
+        return found.reshape(2, act * act, chunk), kept
+
+    other = hop(pair_density, twin)
+    given, sib_three = pick(theirs)
+    got = hop(given, twin)
+    given, mine = lax.optimization_barrier((given, mine))
+    found, own_three = pick(mine)
+    contributions = []
     for k in range(2):
-        given, kept = extract(three_index, shells, active_orbitals, theirs[k], chunk, nb, True)
-        (own,) = extract(three_index, shells, active_orbitals, mine[k], chunk, nb, False)
-        got = hop(given.reshape(act * act, chunk), twin)
-        own = own.reshape(act * act, chunk)
-        sums = [own[j * blk : (j + 1) * blk] + got[j * blk : (j + 1) * blk] for j in range(chips)]
-        sib_three.append(kept)
-        if k == 0:
-            theirs[1], mine[1], sums[chips // 2] = lax.optimization_barrier((theirs[1], mine[1], sums[chips // 2]))
-        else:
-            pair_density, inactive_fock, active_fock, sib_three, sums[chips // 2] = lax.optimization_barrier(
-                (pair_density, inactive_fock, active_fock, sib_three, sums[chips // 2])
-            )
-        contributions.append(sums)
-
-    other = hop(pair_density, twin)
-    sib_three = [hop(x, twin) for x in sib_three]
-    far = chips // 2
+        contributions.append(
+            [found[k, j * blk : (j + 1) * blk] + got[k, j * blk : (j + 1) * blk] for j in range(chips)]
+        )
+    inactive_fock, active_fock, contributions, other, sib_three = lax.optimization_barrier(
+        (inactive_fock, active_fock, contributions, other, sib_three)
+    )
+    sib_three = hop(sib_three, twin)
     first = [(hop(c[far], ahead), hop(c[far + 1], behind)) for c in contributions]
-    first, other, sib_three = lax.optimization_barrier((first, other, sib_three))
+    first, sib_three = lax.optimization_barrier((first, sib_three))
     totals = []
     for c, (a, b) in zip(contributions, first):
         for s in range(1, far):
@@ -367,12 +336,10 @@
 
     gathered = [gather(x) for x in totals]
     near_blocks = [gathered[k][j] for j in range(chips) if j != far for k in range(2)]
-    halves = half_partial(pair_density, other, near_blocks, mine[0], chips)
+    halves = half_partial(pair_density, other, near_blocks, mine, chips)
     halves = [h + jnp.dot(density_far, gathered[k][far], precision=HIGH) for k, h in enumerate(halves)]
     halves = lax.optimization_barrier(halves)
-    q = 0.0
-    for k, x in enumerate(halves):
-        q = q + q_partial(three_index, shells, sib_three[k], gather(x), mine[k], chunk)
+    q = q_partial(own_three, sib_three, [gather(x) for x in halves], mine)
     q = q.reshape(chips, TILE, 2 * rows)[:, :nb].reshape(act, 2 * rows)
 
     share = rows // aux

time: 177 us -> 163 us (0.921)
  Pallas kernels: 38.7 us -> 28.5 us
  waiting for transfers between devices: 64.3 us -> 57.5 us
  starting transfers between devices: 57.9 us -> 63.9 us
  local copies, waits for them, and re-layouts: 9.94 us -> 4.04 us
  other arithmetic: 2.56 us -> 5.96 us
    unnamed x28 -> x20, local copies, waits for them, and re-layouts: 9.27 us -> 3.58 us
    pallas_call x2 -> x1, Pallas kernels: 14.8 us -> 9.79 us  [q_partial(): pl.pallas_call(functools.partial(q_body, nb, count), out_shape=jax.ShapeD...]
    ppermute x51 -> x49, starting transfers between devices: 49.3 us -> 54.3 us  [hop(): return lax.ppermute(x, 'orb', pairs)]
    ppermute x51 -> x49, waiting for transfers between devices: 56.7 us -> 52 us  [hop(): return lax.ppermute(x, 'orb', pairs)]
    add x2 -> x6, other arithmetic: 0.11 us -> 3.84 us  [the longest x2 3.74 us: fast(): found[k, j * blk:(j + 1) * blk] + got[k, j * blk:(j + 1) * blk]]
    pallas_call x1, Pallas kernels: 7.29 us -> 4.46 us  [half_partial(): pl.pallas_call(functools.partial(half_body, chips), out_shape=[jax.ShapeD...]
    pallas_call x4 -> x2, Pallas kernels: 16.6 us -> 14.3 us  [extract(): pl.pallas_call(functools.partial(extract_body, nb), out_shape=out_shape,...]
    ppermute x7, waiting for transfers between devices: 7.65 us -> 5.54 us  [across(): return lax.ppermute(x, ('orb', 'aux'), table)]
  transfers between devices with their start and end apart: 58 -> 56, of which waited for: 32 -> 37; matrix products, arithmetic and copies ran while one was open for 2% -> 4% of each run, Pallas kernels for 17% -> 13%
where the time goes in v3:
time: 163 us
  starting transfers between devices  63.9 us (39%)
  waiting for transfers between devices  57.5 us (35%)
  Pallas kernels  28.5 us (17%)
  other arithmetic  5.96 us (4%)
  local copies, waits for them, and re-layouts  4.04 us (2%)
  matrix products  2.85 us (2%)
    ppermute x49, starting transfers between devices, hop(): return lax.ppermute(x, 'orb', pairs)  54.3 us
    ppermute x49, waiting for transfers between devices, hop(): return lax.ppermute(x, 'orb', pairs)  52 us
    pallas_call x2, Pallas kernels, extract(): pl.pallas_call(functools.partial(extract_body, nb), out_shape=out_shape,...  14.3 us
    pallas_call x1, Pallas kernels, q_partial(): pl.pallas_call(functools.partial(q_body, nb, count), out_shape=jax.ShapeD...  9.79 us
    ppermute x7, starting transfers between devices, across(): return lax.ppermute(x, ('orb', 'aux'), table)  9.53 us
    ppermute x7, waiting for transfers between devices, across(): return lax.ppermute(x, ('orb', 'aux'), table)  5.54 us
    pallas_call x1, Pallas kernels, half_partial(): pl.pallas_call(functools.partial(half_body, chips), out_shape=[jax.ShapeD...  4.46 us
    add x2, other arithmetic, fast(): found[k, j * blk:(j + 1) * blk] + got[k, j * blk:(j + 1) * blk]  3.74 us
  transfers between devices with their start and end apart: 56, of which 37 were waited for; matrix products, arithmetic and copies ran while one was open for 4% of the time, Pallas kernels for 13%

profile of v3, /device:TPU:0, one launch (start us, length us, event | category | flops | bytes accessed | tf_op | source)
XLA Modules:
  0.0 163.2 jit_solution(7259293696735823296)
XLA Ops:
  1.4 7.3 %extract.2 = (f32[2,56,56,128]{3,2,1,0:T(8,128)S(1)}, f32[56,256,128]{2,1,0:T(8,128)}) custom-call(s32[11]{0:T(128)S(1)} %add_add_fusion.4.info, s32[56]{0:T(128)S(1)} %copy-done.5, f32[56,512,128]{2,1,0:T(8,128)} %three.3, s32[8,32]{1,0:T(8,128)S(1)} %bitcast.89), custom_call_target="tpu_custom_call" | custom-call | flops 411041792 | bytes 17891328 | tf_op jit(solution)/shard_map/extract/pallas_call | solution.py:103
  9.5 7.0 %extract.3 = (f32[2,56,56,128]{3,2,1,0:T(8,128)S(1)}, f32[56,256,128]{2,1,0:T(8,128)}) custom-call(s32[11]{0:T(128)S(1)} %add_add_fusion.5.info, s32[56]{0:T(128)S(1)} %copy-done.6, f32[56,512,128]{2,1,0:T(8,128)} %three.3, s32[8,32]{1,0:T(8,128)S(1)} %bitcast.90), custom_call_target="tpu_custom_call" | custom-call | flops 411041792 | bytes 17891328 | tf_op jit(solution)/shard_map/extract/pallas_call | solution.py:103
  16.6 2.0 %collective-permute-done = f32[2,3136,128]{2,1,0:T(8,128)} collective-permute-done((f32[2,3136,128]{2,1,0:T(8,128)S(1)}, f32[2,3136,128]{2,1,0:T(8,128)}, u32[]{:S(2)}, u32[]{:S(2)}) %collective-permute-start) | collective-permute-done | bytes 3211296 | tf_op jit(solution)/shard_map/ppermute | solution.py:283
  20.2 2.0 %fusion.9 = (f32[392,128]{1,0:T(8,128)S(1)}, f32[392,128]{1,0:T(8,128)S(1)}, f32[392,128]{1,0:T(8,128)S(1)}, f32[392,128]{1,0:T(8,128)S(1)}, f32[392,128]{1,0:T(...) fusion(f32[2,3136,128]{2,1,0:T(8,128)} %collective-permute-done, ...), kind=kLoop, calls=%fused_computation.17 | loop fusion | flops 451584 | bytes 5419008 | tf_op jit(solution)/shard_map/add | solution.py:302
  23.2 2.8 %collective-permute-start.2 = (f32[392,128]{1,0:T(8,128)S(1)}, f32[392,128]{1,0:T(8,128)S(1)}, u32[]{:S(2)}, u32[]{:S(2)}) collective-permute-start(f32[392,128]{1,0:T(8,128)S(1)} %get-tuple-element.48), channel_id=1, source_target_pairs={{0,8},{8,16},{16,24},{24,28},{28,20},{20,12},{12,4},{4,0},{10,2},{... | collective-permute-start | bytes 602120 | tf_op jit(solution)/shard_map/ppermute | solution.py:283
  26.0 2.0 %collective-permute-start.4 = (f32[392,128]{1,0:T(8,128)S(1)}, f32[392,128]{1,0:T(8,128)S(1)}, u32[]{:S(2)}, u32[]{:S(2)}) collective-permute-start(f32[392,128]{1,0:T(8,128)S(1)} %get-tuple-element.50), channel_id=1, source_target_pairs={{0,8},{8,16},{16,24},{24,28},{28,20},{20,12},{12,4},{4,0},{10,2},{... | collective-permute-start | bytes 602120 | tf_op jit(solution)/shard_map/ppermute | solution.py:283
  28.0 3.3 %collective-permute-done.2 = f32[392,128]{1,0:T(8,128)S(1)} collective-permute-done((f32[392,128]{1,0:T(8,128)S(1)}, f32[392,128]{1,0:T(8,128)S(1)}, u32[]{:S(2)}, u32[]{:S(2)}) %collective-permute-start.2) | collective-permute-done | bytes 200736 | tf_op jit(solution)/shard_map/ppermute | solution.py:283
  31.3 2.3 %collective-permute-done.3 = f32[392,128]{1,0:T(8,128)S(1)} collective-permute-done((f32[392,128]{1,0:T(8,128)S(1)}, f32[392,128]{1,0:T(8,128)S(1)}, u32[]{:S(2)}, u32[]{:S(2)}) %collective-permute-start.3) | collective-permute-done | bytes 200736 | tf_op jit(solution)/shard_map/ppermute | solution.py:283
  35.8 1.9 %collective-permute-start.7 = (f32[392,128]{1,0:T(8,128)S(1)}, f32[392,128]{1,0:T(8,128)S(1)}, u32[]{:S(2)}, u32[]{:S(2)}) collective-permute-start(f32[392,128]{1,0:T(8,128)S(1)} %add.296), channel_id=1, source_target_pairs={{0,8},{8,16},{16,24},{24,28},{28,20},{20,12},{12,4},{4,0},{10,2},{... | collective-permute-start | bytes 602120 | tf_op jit(solution)/shard_map/ppermute | solution.py:283
  39.9 2.5 %collective-permute-done.7 = f32[392,128]{1,0:T(8,128)S(1)} collective-permute-done((f32[392,128]{1,0:T(8,128)S(1)}, f32[392,128]{1,0:T(8,128)S(1)}, u32[]{:S(2)}, u32[]{:S(2)}) %collective-permute-start.7) | collective-permute-done | bytes 200736 | tf_op jit(solution)/shard_map/ppermute | solution.py:283
  42.5 2.5 %collective-permute-start.8 = (f32[392,128]{1,0:T(8,128)S(1)}, f32[392,128]{1,0:T(8,128)S(1)}, u32[]{:S(2)}, u32[]{:S(2)}) collective-permute-start(f32[392,128]{1,0:T(8,128)S(1)} %add.297), channel_id=1, source_target_pairs={{0,8},{8,16},{16,24},{24,28},{28,20},{20,12},{12,4},{4,0},{10,2},{... | collective-permute-start | bytes 602120 | tf_op jit(solution)/shard_map/ppermute | solution.py:283
  46.8 2.5 %collective-permute-start.13 = (f32[392,128]{1,0:T(8,128)S(1)}, f32[392,128]{1,0:T(8,128)S(1)}, u32[]{:S(2)}, u32[]{:S(2)}) collective-permute-start(f32[392,128]{1,0:T(8,128)S(1)} %add.304), channel_id=1, source_target_pairs={{0,8},{8,16},{16,24},{24,28},{28,20},{20,12},{12,4},{4,0},{10,2},{... | collective-permute-start | bytes 602120 | tf_op jit(solution)/shard_map/ppermute | solution.py:283
  51.1 2.5 %collective-permute-start.9 = (f32[392,128]{1,0:T(8,128)S(1)}, f32[392,128]{1,0:T(8,128)S(1)}, u32[]{:S(2)}, u32[]{:S(2)}) collective-permute-start(f32[392,128]{1,0:T(8,128)S(1)} %add.298), channel_id=1, source_target_pairs={{0,8},{8,16},{16,24},{24,28},{28,20},{20,12},{12,4},{4,0},{10,2},{... | collective-permute-start | bytes 602120 | tf_op jit(solution)/shard_map/ppermute | solution.py:283
  55.4 2.5 %collective-permute-start.14 = (f32[392,128]{1,0:T(8,128)S(1)}, f32[392,128]{1,0:T(8,128)S(1)}, u32[]{:S(2)}, u32[]{:S(2)}) collective-permute-start(f32[392,128]{1,0:T(8,128)S(1)} %add.305), channel_id=1, source_target_pairs={{0,8},{8,16},{16,24},{24,28},{28,20},{20,12},{12,4},{4,0},{10,2},{... | collective-permute-start | bytes 602120 | tf_op jit(solution)/shard_map/ppermute | solution.py:283
  61.2 2.5 %collective-permute-start.23 = (f32[392,128]{1,0:T(8,128)S(1)}, f32[392,128]{1,0:T(8,128)S(1)}, u32[]{:S(2)}, u32[]{:S(2)}) collective-permute-start(f32[392,128]{1,0:T(8,128)S(1)} %add_add_fusion.1.refs_0_), channel_id=1, source_target_pairs={{0,8},{8,16},{16,24},{24,28},{28,20},{20,12},{12,4},{4,0},{10,2},{... | collective-permute-start | bytes 602120 | tf_op jit(solution)/shard_map/ppermute | solution.py:283
  65.8 3.2 %collective-permute-done.23.refs_12_ = f32[392,128]{1,0:T(8,128)S(1)} collective-permute-done((f32[392,128]{1,0:T(8,128)S(1)}, f32[392,128]{1,0:T(8,128)S(1)}, u32[]{:S(2)}, u32[]{:S(2)}) %collective-permute-start.23) | collective-permute-done | bytes 200736 | tf_op jit(solution)/shard_map/ppermute | solution.py:283
  75.2 1.9 %collective-permute-start.27 = (f32[392,128]{1,0:T(8,128)}, f32[392,128]{1,0:T(8,128)S(1)}, u32[]{:S(2)}, u32[]{:S(2)}) collective-permute-start(f32[392,128]{1,0:T(8,128)} %collective-permute-done.26.refs_13_), channel_id=1, source_target_pairs={{0,8},{8,16},{16,24},{24,28},{28,20},{20,12},{12,4},{4,0},{10,2},{... | collective-permute-start | bytes 602120 | tf_op jit(solution)/shard_map/ppermute | solution.py:283
  79.7 3.5 %collective-permute-done.20.refs_5_ = f32[392,128]{1,0:T(8,128)S(1)} collective-permute-done((f32[392,128]{1,0:T(8,128)}, f32[392,128]{1,0:T(8,128)S(1)}, u32[]{:S(2)}, u32[]{:S(2)}) %collective-permute-start.20) | collective-permute-done | bytes 200736 | tf_op jit(solution)/shard_map/ppermute | solution.py:283
  83.4 2.3 %collective-permute-start.28 = (f32[392,128]{1,0:T(8,128)S(1)}, f32[392,128]{1,0:T(8,128)S(1)}, u32[]{:S(2)}, u32[]{:S(2)}) collective-permute-start(f32[392,128]{1,0:T(8,128)S(1)} %collective-permute-done.27.refs_11_), channel_id=1, source_target_pairs={{0,8},{8,16},{16,24},{24,28},{28,20},{20,12},{12,4},{4,0},{10,2},{... | collective-permute-start | bytes 602120 | tf_op jit(solution)/shard_map/ppermute | solution.py:283
  85.7 2.0 %collective-permute-done.25.refs_8_ = f32[392,128]{1,0:T(8,128)S(1)} collective-permute-done((f32[392,128]{1,0:T(8,128)S(1)}, f32[392,128]{1,0:T(8,128)S(1)}, u32[]{:S(2)}, u32[]{:S(2)}) %collective-permute-start.25) | collective-permute-done | bytes 200736 | tf_op jit(solution)/shard_map/ppermute | solution.py:283
  93.6 4.5 %half.1 = (f32[392,128]{1,0:T(8,128)S(1)}, f32[392,128]{1,0:T(8,128)S(1)}) custom-call(s32[11]{0:T(128)S(1)} %add_add_fusion.5.info, f32[196,3136]{1,0:T(8,128)S(1)} %copy-done.1, f32[196,3136]{1,0:T(8,128)S(1)} %copy-done.3, f32[392,128]{1,0:T(8,128)S(1)} %add_add_fusion.1.refs_0_, f32[392,128]{1,0:T(8,128)S(1)} %add_add_fusion.refs_1_, ...), custom_call_target="tpu_custom_call" | custom-call | flops 1888223232 | bytes 8128512 | tf_op jit(solution)/shard_map/half/pallas_call | solution.py:233
  99.0 2.4 %collective-permute-start.34 = (f32[392,128]{1,0:T(8,128)S(1)}, f32[392,128]{1,0:T(8,128)S(1)}, u32[]{:S(2)}, u32[]{:S(2)}) collective-permute-start(f32[392,128]{1,0:T(8,128)S(1)} %convolution_add_fusion.1), channel_id=1, source_target_pairs={{0,8},{8,16},{16,24},{24,28},{28,20},{20,12},{12,4},{4,0},{10,2},{... | collective-permute-start | bytes 602120 | tf_op jit(solution)/shard_map/ppermute | solution.py:283
  103.8 3.1 %collective-permute-done.34 = f32[392,128]{1,0:T(8,128)S(1)} collective-permute-done((f32[392,128]{1,0:T(8,128)S(1)}, f32[392,128]{1,0:T(8,128)S(1)}, u32[]{:S(2)}, u32[]{:S(2)}) %collective-permute-start.34) | collective-permute-done | bytes 200736 | tf_op jit(solution)/shard_map/ppermute | solution.py:283
  107.0 2.1 %collective-permute-start.35 = (f32[392,128]{1,0:T(8,128)S(1)}, f32[392,128]{1,0:T(8,128)S(1)}, u32[]{:S(2)}, u32[]{:S(2)}) collective-permute-start(f32[392,128]{1,0:T(8,128)S(1)} %collective-permute-done.34), channel_id=1, source_target_pairs={{0,8},{8,16},{16,24},{24,28},{28,20},{20,12},{12,4},{4,0},{10,2},{... | collective-permute-start | bytes 602120 | tf_op jit(solution)/shard_map/ppermute | solution.py:283
  112.4 1.9 %collective-permute-start.39 = (f32[392,128]{1,0:T(8,128)S(1)}, f32[392,128]{1,0:T(8,128)S(1)}, u32[]{:S(2)}, u32[]{:S(2)}) collective-permute-start(f32[392,128]{1,0:T(8,128)S(1)} %collective-permute-done.38), channel_id=1, source_target_pairs={{8,0},{16,8},{24,16},{28,24},{20,28},{12,20},{4,12},{0,4},{2,10},{... | collective-permute-start | bytes 602120 | tf_op jit(solution)/shard_map/ppermute | solution.py:283
  114.8 2.4 %collective-permute-done.42 = f32[392,128]{1,0:T(8,128)S(1)} collective-permute-done((f32[392,128]{1,0:T(8,128)S(1)}, f32[392,128]{1,0:T(8,128)S(1)}, u32[]{:S(2)}, u32[]{:S(2)}) %collective-permute-start.42) | collective-permute-done | bytes 200736 | tf_op jit(solution)/shard_map/ppermute | solution.py:283
  117.2 1.9 %collective-permute-start.43 = (f32[392,128]{1,0:T(8,128)S(1)}, f32[392,128]{1,0:T(8,128)S(1)}, u32[]{:S(2)}, u32[]{:S(2)}) collective-permute-start(f32[392,128]{1,0:T(8,128)S(1)} %collective-permute-done.42), channel_id=1, source_target_pairs={{0,8},{8,16},{16,24},{24,28},{28,20},{20,12},{12,4},{4,0},{10,2},{... | collective-permute-start | bytes 602120 | tf_op jit(solution)/shard_map/ppermute | solution.py:283
  119.8 3.7 %collective-permute-done.39 = f32[392,128]{1,0:T(8,128)S(1)} collective-permute-done((f32[392,128]{1,0:T(8,128)S(1)}, f32[392,128]{1,0:T(8,128)S(1)}, u32[]{:S(2)}, u32[]{:S(2)}) %collective-permute-start.39) | collective-permute-done | bytes 200736 | tf_op jit(solution)/shard_map/ppermute | solution.py:283
  127.7 3.7 %collective-permute-done.40 = f32[392,128]{1,0:T(8,128)S(1)} collective-permute-done((f32[392,128]{1,0:T(8,128)S(1)}, f32[392,128]{1,0:T(8,128)S(1)}, u32[]{:S(2)}, u32[]{:S(2)}) %collective-permute-start.40) | collective-permute-done | bytes 200736 | tf_op jit(solution)/shard_map/ppermute | solution.py:283
  133.0 9.8 %qpartial.1 = f32[64,256]{1,0:T(8,128)S(1)} custom-call(s32[11]{0:T(128)S(1)} %add_add_fusion.5.info, f32[56,256,128]{2,1,0:T(8,128)} %get-tuple-element.47.kept, f32[56,256,128]{2,1,0:T(8,128)} %collective-permute-done.6.sib, f32[7,56,128]{2,1,0:T(8,128)S(1)} %bitcast.72, f32[7,56,128]{2,1,0:T(8,128)S(1)} %bitcast.77, f32[7,56,128]{2,1,0:T(8,128)S(1)} %bitcast.81, ...), custom_call_target="tpu_custom_call" | custom-call | flops 1233125376 | bytes 17891328 | tf_op jit(solution)/shard_map/qpartial/pallas_call | solution.py:167
  145.9 2.2 %collective-permute-start.51 = (f32[112,128]{1,0:T(8,128)S(1)}, f32[112,128]{1,0:T(8,128)S(1)}, u32[]{:S(2)}, u32[]{:S(2)}) collective-permute-start(f32[112,128]{1,0:T(8,128)S(1)} %maximum_add_fusion), channel_id=1, source_target_pairs={{0,5},{1,4},{2,7},{3,6},{4,1},{5,0},{6,3},{7,2},{8,13},{9,12},{10,... | collective-permute-start | bytes 172040 | tf_op jit(solution)/shard_map/ppermute | solution.py:350
  153.8 1.9 %collective-permute-start.53 = (f32[112,128]{1,0:T(8,128)S(1)}, f32[112,128]{1,0:T(8,128)S(1)}, u32[]{:S(2)}, u32[]{:S(2)}) collective-permute-start(f32[112,128]{1,0:T(8,128)S(1)} %add_add_fusion.3), channel_id=1, source_target_pairs={{0,16},{1,17},{2,18},{3,19},{4,20},{5,21},{6,22},{7,23},{8,24},{9,... | collective-permute-start | bytes 172040 | tf_op jit(solution)/shard_map/ppermute | solution.py:350
  (154 shorter events, 64.3 us)
Async XLA Ops:
  8.7 9.8 %collective-permute-start = (f32[2,3136,128]{2,1,0:T(8,128)S(1)}, f32[2,3136,128]{2,1,0:T(8,128)}, u32[]{:S(2)}, u32[]{:S(2)}) collective-permute-start(f32[2,3136,128]{2,1,0:T(8,128)S(1)} %bitcast.91), channel_id=1, source_target_pairs={{0,2},{2,0},{4,6},{6,4},{8,10},{10,8},{12,14},{14,12},{16,18},{18,... | collective-permute-start | bytes 9633800 | tf_op jit(solution)/shard_map/ppermute | solution.py:283
  9.3 12.9 %collective-permute-start.1 = (f32[196,3136]{1,0:T(8,128)S(1)}, f32[196,3136]{1,0:T(8,128)S(1)}, u32[]{:S(2)}, u32[]{:S(2)}) collective-permute-start(f32[196,3136]{1,0:T(8,128)S(1)} %copy-done.1), channel_id=1, source_target_pairs={{0,2},{2,0},{4,6},{6,4},{8,10},{10,8},{12,14},{14,12},{16,18},{18,... | collective-permute-start | bytes 7375880 | tf_op jit(solution)/shard_map/ppermute | solution.py:283
  22.8 13.0 %collective-permute-start.6 = (f32[56,256,128]{2,1,0:T(8,128)S(1)}, f32[56,256,128]{2,1,0:T(8,128)}, u32[]{:S(2)}, u32[]{:S(2)}) collective-permute-start(f32[56,256,128]{2,1,0:T(8,128)S(1)} %copy-done.9), channel_id=1, source_target_pairs={{0,2},{2,0},{4,6},{6,4},{8,10},{10,8},{12,14},{14,12},{16,18},{18,... | collective-permute-start | bytes 22020104 | tf_op jit(solution)/shard_map/ppermute | solution.py:283
  23.2 8.2 %collective-permute-start.2 = (f32[392,128]{1,0:T(8,128)S(1)}, f32[392,128]{1,0:T(8,128)S(1)}, u32[]{:S(2)}, u32[]{:S(2)}) collective-permute-start(f32[392,128]{1,0:T(8,128)S(1)} %get-tuple-element.48), channel_id=1, source_target_pairs={{0,8},{8,16},{16,24},{24,28},{28,20},{20,12},{12,4},{4,0},{10,2},{... | collective-permute-start | bytes 602120 | tf_op jit(solution)/shard_map/ppermute | solution.py:283
  26.0 9.1 %collective-permute-start.4 = (f32[392,128]{1,0:T(8,128)S(1)}, f32[392,128]{1,0:T(8,128)S(1)}, u32[]{:S(2)}, u32[]{:S(2)}) collective-permute-start(f32[392,128]{1,0:T(8,128)S(1)} %get-tuple-element.50), channel_id=1, source_target_pairs={{0,8},{8,16},{16,24},{24,28},{28,20},{20,12},{12,4},{4,0},{10,2},{... | collective-permute-start | bytes 602120 | tf_op jit(solution)/shard_map/ppermute | solution.py:283
  37.7 9.0 %collective-permute-start.12 = (f32[392,128]{1,0:T(8,128)S(1)}, f32[392,128]{1,0:T(8,128)S(1)}, u32[]{:S(2)}, u32[]{:S(2)}) collective-permute-start(f32[392,128]{1,0:T(8,128)S(1)} %add.303), channel_id=1, source_target_pairs={{0,8},{8,16},{16,24},{24,28},{28,20},{20,12},{12,4},{4,0},{10,2},{... | collective-permute-start | bytes 602120 | tf_op jit(solution)/shard_map/ppermute | solution.py:283
  39.5 9.8 %collective-permute-start.10 = (f32[392,128]{1,0:T(8,128)S(1)}, f32[392,128]{1,0:T(8,128)S(1)}, u32[]{:S(2)}, u32[]{:S(2)}) collective-permute-start(f32[392,128]{1,0:T(8,128)S(1)} %add.300), channel_id=1, source_target_pairs={{8,0},{16,8},{24,16},{28,24},{20,28},{12,20},{4,12},{0,4},{2,10},{... | collective-permute-start | bytes 602120 | tf_op jit(solution)/shard_map/ppermute | solution.py:283
  42.5 8.6 %collective-permute-start.8 = (f32[392,128]{1,0:T(8,128)S(1)}, f32[392,128]{1,0:T(8,128)S(1)}, u32[]{:S(2)}, u32[]{:S(2)}) collective-permute-start(f32[392,128]{1,0:T(8,128)S(1)} %add.297), channel_id=1, source_target_pairs={{0,8},{8,16},{16,24},{24,28},{28,20},{20,12},{12,4},{4,0},{10,2},{... | collective-permute-start | bytes 602120 | tf_op jit(solution)/shard_map/ppermute | solution.py:283
  45.0 8.6 %collective-permute-start.15 = (f32[392,128]{1,0:T(8,128)S(1)}, f32[392,128]{1,0:T(8,128)S(1)}, u32[]{:S(2)}, u32[]{:S(2)}) collective-permute-start(f32[392,128]{1,0:T(8,128)S(1)} %add.307), channel_id=1, source_target_pairs={{8,0},{16,8},{24,16},{28,24},{20,28},{12,20},{4,12},{0,4},{2,10},{... | collective-permute-start | bytes 602120 | tf_op jit(solution)/shard_map/ppermute | solution.py:283
  46.8 8.6 %collective-permute-start.13 = (f32[392,128]{1,0:T(8,128)S(1)}, f32[392,128]{1,0:T(8,128)S(1)}, u32[]{:S(2)}, u32[]{:S(2)}) collective-permute-start(f32[392,128]{1,0:T(8,128)S(1)} %add.304), channel_id=1, source_target_pairs={{0,8},{8,16},{16,24},{24,28},{28,20},{20,12},{12,4},{4,0},{10,2},{... | collective-permute-start | bytes 602120 | tf_op jit(solution)/shard_map/ppermute | solution.py:283
  49.3 8.6 %collective-permute-start.11 = (f32[392,128]{1,0:T(8,128)S(1)}, f32[392,128]{1,0:T(8,128)S(1)}, u32[]{:S(2)}, u32[]{:S(2)}) collective-permute-start(f32[392,128]{1,0:T(8,128)S(1)} %add.301), channel_id=1, source_target_pairs={{8,0},{16,8},{24,16},{28,24},{20,28},{12,20},{4,12},{0,4},{2,10},{... | collective-permute-start | bytes 602120 | tf_op jit(solution)/shard_map/ppermute | solution.py:283
  63.7 9.7 %collective-permute-start.18 = (f32[392,128]{1,0:T(8,128)S(1)}, f32[392,128]{1,0:T(8,128)}, u32[]{:S(2)}, u32[]{:S(2)}) collective-permute-start(f32[392,128]{1,0:T(8,128)S(1)} %add_add_fusion.refs_1_), channel_id=1, source_target_pairs={{8,0},{16,8},{24,16},{28,24},{20,28},{12,20},{4,12},{0,4},{2,10},{... | collective-permute-start | bytes 602120 | tf_op jit(solution)/shard_map/ppermute | solution.py:283
  64.5 10.7 %collective-permute-start.26 = (f32[392,128]{1,0:T(8,128)S(1)}, f32[392,128]{1,0:T(8,128)}, u32[]{:S(2)}, u32[]{:S(2)}) collective-permute-start(f32[392,128]{1,0:T(8,128)S(1)} %add_add_fusion.refs_1_), channel_id=1, source_target_pairs={{0,8},{8,16},{16,24},{24,28},{28,20},{20,12},{12,4},{4,0},{10,2},{... | collective-permute-start | bytes 602120 | tf_op jit(solution)/shard_map/ppermute | solution.py:283
  69.0 8.6 %collective-permute-start.24 = (f32[392,128]{1,0:T(8,128)S(1)}, f32[392,128]{1,0:T(8,128)S(1)}, u32[]{:S(2)}, u32[]{:S(2)}) collective-permute-start(f32[392,128]{1,0:T(8,128)S(1)} %collective-permute-done.23.refs_12_), channel_id=1, source_target_pairs={{0,8},{8,16},{16,24},{24,28},{28,20},{20,12},{12,4},{4,0},{10,2},{... | collective-permute-start | bytes 602120 | tf_op jit(solution)/shard_map/ppermute | solution.py:283
  71.1 8.2 %collective-permute-start.19 = (f32[392,128]{1,0:T(8,128)S(1)}, f32[392,128]{1,0:T(8,128)S(1)}, u32[]{:S(2)}, u32[]{:S(2)}) collective-permute-start(f32[392,128]{1,0:T(8,128)S(1)} %collective-permute-done.17.refs_2_), channel_id=1, source_target_pairs={{8,0},{16,8},{24,16},{28,24},{20,28},{12,20},{4,12},{0,4},{2,10},{... | collective-permute-start | bytes 602120 | tf_op jit(solution)/shard_map/ppermute | solution.py:283
  73.4 9.9 %collective-permute-start.20 = (f32[392,128]{1,0:T(8,128)}, f32[392,128]{1,0:T(8,128)S(1)}, u32[]{:S(2)}, u32[]{:S(2)}) collective-permute-start(f32[392,128]{1,0:T(8,128)} %collective-permute-done.18.refs_3_), channel_id=1, source_target_pairs={{8,0},{16,8},{24,16},{28,24},{20,28},{12,20},{4,12},{0,4},{2,10},{... | collective-permute-start | bytes 602120 | tf_op jit(solution)/shard_map/ppermute | solution.py:283
  75.2 8.1 %collective-permute-start.27 = (f32[392,128]{1,0:T(8,128)}, f32[392,128]{1,0:T(8,128)S(1)}, u32[]{:S(2)}, u32[]{:S(2)}) collective-permute-start(f32[392,128]{1,0:T(8,128)} %collective-permute-done.26.refs_13_), channel_id=1, source_target_pairs={{0,8},{8,16},{16,24},{24,28},{28,20},{20,12},{12,4},{4,0},{10,2},{... | collective-permute-start | bytes 602120 | tf_op jit(solution)/shard_map/ppermute | solution.py:283
  77.6 10.0 %collective-permute-start.25 = (f32[392,128]{1,0:T(8,128)S(1)}, f32[392,128]{1,0:T(8,128)S(1)}, u32[]{:S(2)}, u32[]{:S(2)}) collective-permute-start(f32[392,128]{1,0:T(8,128)S(1)} %collective-permute-done.24.refs_10_), channel_id=1, source_target_pairs={{0,8},{8,16},{16,24},{24,28},{28,20},{20,12},{12,4},{4,0},{10,2},{... | collective-permute-start | bytes 602120 | tf_op jit(solution)/shard_map/ppermute | solution.py:283
  79.3 12.0 %collective-permute-start.21 = (f32[392,128]{1,0:T(8,128)S(1)}, f32[392,128]{1,0:T(8,128)S(1)}, u32[]{:S(2)}, u32[]{:S(2)}) collective-permute-start(f32[392,128]{1,0:T(8,128)S(1)} %collective-permute-done.19.refs_4_), channel_id=1, source_target_pairs={{8,0},{16,8},{24,16},{28,24},{20,28},{12,20},{4,12},{0,4},{2,10},{... | collective-permute-start | bytes 602120 | tf_op jit(solution)/shard_map/ppermute | solution.py:283
  83.3 8.6 %collective-permute-start.22 = (f32[392,128]{1,0:T(8,128)S(1)}, f32[392,128]{1,0:T(8,128)S(1)}, u32[]{:S(2)}, u32[]{:S(2)}) collective-permute-start(f32[392,128]{1,0:T(8,128)S(1)} %collective-permute-done.20.refs_5_), channel_id=1, source_target_pairs={{8,0},{16,8},{24,16},{28,24},{20,28},{12,20},{4,12},{0,4},{2,10},{... | collective-permute-start | bytes 602120 | tf_op jit(solution)/shard_map/ppermute | solution.py:283
  87.7 10.4 %collective-permute-start.29 = (f32[392,128]{1,0:T(8,128)S(1)}, f32[392,128]{1,0:T(8,128)S(1)}, u32[]{:S(2)}, u32[]{:S(2)}) collective-permute-start(f32[392,128]{1,0:T(8,128)S(1)} %collective-permute-done.25.refs_8_), channel_id=1, source_target_pairs={{0,8},{8,16},{16,24},{24,28},{28,20},{20,12},{12,4},{4,0},{10,2},{... | collective-permute-start | bytes 602120 | tf_op jit(solution)/shard_map/ppermute | solution.py:283
  90.2 8.4 %collective-permute-start.30 = (f32[392,128]{1,0:T(8,128)S(1)}, f32[392,128]{1,0:T(8,128)S(1)}, u32[]{:S(2)}, u32[]{:S(2)}) collective-permute-start(f32[392,128]{1,0:T(8,128)S(1)} %collective-permute-done.28.refs_9_), channel_id=1, source_target_pairs={{0,8},{8,16},{16,24},{24,28},{28,20},{20,12},{12,4},{4,0},{10,2},{... | collective-permute-start | bytes 602120 | tf_op jit(solution)/shard_map/ppermute | solution.py:283
  99.0 7.9 %collective-permute-start.34 = (f32[392,128]{1,0:T(8,128)S(1)}, f32[392,128]{1,0:T(8,128)S(1)}, u32[]{:S(2)}, u32[]{:S(2)}) collective-permute-start(f32[392,128]{1,0:T(8,128)S(1)} %convolution_add_fusion.1), channel_id=1, source_target_pairs={{0,8},{8,16},{16,24},{24,28},{28,20},{20,12},{12,4},{4,0},{10,2},{... | collective-permute-start | bytes 602120 | tf_op jit(solution)/shard_map/ppermute | solution.py:283
  101.5 8.6 %collective-permute-start.41 = (f32[392,128]{1,0:T(8,128)S(1)}, f32[392,128]{1,0:T(8,128)S(1)}, u32[]{:S(2)}, u32[]{:S(2)}) collective-permute-start(f32[392,128]{1,0:T(8,128)S(1)} %convolution_add_fusion), channel_id=1, source_target_pairs={{0,8},{8,16},{16,24},{24,28},{28,20},{20,12},{12,4},{4,0},{10,2},{... | collective-permute-start | bytes 602120 | tf_op jit(solution)/shard_map/ppermute | solution.py:283
  102.9 8.4 %collective-permute-start.31 = (f32[392,128]{1,0:T(8,128)S(1)}, f32[392,128]{1,0:T(8,128)S(1)}, u32[]{:S(2)}, u32[]{:S(2)}) collective-permute-start(f32[392,128]{1,0:T(8,128)S(1)} %convolution_add_fusion.1), channel_id=1, source_target_pairs={{8,0},{16,8},{24,16},{28,24},{20,28},{12,20},{4,12},{0,4},{2,10},{... | collective-permute-start | bytes 602120 | tf_op jit(solution)/shard_map/ppermute | solution.py:283
  103.8 8.7 %collective-permute-start.38 = (f32[392,128]{1,0:T(8,128)S(1)}, f32[392,128]{1,0:T(8,128)S(1)}, u32[]{:S(2)}, u32[]{:S(2)}) collective-permute-start(f32[392,128]{1,0:T(8,128)S(1)} %convolution_add_fusion), channel_id=1, source_target_pairs={{8,0},{16,8},{24,16},{28,24},{20,28},{12,20},{4,12},{0,4},{2,10},{... | collective-permute-start | bytes 602120 | tf_op jit(solution)/shard_map/ppermute | solution.py:283
  111.2 31.7 %collective-permute-start.47 = (f32[128,200]{1,0:T(8,128)S(1)}, f32[128,200]{1,0:T(8,128)S(1)}, u32[]{:S(2)}, u32[]{:S(2)}) collective-permute-start(f32[128,200]{1,0:T(8,128)S(1)} %add_multiply_fusion), channel_id=1, source_target_pairs={{0,2},{2,0},{4,6},{6,4},{8,10},{10,8},{12,14},{14,12},{16,18},{18,... | collective-permute-start | bytes 307208 | tf_op jit(solution)/shard_map/ppermute | solution.py:283
  111.3 8.0 %collective-permute-start.32 = (f32[392,128]{1,0:T(8,128)S(1)}, f32[392,128]{1,0:T(8,128)S(1)}, u32[]{:S(2)}, u32[]{:S(2)}) collective-permute-start(f32[392,128]{1,0:T(8,128)S(1)} %collective-permute-done.31), channel_id=1, source_target_pairs={{8,0},{16,8},{24,16},{28,24},{20,28},{12,20},{4,12},{0,4},{2,10},{... | collective-permute-start | bytes 602120 | tf_op jit(solution)/shard_map/ppermute | solution.py:283
  112.4 11.1 %collective-permute-start.39 = (f32[392,128]{1,0:T(8,128)S(1)}, f32[392,128]{1,0:T(8,128)S(1)}, u32[]{:S(2)}, u32[]{:S(2)}) collective-permute-start(f32[392,128]{1,0:T(8,128)S(1)} %collective-permute-done.38), channel_id=1, source_target_pairs={{8,0},{16,8},{24,16},{28,24},{20,28},{12,20},{4,12},{0,4},{2,10},{... | collective-permute-start | bytes 602120 | tf_op jit(solution)/shard_map/ppermute | solution.py:283
  114.3 9.8 %collective-permute-start.36 = (f32[392,128]{1,0:T(8,128)S(1)}, f32[392,128]{1,0:T(8,128)S(1)}, u32[]{:S(2)}, u32[]{:S(2)}) collective-permute-start(f32[392,128]{1,0:T(8,128)S(1)} %collective-permute-done.35), channel_id=1, source_target_pairs={{0,8},{8,16},{16,24},{24,28},{28,20},{20,12},{12,4},{4,0},{10,2},{... | collective-permute-start | bytes 602120 | tf_op jit(solution)/shard_map/ppermute | solution.py:283
  117.2 9.4 %collective-permute-start.43 = (f32[392,128]{1,0:T(8,128)S(1)}, f32[392,128]{1,0:T(8,128)S(1)}, u32[]{:S(2)}, u32[]{:S(2)}) collective-permute-start(f32[392,128]{1,0:T(8,128)S(1)} %collective-permute-done.42), channel_id=1, source_target_pairs={{0,8},{8,16},{16,24},{24,28},{28,20},{20,12},{12,4},{4,0},{10,2},{... | collective-permute-start | bytes 602120 | tf_op jit(solution)/shard_map/ppermute | solution.py:283
  119.3 8.4 %collective-permute-start.33 = (f32[392,128]{1,0:T(8,128)S(1)}, f32[392,128]{1,0:T(8,128)S(1)}, u32[]{:S(2)}, u32[]{:S(2)}) collective-permute-start(f32[392,128]{1,0:T(8,128)S(1)} %collective-permute-done.32), channel_id=1, source_target_pairs={{8,0},{16,8},{24,16},{28,24},{20,28},{12,20},{4,12},{0,4},{2,10},{... | collective-permute-start | bytes 602120 | tf_op jit(solution)/shard_map/ppermute | solution.py:283
  (34 other events, 371.1 us)

commit v4 on v3

--- a/solution.py
+++ b/solution.py
@@ -39,10 +39,10 @@
     return mxu(tall.astype(jnp.bfloat16), across, ((1,), (0,)))
 
 
-def extract_body(nb, info, active, three, screen, pairs, *refs):
-    kept = refs[0]
+def extract_body(nb, parts, info, active, three, screen, *refs):
+    pairs, kept = refs[:parts], refs[parts] if len(refs) == parts + 8 else None
     value, turned, found, mask, sem_in, sem_out, sem_kept = refs[-7:]
-    act, parts, width = pairs.shape[1], pairs.shape[0], pairs.shape[3]
+    act, _, width = pairs[0].shape
     _, chunk, rows = value.shape
     tiles = act // TILE
     start = pl.multiple_of(info[0] * chunk, chunk)
@@ -66,8 +66,9 @@
     def _(i):
         fetch(i).wait()
         part = value[tile(i)] * mask[...][None]
-        value[tile(i)] = part
-        keep(i).start()
+        if kept is not None:
+            value[tile(i)] = part
+            keep(i).start()
         for w in range(TILE):
             at = pl.ds(pl.multiple_of((i * TILE + w) * rows, rows), rows)
             for k in range(parts):
@@ -85,23 +86,28 @@
                         lines = turned[k, pl.ds(i * TILE * rows + row, TILE, stride=rows), :]
                         found[k, j * nb + t, i * TILE : (i + 1) * TILE, :] = lines
 
-    give = pltpu.make_async_copy(found, pairs, sem_out)
-    give.start()
-    give.wait()
-    for i in range(tiles):
-        keep(i).wait()
-
-
-def extract(three_index, screen_mask, active, info, chunk, width, nb):
+    def give(k):
+        return pltpu.make_async_copy(found.at[k], pairs[k], sem_out.at[k])
+
+    for k in range(parts):
+        give(k).start()
+    for k in range(parts):
+        give(k).wait()
+    if kept is not None:
+        for i in range(tiles):
+            keep(i).wait()
+
+
+def extract(three_index, screen_mask, active, info, chunk, width, nb, keep):
     act, slab, rows = three_index.shape
     tiles = act // TILE
-    out_shape = [
-        jax.ShapeDtypeStruct((chunk // width, act, act, width), jnp.float32),
-        jax.ShapeDtypeStruct((act, chunk, rows), jnp.float32),
-    ]
+    parts = chunk // width
+    out_shape = [jax.ShapeDtypeStruct((act, act, width), jnp.float32)] * parts
+    if keep:
+        out_shape.append(jax.ShapeDtypeStruct((act, chunk, rows), jnp.float32))
     smem, vmem, hbm, anywhere = places()
     return pl.pallas_call(
-        functools.partial(extract_body, nb),
+        functools.partial(extract_body, nb, parts),
         out_shape=out_shape,
         in_specs=[smem, smem, hbm, vmem],
         out_specs=[anywhere] * len(out_shape),
@@ -111,30 +117,33 @@
             pltpu.VMEM((chunk // width, act, act, width), jnp.float32),
             pltpu.VMEM((chunk, rows), jnp.float32),
             pltpu.SemaphoreType.DMA((tiles,)),
-            pltpu.SemaphoreType.DMA,
+            pltpu.SemaphoreType.DMA((parts,)),
             pltpu.SemaphoreType.DMA((tiles,)),
         ],
         compiler_params=pltpu.CompilerParams(vmem_limit_bytes=50 * MIB),
         cost_estimate=pl.CostEstimate(
             flops=4 * act * act * chunk * rows,
             transcendentals=0,
-            bytes_accessed=4 * act * chunk * (act + 2 * rows),
+            bytes_accessed=4 * act * chunk * (act + rows * (2 if keep else 1)),
         ),
         name="extract",
     )(info, active, three_index, screen_mask)
 
 
-def q_body(nb, count, info, kept, sib, *refs):
-    blocks, (out, own, lhs, acc, sems) = refs[: 2 * count], refs[2 * count :]
+def q_body(nb, count, info, three, screen, sib, *refs):
+    blocks, (out, own, lhs, acc, mask, sems) = refs[: 2 * count], refs[2 * count :]
     act, depth, rows = own.shape
     chunk = depth // 2
     height = acc.shape[0]
 
+    start = pl.multiple_of(info[0] * depth, depth)
+
     def bring(tile, i):
-        return pltpu.make_async_copy(kept.at[tile], own.at[tile], sems.at[i])
+        return pltpu.make_async_copy(three.at[tile, pl.ds(start, depth), :], own.at[tile], sems.at[i])
 
     for i in range(act // TILE):
         bring(pl.ds(i * TILE, TILE), i).start()
+    mask[...] = expand_mask(screen, info[0], depth, rows)
     lhs[...] = jnp.zeros_like(lhs)
     acc[...] = jnp.zeros_like(acc)
     nn = ((1,), (0,))
@@ -149,7 +158,7 @@
         pieces = [lhs[k, n * height : (n + 1) * height, :] for n in range(TILE) for k in range(2)]
         left, left_low = split(jnp.concatenate(pieces, axis=1))
         bring(tile, i).wait()
-        right = [x[tile].reshape(TILE * depth, rows) for x in (own, sib)]
+        right = [x.reshape(TILE * depth, rows) for x in (own[tile] * mask[...][None], sib[tile])]
         top, low = split(jnp.concatenate(right, axis=1))
         both = mxu(jnp.concatenate([left, left_low], axis=0), top, nn)
         acc[...] += both[:height] + both[height:] + mxu(left, low, nn)
@@ -159,20 +168,21 @@
         out[pl.ds(where, TILE), :] = acc[j * TILE : (j + 1) * TILE, :]
 
 
-def q_partial(own, sib, blocks, info):
-    act, depth, rows = own.shape
+def q_partial(three_index, screen_mask, sib, blocks, info):
+    act, depth, rows = sib.shape
     count = len(blocks[0])
     nb = act // count
     smem, vmem, hbm, anywhere = places()
     return pl.pallas_call(
         functools.partial(q_body, nb, count),
         out_shape=jax.ShapeDtypeStruct((count * TILE, 2 * rows), jnp.float32),
-        in_specs=[smem, hbm, vmem] + [vmem] * (2 * count),
+        in_specs=[smem, hbm, vmem, vmem] + [vmem] * (2 * count),
         out_specs=vmem,
         scratch_shapes=[
             pltpu.VMEM((act, depth, rows), jnp.float32),
             pltpu.VMEM((2, TILE * count * TILE, depth // 2), jnp.float32),
             pltpu.VMEM((count * TILE, 2 * rows), jnp.float32),
+            pltpu.VMEM((depth, rows), jnp.float32),
             pltpu.SemaphoreType.DMA((act // TILE,)),
         ],
         compiler_params=pltpu.CompilerParams(vmem_limit_bytes=49 * MIB),
@@ -182,7 +192,7 @@
             bytes_accessed=4 * act * depth * (act + 2 * rows),
         ),
         name="qpartial",
-    )(info, own, sib, *[b.reshape(nb, act, depth // 2) for half in blocks for b in half])
+    )(info, three_index, screen_mask, sib, *[b.reshape(nb, act, depth // 2) for half in blocks for b in half])
 
 
 def half_body(chips, info, own, twin, *refs):
@@ -287,20 +297,19 @@
 
     shells = screen_mask.T
     far = chips // 2
-    def pick(info):
-        found, kept = extract(three_index, shells, active_orbitals, info, depth, chunk, nb)
-        return found.reshape(2, act * act, chunk), kept
+    def pick(info, keep):
+        *found, last = extract(three_index, shells, active_orbitals, info, depth, chunk, nb, keep)
+        flat = [f.reshape(act * act, chunk) for f in (found if keep else found + [last])]
+        return flat, last
 
     other = hop(pair_density, twin)
-    given, sib_three = pick(theirs)
-    got = hop(given, twin)
+    given, sib_three = pick(theirs, True)
+    got = [hop(g, twin) for g in given]
     given, mine = lax.optimization_barrier((given, mine))
-    found, own_three = pick(mine)
+    found, _ = pick(mine, False)
     contributions = []
-    for k in range(2):
-        contributions.append(
-            [found[k, j * blk : (j + 1) * blk] + got[k, j * blk : (j + 1) * blk] for j in range(chips)]
-        )
+    for f, g in zip(found, got):
+        contributions.append([f[j * blk : (j + 1) * blk] + g[j * blk : (j + 1) * blk] for j in range(chips)])
     inactive_fock, active_fock, contributions, other, sib_three = lax.optimization_barrier(
         (inactive_fock, active_fock, contributions, other, sib_three)
     )
@@ -339,7 +348,7 @@
     halves = half_partial(pair_density, other, near_blocks, mine, chips)
     halves = [h + jnp.dot(density_far, gathered[k][far], precision=HIGH) for k, h in enumerate(halves)]
     halves = lax.optimization_barrier(halves)
-    q = q_partial(own_three, sib_three, [gather(x) for x in halves], mine)
+    q = q_partial(three_index, shells, sib_three, [gather(x) for x in halves], mine)
     q = q.reshape(chips, TILE, 2 * rows)[:, :nb].reshape(act, 2 * rows)
 
     share = rows // aux
@@ -358,10 +367,6 @@
 
     once = (aux_at == 0).astype(jnp.float32)
     own_q, twin_q = q[:, :rows] + once * opened.T, q[:, rows:]
-    q_mine = own_q + hop(twin_q, twin)
-    sent = lax.dynamic_slice_in_dim(q_mine, (1 - aux_at) * share, share, 1)
-    q_rows = lax.dynamic_slice_in_dim(q_mine, aux_at * share, share, 1) + across(sent, 0, 1)
-
     occ_index = jnp.concatenate([jnp.arange(inactive, dtype=jnp.int32), active_orbitals])
     my_rows, twin_rows = first_row + local_rows, (me ^ 1) * rows + local_rows
     width = (inactive + act) // 2
@@ -374,7 +379,14 @@
         top = jnp.dot(jnp.concatenate([own_q, twin_q], axis=1), jnp.concatenate(chosen, axis=0), precision=HIGHEST)
         return jnp.concatenate([top, lax.dynamic_slice_in_dim(act_closed, half * width, width, 1)], axis=0)
 
-    occ = picked(core) + hop(picked(1 - core), twin)
+    keep_occ, send_occ = picked(core), picked(1 - core)
+    twin_q, keep_occ, send_occ = lax.optimization_barrier((twin_q, keep_occ, send_occ))
+    occ = keep_occ + hop(send_occ, twin)
+
+    q_mine = own_q + hop(twin_q, twin)
+    sent = lax.dynamic_slice_in_dim(q_mine, (1 - aux_at) * share, share, 1)
+    q_rows = lax.dynamic_slice_in_dim(q_mine, aux_at * share, share, 1) + across(sent, 0, 1)
+
     occ = occ + across(occ, 2, 0) + across(occ, 0, 1) + across(occ, 2, 1)
     occ = occ + across(occ, 4, 0) + across(occ, 8, 0) + across(occ, 12, 0)
     occ_twin = hop(occ, twin)

time: 163 us -> 159 us (0.975)
  other arithmetic: 5.96 us -> 2.66 us
  local copies, waits for them, and re-layouts: 4.04 us -> 7.19 us
  starting transfers between devices: 63.9 us -> 62 us
    add x3 -> x4, other arithmetic: 3.75 us -> 0.47 us  [the longest x2 0.45 us: fast(): f[j * blk:(j + 1) * blk] + g[j * blk:(j + 1) * blk]]
    unnamed x20 -> x24, local copies, waits for them, and re-layouts: 3.58 us -> 6.52 us
    ppermute x49 -> x50, starting transfers between devices: 54.3 us -> 52.5 us  [hop(): return lax.ppermute(x, 'orb', pairs)]
    pallas_call x2, Pallas kernels: 14.3 us -> 12.5 us  [extract(): pl.pallas_call(functools.partial(extract_body, nb, parts), out_shape=out_...]
    ppermute x49 -> x50, waiting for transfers between devices: 52 us -> 51.7 us  [hop(): return lax.ppermute(x, 'orb', pairs)]
  transfers between devices with their start and end apart: 56 -> 57, of which waited for: 37 -> 35; matrix products, arithmetic and copies ran while one was open for 4% -> 3% of each run, Pallas kernels for 13% -> 17%
where the time goes in v4:
time: 159 us
  starting transfers between devices  62 us (39%)
  waiting for transfers between devices  56.6 us (36%)
  Pallas kernels  27 us (17%)
  local copies, waits for them, and re-layouts  7.19 us (5%)
  matrix products  2.85 us (2%)
  other arithmetic  2.66 us (2%)
    ppermute x50, starting transfers between devices, hop(): return lax.ppermute(x, 'orb', pairs)  52.5 us
    ppermute x50, waiting for transfers between devices, hop(): return lax.ppermute(x, 'orb', pairs)  51.7 us
    pallas_call x2, Pallas kernels, extract(): pl.pallas_call(functools.partial(extract_body, nb, parts), out_shape=out_...  12.5 us
    pallas_call x1, Pallas kernels, q_partial(): pl.pallas_call(functools.partial(q_body, nb, count), out_shape=jax.ShapeD...  9.98 us
    ppermute x7, starting transfers between devices, across(): return lax.ppermute(x, ('orb', 'aux'), table)  9.52 us
    unnamed x24, local copies, waits for them, and re-layouts  6.52 us
    ppermute x7, waiting for transfers between devices, across(): return lax.ppermute(x, ('orb', 'aux'), table)  4.92 us
    pallas_call x1, Pallas kernels, half_partial(): pl.pallas_call(functools.partial(half_body, chips), out_shape=[jax.ShapeD...  4.46 us
  transfers between devices with their start and end apart: 57, of which 35 were waited for; matrix products, arithmetic and copies ran while one was open for 3% of the time, Pallas kernels for 17%

profile of v4, /device:TPU:0, one launch (start us, length us, event | category | flops | bytes accessed | tf_op | source)
XLA Modules:
  0.0 158.8 jit_solution(18041610146085328006)
XLA Ops:
  1.9 7.0 %extract.2 = (f32[56,56,128]{2,1,0:T(8,128)S(1)}, f32[56,56,128]{2,1,0:T(8,128)S(1)}, f32[56,256,128]{2,1,0:T(8,128)}) custom-call(s32[11]{0:T(128)S(1)} %add_add_fusion.4.info, s32[56]{0:T(128)S(1)} %copy-done.6, f32[56,512,128]{2,1,0:T(8,128)} %three.5, s32[8,32]{1,0:T(8,128)S(1)} %bitcast.87), custom_call_target="tpu_custom_call" | custom-call | flops 411041792 | bytes 17891328 | tf_op jit(solution)/shard_map/extract/pallas_call | solution.py:109
  9.6 5.5 %extract.3 = (f32[56,56,128]{2,1,0:T(8,128)S(1)}, f32[56,56,128]{2,1,0:T(8,128)S(1)}) custom-call(s32[11]{0:T(128)S(1)} %add_add_fusion.5.info, s32[56]{0:T(128)S(1)} %copy-done.6, f32[56,512,128]{2,1,0:T(8,128)} %three.5, s32[8,32]{1,0:T(8,128)S(1)} %bitcast.88), custom_call_target="tpu_custom_call" | custom-call | flops 411041792 | bytes 10551296 | tf_op jit(solution)/shard_map/extract/pallas_call | solution.py:109
  15.9 2.4 %slice-done = s8[4194304]{0:T(1024)(128)(4,1)S(1)} async-done(((s8[7340032]{0:T(1024)(128)(4,1)}), s8[4194304]{0:T(1024)(128)(4,1)S(1)}, s32[]{:S(2)}) %slice-start) | async-done | bytes 4194328
  19.4 3.2 %collective-permute-start.3 = (f32[392,128]{1,0:T(8,128)S(1)}, f32[392,128]{1,0:T(8,128)S(1)}, u32[]{:S(2)}, u32[]{:S(2)}) collective-permute-start(f32[392,128]{1,0:T(8,128)S(1)} %get-tuple-element.53), channel_id=1, source_target_pairs={{0,8},{8,16},{16,24},{24,28},{28,20},{20,12},{12,4},{4,0},{10,2},{... | collective-permute-start | bytes 602120 | tf_op jit(solution)/shard_map/ppermute | solution.py:293
  22.7 2.0 %collective-permute-start.5 = (f32[392,128]{1,0:T(8,128)S(1)}, f32[392,128]{1,0:T(8,128)S(1)}, u32[]{:S(2)}, u32[]{:S(2)}) collective-permute-start(f32[392,128]{1,0:T(8,128)S(1)} %get-tuple-element.55), channel_id=1, source_target_pairs={{0,8},{8,16},{16,24},{24,28},{28,20},{20,12},{12,4},{4,0},{10,2},{... | collective-permute-start | bytes 602120 | tf_op jit(solution)/shard_map/ppermute | solution.py:293
  24.7 3.3 %collective-permute-done.3 = f32[392,128]{1,0:T(8,128)S(1)} collective-permute-done((f32[392,128]{1,0:T(8,128)S(1)}, f32[392,128]{1,0:T(8,128)S(1)}, u32[]{:S(2)}, u32[]{:S(2)}) %collective-permute-start.3) | collective-permute-done | bytes 200736 | tf_op jit(solution)/shard_map/ppermute | solution.py:293
  28.0 2.5 %collective-permute-done.4 = f32[392,128]{1,0:T(8,128)S(1)} collective-permute-done((f32[392,128]{1,0:T(8,128)S(1)}, f32[392,128]{1,0:T(8,128)S(1)}, u32[]{:S(2)}, u32[]{:S(2)}) %collective-permute-start.4) | collective-permute-done | bytes 200736 | tf_op jit(solution)/shard_map/ppermute | solution.py:293
  32.7 1.9 %collective-permute-start.8 = (f32[392,128]{1,0:T(8,128)S(1)}, f32[392,128]{1,0:T(8,128)S(1)}, u32[]{:S(2)}, u32[]{:S(2)}) collective-permute-start(f32[392,128]{1,0:T(8,128)S(1)} %add.232), channel_id=1, source_target_pairs={{0,8},{8,16},{16,24},{24,28},{28,20},{20,12},{12,4},{4,0},{10,2},{... | collective-permute-start | bytes 602120 | tf_op jit(solution)/shard_map/ppermute | solution.py:293
  34.6 1.8 %collective-permute-start.13 = (f32[392,128]{1,0:T(8,128)S(1)}, f32[392,128]{1,0:T(8,128)S(1)}, u32[]{:S(2)}, u32[]{:S(2)}) collective-permute-start(f32[392,128]{1,0:T(8,128)S(1)} %add.239), channel_id=1, source_target_pairs={{0,8},{8,16},{16,24},{24,28},{28,20},{20,12},{12,4},{4,0},{10,2},{... | collective-permute-start | bytes 602120 | tf_op jit(solution)/shard_map/ppermute | solution.py:293
  36.7 1.9 %collective-permute-done.8 = f32[392,128]{1,0:T(8,128)S(1)} collective-permute-done((f32[392,128]{1,0:T(8,128)S(1)}, f32[392,128]{1,0:T(8,128)S(1)}, u32[]{:S(2)}, u32[]{:S(2)}) %collective-permute-start.8) | collective-permute-done | bytes 200736 | tf_op jit(solution)/shard_map/ppermute | solution.py:293
  38.6 2.5 %collective-permute-start.9 = (f32[392,128]{1,0:T(8,128)S(1)}, f32[392,128]{1,0:T(8,128)S(1)}, u32[]{:S(2)}, u32[]{:S(2)}) collective-permute-start(f32[392,128]{1,0:T(8,128)S(1)} %add.233), channel_id=1, source_target_pairs={{0,8},{8,16},{16,24},{24,28},{28,20},{20,12},{12,4},{4,0},{10,2},{... | collective-permute-start | bytes 602120 | tf_op jit(solution)/shard_map/ppermute | solution.py:293
  42.9 2.5 %collective-permute-start.14 = (f32[392,128]{1,0:T(8,128)S(1)}, f32[392,128]{1,0:T(8,128)S(1)}, u32[]{:S(2)}, u32[]{:S(2)}) collective-permute-start(f32[392,128]{1,0:T(8,128)S(1)} %add.240), channel_id=1, source_target_pairs={{0,8},{8,16},{16,24},{24,28},{28,20},{20,12},{12,4},{4,0},{10,2},{... | collective-permute-start | bytes 602120 | tf_op jit(solution)/shard_map/ppermute | solution.py:293
  47.2 2.5 %collective-permute-start.10 = (f32[392,128]{1,0:T(8,128)S(1)}, f32[392,128]{1,0:T(8,128)S(1)}, u32[]{:S(2)}, u32[]{:S(2)}) collective-permute-start(f32[392,128]{1,0:T(8,128)S(1)} %add.234), channel_id=1, source_target_pairs={{0,8},{8,16},{16,24},{24,28},{28,20},{20,12},{12,4},{4,0},{10,2},{... | collective-permute-start | bytes 602120 | tf_op jit(solution)/shard_map/ppermute | solution.py:293
  51.5 2.5 %collective-permute-start.15 = (f32[392,128]{1,0:T(8,128)S(1)}, f32[392,128]{1,0:T(8,128)S(1)}, u32[]{:S(2)}, u32[]{:S(2)}) collective-permute-start(f32[392,128]{1,0:T(8,128)S(1)} %add.241), channel_id=1, source_target_pairs={{0,8},{8,16},{16,24},{24,28},{28,20},{20,12},{12,4},{4,0},{10,2},{... | collective-permute-start | bytes 602120 | tf_op jit(solution)/shard_map/ppermute | solution.py:293
  57.9 1.9 %collective-permute-start.24 = (f32[392,128]{1,0:T(8,128)S(1)}, f32[392,128]{1,0:T(8,128)S(1)}, u32[]{:S(2)}, u32[]{:S(2)}) collective-permute-start(f32[392,128]{1,0:T(8,128)S(1)} %add_add_fusion.1.refs_0_), channel_id=1, source_target_pairs={{0,8},{8,16},{16,24},{24,28},{28,20},{20,12},{12,4},{4,0},{10,2},{... | collective-permute-start | bytes 602120 | tf_op jit(solution)/shard_map/ppermute | solution.py:293
  60.6 2.0 %collective-permute-start.19 = (f32[392,128]{1,0:T(8,128)S(1)}, f32[392,128]{1,0:T(8,128)}, u32[]{:S(2)}, u32[]{:S(2)}) collective-permute-start(f32[392,128]{1,0:T(8,128)S(1)} %add_add_fusion.refs_1_), channel_id=1, source_target_pairs={{8,0},{16,8},{24,16},{28,24},{20,28},{12,20},{4,12},{0,4},{2,10},{... | collective-permute-start | bytes 602120 | tf_op jit(solution)/shard_map/ppermute | solution.py:293
  62.6 3.7 %collective-permute-done.24.refs_12_ = f32[392,128]{1,0:T(8,128)S(1)} collective-permute-done((f32[392,128]{1,0:T(8,128)S(1)}, f32[392,128]{1,0:T(8,128)S(1)}, u32[]{:S(2)}, u32[]{:S(2)}) %collective-permute-start.24) | collective-permute-done | bytes 200736 | tf_op jit(solution)/shard_map/ppermute | solution.py:293
  68.5 1.9 %collective-permute-done.19.refs_3_ = f32[392,128]{1,0:T(8,128)} collective-permute-done((f32[392,128]{1,0:T(8,128)S(1)}, f32[392,128]{1,0:T(8,128)}, u32[]{:S(2)}, u32[]{:S(2)}) %collective-permute-start.19) | collective-permute-done | bytes 200736 | tf_op jit(solution)/shard_map/ppermute | solution.py:293
  70.5 2.0 %collective-permute-start.21 = (f32[392,128]{1,0:T(8,128)}, f32[392,128]{1,0:T(8,128)S(1)}, u32[]{:S(2)}, u32[]{:S(2)}) collective-permute-start(f32[392,128]{1,0:T(8,128)} %collective-permute-done.19.refs_3_), channel_id=1, source_target_pairs={{8,0},{16,8},{24,16},{28,24},{20,28},{12,20},{4,12},{0,4},{2,10},{... | collective-permute-start | bytes 602120 | tf_op jit(solution)/shard_map/ppermute | solution.py:293
  73.0 1.9 %collective-permute-done.25.refs_10_ = f32[392,128]{1,0:T(8,128)S(1)} collective-permute-done((f32[392,128]{1,0:T(8,128)S(1)}, f32[392,128]{1,0:T(8,128)S(1)}, u32[]{:S(2)}, u32[]{:S(2)}) %collective-permute-start.25) | collective-permute-done | bytes 200736 | tf_op jit(solution)/shard_map/ppermute | solution.py:293
  77.1 2.0 %collective-permute-done.21.refs_5_ = f32[392,128]{1,0:T(8,128)S(1)} collective-permute-done((f32[392,128]{1,0:T(8,128)}, f32[392,128]{1,0:T(8,128)S(1)}, u32[]{:S(2)}, u32[]{:S(2)}) %collective-permute-start.21) | collective-permute-done | bytes 200736 | tf_op jit(solution)/shard_map/ppermute | solution.py:293
  81.8 3.3 %collective-permute-done.26.refs_8_ = f32[392,128]{1,0:T(8,128)S(1)} collective-permute-done((f32[392,128]{1,0:T(8,128)S(1)}, f32[392,128]{1,0:T(8,128)S(1)}, u32[]{:S(2)}, u32[]{:S(2)}) %collective-permute-start.26) | collective-permute-done | bytes 200736 | tf_op jit(solution)/shard_map/ppermute | solution.py:293
  89.7 4.5 %half.1 = (f32[392,128]{1,0:T(8,128)S(1)}, f32[392,128]{1,0:T(8,128)S(1)}) custom-call(s32[11]{0:T(128)S(1)} %add_add_fusion.5.info, f32[196,3136]{1,0:T(8,128)S(1)} %copy-done.1, f32[196,3136]{1,0:T(8,128)S(1)} %copy-done.3, f32[392,128]{1,0:T(8,128)S(1)} %add_add_fusion.1.refs_0_, f32[392,128]{1,0:T(8,128)S(1)} %add_add_fusion.refs_1_, ...), custom_call_target="tpu_custom_call" | custom-call | flops 1888223232 | bytes 8128512 | tf_op jit(solution)/shard_map/half/pallas_call | solution.py:243
  95.2 2.5 %collective-permute-start.35 = (f32[392,128]{1,0:T(8,128)S(1)}, f32[392,128]{1,0:T(8,128)S(1)}, u32[]{:S(2)}, u32[]{:S(2)}) collective-permute-start(f32[392,128]{1,0:T(8,128)S(1)} %convolution_add_fusion.1), channel_id=1, source_target_pairs={{0,8},{8,16},{16,24},{24,28},{28,20},{20,12},{12,4},{4,0},{10,2},{... | collective-permute-start | bytes 602120 | tf_op jit(solution)/shard_map/ppermute | solution.py:293
  97.7 2.0 %collective-permute-start.42 = (f32[392,128]{1,0:T(8,128)S(1)}, f32[392,128]{1,0:T(8,128)S(1)}, u32[]{:S(2)}, u32[]{:S(2)}) collective-permute-start(f32[392,128]{1,0:T(8,128)S(1)} %convolution_add_fusion), channel_id=1, source_target_pairs={{0,8},{8,16},{16,24},{24,28},{28,20},{20,12},{12,4},{4,0},{10,2},{... | collective-permute-start | bytes 602120 | tf_op jit(solution)/shard_map/ppermute | solution.py:293
  100.1 3.1 %collective-permute-done.35 = f32[392,128]{1,0:T(8,128)S(1)} collective-permute-done((f32[392,128]{1,0:T(8,128)S(1)}, f32[392,128]{1,0:T(8,128)S(1)}, u32[]{:S(2)}, u32[]{:S(2)}) %collective-permute-start.35) | collective-permute-done | bytes 200736 | tf_op jit(solution)/shard_map/ppermute | solution.py:293
  103.1 2.5 %collective-permute-start.36 = (f32[392,128]{1,0:T(8,128)S(1)}, f32[392,128]{1,0:T(8,128)S(1)}, u32[]{:S(2)}, u32[]{:S(2)}) collective-permute-start(f32[392,128]{1,0:T(8,128)S(1)} %collective-permute-done.35), channel_id=1, source_target_pairs={{0,8},{8,16},{16,24},{24,28},{28,20},{20,12},{12,4},{4,0},{10,2},{... | collective-permute-start | bytes 602120 | tf_op jit(solution)/shard_map/ppermute | solution.py:293
  111.4 2.7 %collective-permute-done.43 = f32[392,128]{1,0:T(8,128)S(1)} collective-permute-done((f32[392,128]{1,0:T(8,128)S(1)}, f32[392,128]{1,0:T(8,128)S(1)}, u32[]{:S(2)}, u32[]{:S(2)}) %collective-permute-start.43) | collective-permute-done | bytes 200736 | tf_op jit(solution)/shard_map/ppermute | solution.py:293
  116.6 3.6 %collective-permute-done.40 = f32[392,128]{1,0:T(8,128)S(1)} collective-permute-done((f32[392,128]{1,0:T(8,128)S(1)}, f32[392,128]{1,0:T(8,128)S(1)}, u32[]{:S(2)}, u32[]{:S(2)}) %collective-permute-start.40) | collective-permute-done | bytes 200736 | tf_op jit(solution)/shard_map/ppermute | solution.py:293
  124.3 3.7 %collective-permute-done.41 = f32[392,128]{1,0:T(8,128)S(1)} collective-permute-done((f32[392,128]{1,0:T(8,128)S(1)}, f32[392,128]{1,0:T(8,128)S(1)}, u32[]{:S(2)}, u32[]{:S(2)}) %collective-permute-start.41) | collective-permute-done | bytes 200736 | tf_op jit(solution)/shard_map/ppermute | solution.py:293
  129.8 10.0 %qpartial.1 = f32[64,256]{1,0:T(8,128)S(1)} custom-call(s32[11]{0:T(128)S(1)} %add_add_fusion.5.info, f32[56,512,128]{2,1,0:T(8,128)} %three.5, s32[8,32]{1,0:T(8,128)S(1)} %bitcast.89, f32[56,256,128]{2,1,0:T(8,128)} %collective-permute-done.7.sib, f32[7,56,128]{2,1,0:T(8,128)S(1)} %bitcast.70, f32[7,56,128]{2,1,0:T(8,128)S(1)} %bitcast.75, ...), custom_call_target="tpu_custom_call" | custom-call | flops 1233125376 | bytes 17891328 | tf_op jit(solution)/shard_map/qpartial/pallas_call | solution.py:176
  150.5 2.0 %collective-permute-start.53 = (f32[112,128]{1,0:T(8,128)S(1)}, f32[112,128]{1,0:T(8,128)S(1)}, u32[]{:S(2)}, u32[]{:S(2)}) collective-permute-start(f32[112,128]{1,0:T(8,128)S(1)} %add_add_fusion.3), channel_id=1, source_target_pairs={{0,8},{1,9},{2,10},{3,11},{4,12},{5,13},{6,14},{7,15},{8,0},{9,1},... | collective-permute-start | bytes 172040 | tf_op jit(solution)/shard_map/ppermute | solution.py:359
  (165 shorter events, 61.4 us)
Async XLA Ops:
  0.0 15.8 %collective-permute-start.2 = (f32[196,3136]{1,0:T(8,128)}, f32[196,3136]{1,0:T(8,128)S(1)}, u32[]{:S(2)}, u32[]{:S(2)}) collective-permute-start(f32[196,3136]{1,0:T(8,128)} %own.1), channel_id=1, source_target_pairs={{0,2},{2,0},{4,6},{6,4},{8,10},{10,8},{12,14},{14,12},{16,18},{18,... | collective-permute-start | bytes 7375880 | tf_op jit(solution)/shard_map/ppermute | solution.py:293
  19.3 13.4 %collective-permute-start.7 = (f32[56,256,128]{2,1,0:T(8,128)S(1)}, f32[56,256,128]{2,1,0:T(8,128)}, u32[]{:S(2)}, u32[]{:S(2)}) collective-permute-start(f32[56,256,128]{2,1,0:T(8,128)S(1)} %bitcast.93), channel_id=1, source_target_pairs={{0,2},{2,0},{4,6},{6,4},{8,10},{10,8},{12,14},{14,12},{16,18},{18,... | collective-permute-start | bytes 22020104 | tf_op jit(solution)/shard_map/ppermute | solution.py:293
  19.4 8.5 %collective-permute-start.3 = (f32[392,128]{1,0:T(8,128)S(1)}, f32[392,128]{1,0:T(8,128)S(1)}, u32[]{:S(2)}, u32[]{:S(2)}) collective-permute-start(f32[392,128]{1,0:T(8,128)S(1)} %get-tuple-element.53), channel_id=1, source_target_pairs={{0,8},{8,16},{16,24},{24,28},{28,20},{20,12},{12,4},{4,0},{10,2},{... | collective-permute-start | bytes 602120 | tf_op jit(solution)/shard_map/ppermute | solution.py:293
  22.7 9.2 %collective-permute-start.5 = (f32[392,128]{1,0:T(8,128)S(1)}, f32[392,128]{1,0:T(8,128)S(1)}, u32[]{:S(2)}, u32[]{:S(2)}) collective-permute-start(f32[392,128]{1,0:T(8,128)S(1)} %get-tuple-element.55), channel_id=1, source_target_pairs={{0,8},{8,16},{16,24},{24,28},{28,20},{20,12},{12,4},{4,0},{10,2},{... | collective-permute-start | bytes 602120 | tf_op jit(solution)/shard_map/ppermute | solution.py:293
  34.6 8.3 %collective-permute-start.13 = (f32[392,128]{1,0:T(8,128)S(1)}, f32[392,128]{1,0:T(8,128)S(1)}, u32[]{:S(2)}, u32[]{:S(2)}) collective-permute-start(f32[392,128]{1,0:T(8,128)S(1)} %add.239), channel_id=1, source_target_pairs={{0,8},{8,16},{16,24},{24,28},{28,20},{20,12},{12,4},{4,0},{10,2},{... | collective-permute-start | bytes 602120 | tf_op jit(solution)/shard_map/ppermute | solution.py:293
  36.3 9.1 %collective-permute-start.11 = (f32[392,128]{1,0:T(8,128)S(1)}, f32[392,128]{1,0:T(8,128)S(1)}, u32[]{:S(2)}, u32[]{:S(2)}) collective-permute-start(f32[392,128]{1,0:T(8,128)S(1)} %add.236), channel_id=1, source_target_pairs={{8,0},{16,8},{24,16},{28,24},{20,28},{12,20},{4,12},{0,4},{2,10},{... | collective-permute-start | bytes 602120 | tf_op jit(solution)/shard_map/ppermute | solution.py:293
  38.6 8.6 %collective-permute-start.9 = (f32[392,128]{1,0:T(8,128)S(1)}, f32[392,128]{1,0:T(8,128)S(1)}, u32[]{:S(2)}, u32[]{:S(2)}) collective-permute-start(f32[392,128]{1,0:T(8,128)S(1)} %add.233), channel_id=1, source_target_pairs={{0,8},{8,16},{16,24},{24,28},{28,20},{20,12},{12,4},{4,0},{10,2},{... | collective-permute-start | bytes 602120 | tf_op jit(solution)/shard_map/ppermute | solution.py:293
  41.2 8.6 %collective-permute-start.16 = (f32[392,128]{1,0:T(8,128)S(1)}, f32[392,128]{1,0:T(8,128)S(1)}, u32[]{:S(2)}, u32[]{:S(2)}) collective-permute-start(f32[392,128]{1,0:T(8,128)S(1)} %add.243), channel_id=1, source_target_pairs={{8,0},{16,8},{24,16},{28,24},{20,28},{12,20},{4,12},{0,4},{2,10},{... | collective-permute-start | bytes 602120 | tf_op jit(solution)/shard_map/ppermute | solution.py:293
  42.9 8.6 %collective-permute-start.14 = (f32[392,128]{1,0:T(8,128)S(1)}, f32[392,128]{1,0:T(8,128)S(1)}, u32[]{:S(2)}, u32[]{:S(2)}) collective-permute-start(f32[392,128]{1,0:T(8,128)S(1)} %add.240), channel_id=1, source_target_pairs={{0,8},{8,16},{16,24},{24,28},{28,20},{20,12},{12,4},{4,0},{10,2},{... | collective-permute-start | bytes 602120 | tf_op jit(solution)/shard_map/ppermute | solution.py:293
  45.5 8.5 %collective-permute-start.12 = (f32[392,128]{1,0:T(8,128)S(1)}, f32[392,128]{1,0:T(8,128)S(1)}, u32[]{:S(2)}, u32[]{:S(2)}) collective-permute-start(f32[392,128]{1,0:T(8,128)S(1)} %add.237), channel_id=1, source_target_pairs={{8,0},{16,8},{24,16},{28,24},{20,28},{12,20},{4,12},{0,4},{2,10},{... | collective-permute-start | bytes 602120 | tf_op jit(solution)/shard_map/ppermute | solution.py:293
  47.2 8.4 %collective-permute-start.10 = (f32[392,128]{1,0:T(8,128)S(1)}, f32[392,128]{1,0:T(8,128)S(1)}, u32[]{:S(2)}, u32[]{:S(2)}) collective-permute-start(f32[392,128]{1,0:T(8,128)S(1)} %add.234), channel_id=1, source_target_pairs={{0,8},{8,16},{16,24},{24,28},{28,20},{20,12},{12,4},{4,0},{10,2},{... | collective-permute-start | bytes 602120 | tf_op jit(solution)/shard_map/ppermute | solution.py:293
  57.9 8.5 %collective-permute-start.24 = (f32[392,128]{1,0:T(8,128)S(1)}, f32[392,128]{1,0:T(8,128)S(1)}, u32[]{:S(2)}, u32[]{:S(2)}) collective-permute-start(f32[392,128]{1,0:T(8,128)S(1)} %add_add_fusion.1.refs_0_), channel_id=1, source_target_pairs={{0,8},{8,16},{16,24},{24,28},{28,20},{20,12},{12,4},{4,0},{10,2},{... | collective-permute-start | bytes 602120 | tf_op jit(solution)/shard_map/ppermute | solution.py:293
  59.8 7.9 %collective-permute-start.18 = (f32[392,128]{1,0:T(8,128)S(1)}, f32[392,128]{1,0:T(8,128)S(1)}, u32[]{:S(2)}, u32[]{:S(2)}) collective-permute-start(f32[392,128]{1,0:T(8,128)S(1)} %add_add_fusion.1.refs_0_), channel_id=1, source_target_pairs={{8,0},{16,8},{24,16},{28,24},{20,28},{12,20},{4,12},{0,4},{2,10},{... | collective-permute-start | bytes 602120 | tf_op jit(solution)/shard_map/ppermute | solution.py:293
  60.6 9.9 %collective-permute-start.19 = (f32[392,128]{1,0:T(8,128)S(1)}, f32[392,128]{1,0:T(8,128)}, u32[]{:S(2)}, u32[]{:S(2)}) collective-permute-start(f32[392,128]{1,0:T(8,128)S(1)} %add_add_fusion.refs_1_), channel_id=1, source_target_pairs={{8,0},{16,8},{24,16},{28,24},{20,28},{12,20},{4,12},{0,4},{2,10},{... | collective-permute-start | bytes 602120 | tf_op jit(solution)/shard_map/ppermute | solution.py:293
  62.6 9.8 %collective-permute-start.27 = (f32[392,128]{1,0:T(8,128)S(1)}, f32[392,128]{1,0:T(8,128)}, u32[]{:S(2)}, u32[]{:S(2)}) collective-permute-start(f32[392,128]{1,0:T(8,128)S(1)} %add_add_fusion.refs_1_), channel_id=1, source_target_pairs={{0,8},{8,16},{16,24},{24,28},{28,20},{20,12},{12,4},{4,0},{10,2},{... | collective-permute-start | bytes 602120 | tf_op jit(solution)/shard_map/ppermute | solution.py:293
  66.4 8.6 %collective-permute-start.25 = (f32[392,128]{1,0:T(8,128)S(1)}, f32[392,128]{1,0:T(8,128)S(1)}, u32[]{:S(2)}, u32[]{:S(2)}) collective-permute-start(f32[392,128]{1,0:T(8,128)S(1)} %collective-permute-done.24.refs_12_), channel_id=1, source_target_pairs={{0,8},{8,16},{16,24},{24,28},{28,20},{20,12},{12,4},{4,0},{10,2},{... | collective-permute-start | bytes 602120 | tf_op jit(solution)/shard_map/ppermute | solution.py:293
  70.5 8.6 %collective-permute-start.21 = (f32[392,128]{1,0:T(8,128)}, f32[392,128]{1,0:T(8,128)S(1)}, u32[]{:S(2)}, u32[]{:S(2)}) collective-permute-start(f32[392,128]{1,0:T(8,128)} %collective-permute-done.19.refs_3_), channel_id=1, source_target_pairs={{8,0},{16,8},{24,16},{28,24},{20,28},{12,20},{4,12},{0,4},{2,10},{... | collective-permute-start | bytes 602120 | tf_op jit(solution)/shard_map/ppermute | solution.py:293
  72.4 8.3 %collective-permute-start.28 = (f32[392,128]{1,0:T(8,128)}, f32[392,128]{1,0:T(8,128)S(1)}, u32[]{:S(2)}, u32[]{:S(2)}) collective-permute-start(f32[392,128]{1,0:T(8,128)} %collective-permute-done.27.refs_13_), channel_id=1, source_target_pairs={{0,8},{8,16},{16,24},{24,28},{28,20},{20,12},{12,4},{4,0},{10,2},{... | collective-permute-start | bytes 602120 | tf_op jit(solution)/shard_map/ppermute | solution.py:293
  75.0 10.1 %collective-permute-start.26 = (f32[392,128]{1,0:T(8,128)S(1)}, f32[392,128]{1,0:T(8,128)S(1)}, u32[]{:S(2)}, u32[]{:S(2)}) collective-permute-start(f32[392,128]{1,0:T(8,128)S(1)} %collective-permute-done.25.refs_10_), channel_id=1, source_target_pairs={{0,8},{8,16},{16,24},{24,28},{28,20},{20,12},{12,4},{4,0},{10,2},{... | collective-permute-start | bytes 602120 | tf_op jit(solution)/shard_map/ppermute | solution.py:293
  75.6 12.0 %collective-permute-start.22 = (f32[392,128]{1,0:T(8,128)S(1)}, f32[392,128]{1,0:T(8,128)S(1)}, u32[]{:S(2)}, u32[]{:S(2)}) collective-permute-start(f32[392,128]{1,0:T(8,128)S(1)} %collective-permute-done.20.refs_4_), channel_id=1, source_target_pairs={{8,0},{16,8},{24,16},{28,24},{20,28},{12,20},{4,12},{0,4},{2,10},{... | collective-permute-start | bytes 602120 | tf_op jit(solution)/shard_map/ppermute | solution.py:293
  79.1 8.9 %collective-permute-start.23 = (f32[392,128]{1,0:T(8,128)S(1)}, f32[392,128]{1,0:T(8,128)S(1)}, u32[]{:S(2)}, u32[]{:S(2)}) collective-permute-start(f32[392,128]{1,0:T(8,128)S(1)} %collective-permute-done.21.refs_5_), channel_id=1, source_target_pairs={{8,0},{16,8},{24,16},{28,24},{20,28},{12,20},{4,12},{0,4},{2,10},{... | collective-permute-start | bytes 602120 | tf_op jit(solution)/shard_map/ppermute | solution.py:293
  85.1 9.1 %collective-permute-start.30 = (f32[392,128]{1,0:T(8,128)S(1)}, f32[392,128]{1,0:T(8,128)S(1)}, u32[]{:S(2)}, u32[]{:S(2)}) collective-permute-start(f32[392,128]{1,0:T(8,128)S(1)} %collective-permute-done.26.refs_8_), channel_id=1, source_target_pairs={{0,8},{8,16},{16,24},{24,28},{28,20},{20,12},{12,4},{4,0},{10,2},{... | collective-permute-start | bytes 602120 | tf_op jit(solution)/shard_map/ppermute | solution.py:293
  95.2 8.0 %collective-permute-start.35 = (f32[392,128]{1,0:T(8,128)S(1)}, f32[392,128]{1,0:T(8,128)S(1)}, u32[]{:S(2)}, u32[]{:S(2)}) collective-permute-start(f32[392,128]{1,0:T(8,128)S(1)} %convolution_add_fusion.1), channel_id=1, source_target_pairs={{0,8},{8,16},{16,24},{24,28},{28,20},{20,12},{12,4},{4,0},{10,2},{... | collective-permute-start | bytes 602120 | tf_op jit(solution)/shard_map/ppermute | solution.py:293
  97.7 9.2 %collective-permute-start.42 = (f32[392,128]{1,0:T(8,128)S(1)}, f32[392,128]{1,0:T(8,128)S(1)}, u32[]{:S(2)}, u32[]{:S(2)}) collective-permute-start(f32[392,128]{1,0:T(8,128)S(1)} %convolution_add_fusion), channel_id=1, source_target_pairs={{0,8},{8,16},{16,24},{24,28},{28,20},{20,12},{12,4},{4,0},{10,2},{... | collective-permute-start | bytes 602120 | tf_op jit(solution)/shard_map/ppermute | solution.py:293
  99.9 8.1 %collective-permute-start.32 = (f32[392,128]{1,0:T(8,128)S(1)}, f32[392,128]{1,0:T(8,128)S(1)}, u32[]{:S(2)}, u32[]{:S(2)}) collective-permute-start(f32[392,128]{1,0:T(8,128)S(1)} %convolution_add_fusion.1), channel_id=1, source_target_pairs={{8,0},{16,8},{24,16},{28,24},{20,28},{12,20},{4,12},{0,4},{2,10},{... | collective-permute-start | bytes 602120 | tf_op jit(solution)/shard_map/ppermute | solution.py:293
  100.0 9.4 %collective-permute-start.39 = (f32[392,128]{1,0:T(8,128)S(1)}, f32[392,128]{1,0:T(8,128)S(1)}, u32[]{:S(2)}, u32[]{:S(2)}) collective-permute-start(f32[392,128]{1,0:T(8,128)S(1)} %convolution_add_fusion), channel_id=1, source_target_pairs={{8,0},{16,8},{24,16},{28,24},{20,28},{12,20},{4,12},{0,4},{2,10},{... | collective-permute-start | bytes 602120 | tf_op jit(solution)/shard_map/ppermute | solution.py:293
  107.9 32.7 %collective-permute-start.48 = (f32[128,200]{1,0:T(8,128)S(1)}, f32[128,200]{1,0:T(8,128)S(1)}, u32[]{:S(2)}, u32[]{:S(2)}) collective-permute-start(f32[128,200]{1,0:T(8,128)S(1)} %add_multiply_fusion), channel_id=1, source_target_pairs={{0,2},{2,0},{4,6},{6,4},{8,10},{10,8},{12,14},{14,12},{16,18},{18,... | collective-permute-start | bytes 307208 | tf_op jit(solution)/shard_map/ppermute | solution.py:293
  108.0 8.0 %collective-permute-start.33 = (f32[392,128]{1,0:T(8,128)S(1)}, f32[392,128]{1,0:T(8,128)S(1)}, u32[]{:S(2)}, u32[]{:S(2)}) collective-permute-start(f32[392,128]{1,0:T(8,128)S(1)} %collective-permute-done.32), channel_id=1, source_target_pairs={{8,0},{16,8},{24,16},{28,24},{20,28},{12,20},{4,12},{0,4},{2,10},{... | collective-permute-start | bytes 602120 | tf_op jit(solution)/shard_map/ppermute | solution.py:293
  109.4 10.8 %collective-permute-start.40 = (f32[392,128]{1,0:T(8,128)S(1)}, f32[392,128]{1,0:T(8,128)S(1)}, u32[]{:S(2)}, u32[]{:S(2)}) collective-permute-start(f32[392,128]{1,0:T(8,128)S(1)} %collective-permute-done.39), channel_id=1, source_target_pairs={{8,0},{16,8},{24,16},{28,24},{20,28},{12,20},{4,12},{0,4},{2,10},{... | collective-permute-start | bytes 602120 | tf_op jit(solution)/shard_map/ppermute | solution.py:293
  110.7 10.2 %collective-permute-start.37 = (f32[392,128]{1,0:T(8,128)S(1)}, f32[392,128]{1,0:T(8,128)S(1)}, u32[]{:S(2)}, u32[]{:S(2)}) collective-permute-start(f32[392,128]{1,0:T(8,128)S(1)} %collective-permute-done.36), channel_id=1, source_target_pairs={{0,8},{8,16},{16,24},{24,28},{28,20},{20,12},{12,4},{4,0},{10,2},{... | collective-permute-start | bytes 602120 | tf_op jit(solution)/shard_map/ppermute | solution.py:293
  114.1 8.8 %collective-permute-start.44 = (f32[392,128]{1,0:T(8,128)S(1)}, f32[392,128]{1,0:T(8,128)S(1)}, u32[]{:S(2)}, u32[]{:S(2)}) collective-permute-start(f32[392,128]{1,0:T(8,128)S(1)} %collective-permute-done.43), channel_id=1, source_target_pairs={{0,8},{8,16},{16,24},{24,28},{28,20},{20,12},{12,4},{4,0},{10,2},{... | collective-permute-start | bytes 602120 | tf_op jit(solution)/shard_map/ppermute | solution.py:293
  115.9 8.4 %collective-permute-start.34 = (f32[392,128]{1,0:T(8,128)S(1)}, f32[392,128]{1,0:T(8,128)S(1)}, u32[]{:S(2)}, u32[]{:S(2)}) collective-permute-start(f32[392,128]{1,0:T(8,128)S(1)} %collective-permute-done.33), channel_id=1, source_target_pairs={{8,0},{16,8},{24,16},{28,24},{20,28},{12,20},{4,12},{0,4},{2,10},{... | collective-permute-start | bytes 602120 | tf_op jit(solution)/shard_map/ppermute | solution.py:293
  (37 other events, 450.1 us)

commit v5 on v4

--- a/solution.py
+++ b/solution.py
@@ -219,7 +219,7 @@
             left, left_low = split(density[:, pl.ds(start, length)])
             acc[h] += mxu(left, top, nn) + mxu(left_low, top, nn) + mxu(left, low, nn)
 
-    @pl.loop(0, depth // step)
+    @pl.loop(0, depth // step, unroll=True)
     def _(i):
         add(pl.multiple_of(i * step, step), step)
 

time: 159 us -> 158 us (level)
  waiting for transfers between devices: 56.6 us -> 52.5 us
  starting transfers between devices: 62 us -> 66.1 us
    ppermute x50, waiting for transfers between devices: 51.7 us -> 46.5 us  [hop(): return lax.ppermute(x, 'orb', pairs)]
    ppermute x50, starting transfers between devices: 52.5 us -> 56.5 us  [hop(): return lax.ppermute(x, 'orb', pairs)]
where the time goes in v5:
time: 158 us
  starting transfers between devices  66.1 us (42%)
  waiting for transfers between devices  52.5 us (33%)
  Pallas kernels  26.2 us (17%)
  local copies, waits for them, and re-layouts  7.19 us (5%)
  matrix products  2.86 us (2%)
  other arithmetic  2.65 us (2%)
    ppermute x50, starting transfers between devices, hop(): return lax.ppermute(x, 'orb', pairs)  56.5 us
    ppermute x50, waiting for transfers between devices, hop(): return lax.ppermute(x, 'orb', pairs)  46.5 us
    pallas_call x2, Pallas kernels, extract(): pl.pallas_call(functools.partial(extract_body, nb, parts), out_shape=out_...  12.5 us
    pallas_call x1, Pallas kernels, q_partial(): pl.pallas_call(functools.partial(q_body, nb, count), out_shape=jax.ShapeD...  9.97 us
    ppermute x7, starting transfers between devices, across(): return lax.ppermute(x, ('orb', 'aux'), table)  9.53 us
    unnamed x24, local copies, waits for them, and re-layouts  6.52 us
    ppermute x7, waiting for transfers between devices, across(): return lax.ppermute(x, ('orb', 'aux'), table)  6.02 us
    pallas_call x1, Pallas kernels, half_partial(): pl.pallas_call(functools.partial(half_body, chips), out_shape=[jax.ShapeD...  3.69 us
  transfers between devices with their start and end apart: 57, of which 35 were waited for; matrix products, arithmetic and copies ran while one was open for 3% of the time, Pallas kernels for 17%

profile of v5, /device:TPU:0, one launch (start us, length us, event | category | flops | bytes accessed | tf_op | source)
XLA Modules:
  0.0 157.9 jit_solution(6384651870982292676)
XLA Ops:
  1.9 7.0 %extract.2 = (f32[56,56,128]{2,1,0:T(8,128)S(1)}, f32[56,56,128]{2,1,0:T(8,128)S(1)}, f32[56,256,128]{2,1,0:T(8,128)}) custom-call(s32[11]{0:T(128)S(1)} %add_add_fusion.4.info, s32[56]{0:T(128)S(1)} %copy-done.6, f32[56,512,128]{2,1,0:T(8,128)} %three.5, s32[8,32]{1,0:T(8,128)S(1)} %bitcast.87), custom_call_target="tpu_custom_call" | custom-call | flops 411041792 | bytes 17891328 | tf_op jit(solution)/shard_map/extract/pallas_call | solution.py:109
  9.6 5.5 %extract.3 = (f32[56,56,128]{2,1,0:T(8,128)S(1)}, f32[56,56,128]{2,1,0:T(8,128)S(1)}) custom-call(s32[11]{0:T(128)S(1)} %add_add_fusion.5.info, s32[56]{0:T(128)S(1)} %copy-done.6, f32[56,512,128]{2,1,0:T(8,128)} %three.5, s32[8,32]{1,0:T(8,128)S(1)} %bitcast.88), custom_call_target="tpu_custom_call" | custom-call | flops 411041792 | bytes 10551296 | tf_op jit(solution)/shard_map/extract/pallas_call | solution.py:109
  15.9 2.4 %slice-done = s8[4194304]{0:T(1024)(128)(4,1)S(1)} async-done(((s8[7340032]{0:T(1024)(128)(4,1)}), s8[4194304]{0:T(1024)(128)(4,1)S(1)}, s32[]{:S(2)}) %slice-start) | async-done | bytes 4194328
  19.9 3.0 %collective-permute-start.3 = (f32[392,128]{1,0:T(8,128)S(1)}, f32[392,128]{1,0:T(8,128)S(1)}, u32[]{:S(2)}, u32[]{:S(2)}) collective-permute-start(f32[392,128]{1,0:T(8,128)S(1)} %get-tuple-element.53), channel_id=1, source_target_pairs={{0,8},{8,16},{16,24},{24,28},{28,20},{20,12},{12,4},{4,0},{10,2},{... | collective-permute-start | bytes 602120 | tf_op jit(solution)/shard_map/ppermute | solution.py:293
  22.9 2.0 %collective-permute-start.5 = (f32[392,128]{1,0:T(8,128)S(1)}, f32[392,128]{1,0:T(8,128)S(1)}, u32[]{:S(2)}, u32[]{:S(2)}) collective-permute-start(f32[392,128]{1,0:T(8,128)S(1)} %get-tuple-element.55), channel_id=1, source_target_pairs={{0,8},{8,16},{16,24},{24,28},{28,20},{20,12},{12,4},{4,0},{10,2},{... | collective-permute-start | bytes 602120 | tf_op jit(solution)/shard_map/ppermute | solution.py:293
  24.9 3.3 %collective-permute-done.3 = f32[392,128]{1,0:T(8,128)S(1)} collective-permute-done((f32[392,128]{1,0:T(8,128)S(1)}, f32[392,128]{1,0:T(8,128)S(1)}, u32[]{:S(2)}, u32[]{:S(2)}) %collective-permute-start.3) | collective-permute-done | bytes 200736 | tf_op jit(solution)/shard_map/ppermute | solution.py:293
  32.4 2.0 %collective-permute-start.8 = (f32[392,128]{1,0:T(8,128)S(1)}, f32[392,128]{1,0:T(8,128)S(1)}, u32[]{:S(2)}, u32[]{:S(2)}) collective-permute-start(f32[392,128]{1,0:T(8,128)S(1)} %add.232), channel_id=1, source_target_pairs={{0,8},{8,16},{16,24},{24,28},{28,20},{20,12},{12,4},{4,0},{10,2},{... | collective-permute-start | bytes 602120 | tf_op jit(solution)/shard_map/ppermute | solution.py:293
  38.5 2.8 %collective-permute-start.9 = (f32[392,128]{1,0:T(8,128)S(1)}, f32[392,128]{1,0:T(8,128)S(1)}, u32[]{:S(2)}, u32[]{:S(2)}) collective-permute-start(f32[392,128]{1,0:T(8,128)S(1)} %add.233), channel_id=1, source_target_pairs={{0,8},{8,16},{16,24},{24,28},{28,20},{20,12},{12,4},{4,0},{10,2},{... | collective-permute-start | bytes 602120 | tf_op jit(solution)/shard_map/ppermute | solution.py:293
  42.8 2.5 %collective-permute-start.14 = (f32[392,128]{1,0:T(8,128)S(1)}, f32[392,128]{1,0:T(8,128)S(1)}, u32[]{:S(2)}, u32[]{:S(2)}) collective-permute-start(f32[392,128]{1,0:T(8,128)S(1)} %add.240), channel_id=1, source_target_pairs={{0,8},{8,16},{16,24},{24,28},{28,20},{20,12},{12,4},{4,0},{10,2},{... | collective-permute-start | bytes 602120 | tf_op jit(solution)/shard_map/ppermute | solution.py:293
  47.1 2.5 %collective-permute-start.10 = (f32[392,128]{1,0:T(8,128)S(1)}, f32[392,128]{1,0:T(8,128)S(1)}, u32[]{:S(2)}, u32[]{:S(2)}) collective-permute-start(f32[392,128]{1,0:T(8,128)S(1)} %add.234), channel_id=1, source_target_pairs={{0,8},{8,16},{16,24},{24,28},{28,20},{20,12},{12,4},{4,0},{10,2},{... | collective-permute-start | bytes 602120 | tf_op jit(solution)/shard_map/ppermute | solution.py:293
  51.4 2.5 %collective-permute-start.15 = (f32[392,128]{1,0:T(8,128)S(1)}, f32[392,128]{1,0:T(8,128)S(1)}, u32[]{:S(2)}, u32[]{:S(2)}) collective-permute-start(f32[392,128]{1,0:T(8,128)S(1)} %add.241), channel_id=1, source_target_pairs={{0,8},{8,16},{16,24},{24,28},{28,20},{20,12},{12,4},{4,0},{10,2},{... | collective-permute-start | bytes 602120 | tf_op jit(solution)/shard_map/ppermute | solution.py:293
  55.1 2.1 %collective-permute-done.17 = f32[392,128]{1,0:T(8,128)S(1)} collective-permute-done((f32[392,128]{1,0:T(8,128)S(1)}, f32[392,128]{1,0:T(8,128)S(1)}, u32[]{:S(2)}, u32[]{:S(2)}) %collective-permute-start.17) | collective-permute-done | bytes 200736 | tf_op jit(solution)/shard_map/ppermute | solution.py:293
  57.6 2.1 %collective-permute-start.24 = (f32[392,128]{1,0:T(8,128)S(1)}, f32[392,128]{1,0:T(8,128)S(1)}, u32[]{:S(2)}, u32[]{:S(2)}) collective-permute-start(f32[392,128]{1,0:T(8,128)S(1)} %add_add_fusion.1.refs_0_), channel_id=1, source_target_pairs={{0,8},{8,16},{16,24},{24,28},{28,20},{20,12},{12,4},{4,0},{10,2},{... | collective-permute-start | bytes 602120 | tf_op jit(solution)/shard_map/ppermute | solution.py:293
  60.0 2.0 %collective-permute-start.19 = (f32[392,128]{1,0:T(8,128)S(1)}, f32[392,128]{1,0:T(8,128)}, u32[]{:S(2)}, u32[]{:S(2)}) collective-permute-start(f32[392,128]{1,0:T(8,128)S(1)} %add_add_fusion.refs_1_), channel_id=1, source_target_pairs={{8,0},{16,8},{24,16},{28,24},{20,28},{12,20},{4,12},{0,4},{2,10},{... | collective-permute-start | bytes 602120 | tf_op jit(solution)/shard_map/ppermute | solution.py:293
  62.0 3.5 %collective-permute-done.24.refs_12_ = f32[392,128]{1,0:T(8,128)S(1)} collective-permute-done((f32[392,128]{1,0:T(8,128)S(1)}, f32[392,128]{1,0:T(8,128)S(1)}, u32[]{:S(2)}, u32[]{:S(2)}) %collective-permute-start.24) | collective-permute-done | bytes 200736 | tf_op jit(solution)/shard_map/ppermute | solution.py:293
  65.6 2.1 %collective-permute-start.25 = (f32[392,128]{1,0:T(8,128)S(1)}, f32[392,128]{1,0:T(8,128)S(1)}, u32[]{:S(2)}, u32[]{:S(2)}) collective-permute-start(f32[392,128]{1,0:T(8,128)S(1)} %collective-permute-done.24.refs_12_), channel_id=1, source_target_pairs={{0,8},{8,16},{16,24},{24,28},{28,20},{20,12},{12,4},{4,0},{10,2},{... | collective-permute-start | bytes 602120 | tf_op jit(solution)/shard_map/ppermute | solution.py:293
  67.9 2.2 %collective-permute-done.19.refs_3_ = f32[392,128]{1,0:T(8,128)} collective-permute-done((f32[392,128]{1,0:T(8,128)S(1)}, f32[392,128]{1,0:T(8,128)}, u32[]{:S(2)}, u32[]{:S(2)}) %collective-permute-start.19) | collective-permute-done | bytes 200736 | tf_op jit(solution)/shard_map/ppermute | solution.py:293
  70.2 2.2 %collective-permute-start.21 = (f32[392,128]{1,0:T(8,128)}, f32[392,128]{1,0:T(8,128)S(1)}, u32[]{:S(2)}, u32[]{:S(2)}) collective-permute-start(f32[392,128]{1,0:T(8,128)} %collective-permute-done.19.refs_3_), channel_id=1, source_target_pairs={{8,0},{16,8},{24,16},{28,24},{20,28},{12,20},{4,12},{0,4},{2,10},{... | collective-permute-start | bytes 602120 | tf_op jit(solution)/shard_map/ppermute | solution.py:293
  76.5 3.6 %collective-permute-done.21.refs_5_ = f32[392,128]{1,0:T(8,128)S(1)} collective-permute-done((f32[392,128]{1,0:T(8,128)}, f32[392,128]{1,0:T(8,128)S(1)}, u32[]{:S(2)}, u32[]{:S(2)}) %collective-permute-start.21) | collective-permute-done | bytes 200736 | tf_op jit(solution)/shard_map/ppermute | solution.py:293
  80.4 2.0 %collective-permute-start.29 = (f32[392,128]{1,0:T(8,128)S(1)}, f32[392,128]{1,0:T(8,128)S(1)}, u32[]{:S(2)}, u32[]{:S(2)}) collective-permute-start(f32[392,128]{1,0:T(8,128)S(1)} %collective-permute-done.28.refs_11_), channel_id=1, source_target_pairs={{0,8},{8,16},{16,24},{24,28},{28,20},{20,12},{12,4},{4,0},{10,2},{... | collective-permute-start | bytes 602120 | tf_op jit(solution)/shard_map/ppermute | solution.py:293
  82.5 1.9 %collective-permute-done.26.refs_8_ = f32[392,128]{1,0:T(8,128)S(1)} collective-permute-done((f32[392,128]{1,0:T(8,128)S(1)}, f32[392,128]{1,0:T(8,128)S(1)}, u32[]{:S(2)}, u32[]{:S(2)}) %collective-permute-start.26) | collective-permute-done | bytes 200736 | tf_op jit(solution)/shard_map/ppermute | solution.py:293
  90.4 3.7 %half.1 = (f32[392,128]{1,0:T(8,128)S(1)}, f32[392,128]{1,0:T(8,128)S(1)}) custom-call(s32[11]{0:T(128)S(1)} %add_add_fusion.5.info, f32[196,3136]{1,0:T(8,128)S(1)} %copy-done.1, f32[196,3136]{1,0:T(8,128)S(1)} %copy-done.3, f32[392,128]{1,0:T(8,128)S(1)} %add_add_fusion.1.refs_0_, f32[392,128]{1,0:T(8,128)S(1)} %add_add_fusion.refs_1_, ...), custom_call_target="tpu_custom_call" | custom-call | flops 1888223232 | bytes 8128512 | tf_op jit(solution)/shard_map/half/pallas_call | solution.py:243
  95.1 2.4 %collective-permute-start.35 = (f32[392,128]{1,0:T(8,128)S(1)}, f32[392,128]{1,0:T(8,128)S(1)}, u32[]{:S(2)}, u32[]{:S(2)}) collective-permute-start(f32[392,128]{1,0:T(8,128)S(1)} %convolution_add_fusion.1), channel_id=1, source_target_pairs={{0,8},{8,16},{16,24},{24,28},{28,20},{20,12},{12,4},{4,0},{10,2},{... | collective-permute-start | bytes 602120 | tf_op jit(solution)/shard_map/ppermute | solution.py:293
  99.9 3.2 %collective-permute-done.35 = f32[392,128]{1,0:T(8,128)S(1)} collective-permute-done((f32[392,128]{1,0:T(8,128)S(1)}, f32[392,128]{1,0:T(8,128)S(1)}, u32[]{:S(2)}, u32[]{:S(2)}) %collective-permute-start.35) | collective-permute-done | bytes 200736 | tf_op jit(solution)/shard_map/ppermute | solution.py:293
  103.1 2.2 %collective-permute-start.36 = (f32[392,128]{1,0:T(8,128)S(1)}, f32[392,128]{1,0:T(8,128)S(1)}, u32[]{:S(2)}, u32[]{:S(2)}) collective-permute-start(f32[392,128]{1,0:T(8,128)S(1)} %collective-permute-done.35), channel_id=1, source_target_pairs={{0,8},{8,16},{16,24},{24,28},{28,20},{20,12},{12,4},{4,0},{10,2},{... | collective-permute-start | bytes 602120 | tf_op jit(solution)/shard_map/ppermute | solution.py:293
  112.6 2.5 %collective-permute-start.44 = (f32[392,128]{1,0:T(8,128)S(1)}, f32[392,128]{1,0:T(8,128)S(1)}, u32[]{:S(2)}, u32[]{:S(2)}) collective-permute-start(f32[392,128]{1,0:T(8,128)S(1)} %collective-permute-done.43), channel_id=1, source_target_pairs={{0,8},{8,16},{16,24},{24,28},{28,20},{20,12},{12,4},{4,0},{10,2},{... | collective-permute-start | bytes 602120 | tf_op jit(solution)/shard_map/ppermute | solution.py:293
  115.8 3.9 %collective-permute-done.40 = f32[392,128]{1,0:T(8,128)S(1)} collective-permute-done((f32[392,128]{1,0:T(8,128)S(1)}, f32[392,128]{1,0:T(8,128)S(1)}, u32[]{:S(2)}, u32[]{:S(2)}) %collective-permute-start.40) | collective-permute-done | bytes 200736 | tf_op jit(solution)/shard_map/ppermute | solution.py:293
  119.7 2.0 %collective-permute-start.38 = (f32[392,128]{1,0:T(8,128)S(1)}, f32[392,128]{1,0:T(8,128)S(1)}, u32[]{:S(2)}, u32[]{:S(2)}) collective-permute-start(f32[392,128]{1,0:T(8,128)S(1)} %collective-permute-done.37), channel_id=1, source_target_pairs={{0,8},{8,16},{16,24},{24,28},{28,20},{20,12},{12,4},{4,0},{10,2},{... | collective-permute-start | bytes 602120 | tf_op jit(solution)/shard_map/ppermute | solution.py:293
  123.8 3.7 %collective-permute-done.41 = f32[392,128]{1,0:T(8,128)S(1)} collective-permute-done((f32[392,128]{1,0:T(8,128)S(1)}, f32[392,128]{1,0:T(8,128)S(1)}, u32[]{:S(2)}, u32[]{:S(2)}) %collective-permute-start.41) | collective-permute-done | bytes 200736 | tf_op jit(solution)/shard_map/ppermute | solution.py:293
  128.8 10.0 %qpartial.1 = f32[64,256]{1,0:T(8,128)S(1)} custom-call(s32[11]{0:T(128)S(1)} %add_add_fusion.5.info, f32[56,512,128]{2,1,0:T(8,128)} %three.5, s32[8,32]{1,0:T(8,128)S(1)} %bitcast.89, f32[56,256,128]{2,1,0:T(8,128)} %collective-permute-done.7.sib, f32[7,56,128]{2,1,0:T(8,128)S(1)} %bitcast.70, f32[7,56,128]{2,1,0:T(8,128)S(1)} %bitcast.75, ...), custom_call_target="tpu_custom_call" | custom-call | flops 1233125376 | bytes 17891328 | tf_op jit(solution)/shard_map/qpartial/pallas_call | solution.py:176
  140.8 2.7 %collective-permute-start.52 = (f32[112,128]{1,0:T(8,128)S(1)}, f32[112,128]{1,0:T(8,128)S(1)}, u32[]{:S(2)}, u32[]{:S(2)}) collective-permute-start(f32[112,128]{1,0:T(8,128)S(1)} %add.264), channel_id=1, source_target_pairs={{0,5},{1,4},{2,7},{3,6},{4,1},{5,0},{6,3},{7,2},{8,13},{9,12},{10,... | collective-permute-start | bytes 172040 | tf_op jit(solution)/shard_map/ppermute | solution.py:359
  150.7 2.0 %collective-permute-start.53 = (f32[112,128]{1,0:T(8,128)S(1)}, f32[112,128]{1,0:T(8,128)S(1)}, u32[]{:S(2)}, u32[]{:S(2)}) collective-permute-start(f32[112,128]{1,0:T(8,128)S(1)} %add_add_fusion.3), channel_id=1, source_target_pairs={{0,8},{1,9},{2,10},{3,11},{4,12},{5,13},{6,14},{7,15},{8,0},{9,1},... | collective-permute-start | bytes 172040 | tf_op jit(solution)/shard_map/ppermute | solution.py:359
  (165 shorter events, 59.7 us)
Async XLA Ops:
  0.0 15.8 %collective-permute-start.2 = (f32[196,3136]{1,0:T(8,128)}, f32[196,3136]{1,0:T(8,128)S(1)}, u32[]{:S(2)}, u32[]{:S(2)}) collective-permute-start(f32[196,3136]{1,0:T(8,128)} %own.1), channel_id=1, source_target_pairs={{0,2},{2,0},{4,6},{6,4},{8,10},{10,8},{12,14},{14,12},{16,18},{18,... | collective-permute-start | bytes 7375880 | tf_op jit(solution)/shard_map/ppermute | solution.py:293
  19.3 13.1 %collective-permute-start.7 = (f32[56,256,128]{2,1,0:T(8,128)S(1)}, f32[56,256,128]{2,1,0:T(8,128)}, u32[]{:S(2)}, u32[]{:S(2)}) collective-permute-start(f32[56,256,128]{2,1,0:T(8,128)S(1)} %bitcast.93), channel_id=1, source_target_pairs={{0,2},{2,0},{4,6},{6,4},{8,10},{10,8},{12,14},{14,12},{16,18},{18,... | collective-permute-start | bytes 22020104 | tf_op jit(solution)/shard_map/ppermute | solution.py:293
  19.9 8.4 %collective-permute-start.3 = (f32[392,128]{1,0:T(8,128)S(1)}, f32[392,128]{1,0:T(8,128)S(1)}, u32[]{:S(2)}, u32[]{:S(2)}) collective-permute-start(f32[392,128]{1,0:T(8,128)S(1)} %get-tuple-element.53), channel_id=1, source_target_pairs={{0,8},{8,16},{16,24},{24,28},{28,20},{20,12},{12,4},{4,0},{10,2},{... | collective-permute-start | bytes 602120 | tf_op jit(solution)/shard_map/ppermute | solution.py:293
  22.9 8.8 %collective-permute-start.5 = (f32[392,128]{1,0:T(8,128)S(1)}, f32[392,128]{1,0:T(8,128)S(1)}, u32[]{:S(2)}, u32[]{:S(2)}) collective-permute-start(f32[392,128]{1,0:T(8,128)S(1)} %get-tuple-element.55), channel_id=1, source_target_pairs={{0,8},{8,16},{16,24},{24,28},{28,20},{20,12},{12,4},{4,0},{10,2},{... | collective-permute-start | bytes 602120 | tf_op jit(solution)/shard_map/ppermute | solution.py:293
  34.4 8.3 %collective-permute-start.13 = (f32[392,128]{1,0:T(8,128)S(1)}, f32[392,128]{1,0:T(8,128)S(1)}, u32[]{:S(2)}, u32[]{:S(2)}) collective-permute-start(f32[392,128]{1,0:T(8,128)S(1)} %add.239), channel_id=1, source_target_pairs={{0,8},{8,16},{16,24},{24,28},{28,20},{20,12},{12,4},{4,0},{10,2},{... | collective-permute-start | bytes 602120 | tf_op jit(solution)/shard_map/ppermute | solution.py:293
  36.1 9.2 %collective-permute-start.11 = (f32[392,128]{1,0:T(8,128)S(1)}, f32[392,128]{1,0:T(8,128)S(1)}, u32[]{:S(2)}, u32[]{:S(2)}) collective-permute-start(f32[392,128]{1,0:T(8,128)S(1)} %add.236), channel_id=1, source_target_pairs={{8,0},{16,8},{24,16},{28,24},{20,28},{12,20},{4,12},{0,4},{2,10},{... | collective-permute-start | bytes 602120 | tf_op jit(solution)/shard_map/ppermute | solution.py:293
  38.5 8.6 %collective-permute-start.9 = (f32[392,128]{1,0:T(8,128)S(1)}, f32[392,128]{1,0:T(8,128)S(1)}, u32[]{:S(2)}, u32[]{:S(2)}) collective-permute-start(f32[392,128]{1,0:T(8,128)S(1)} %add.233), channel_id=1, source_target_pairs={{0,8},{8,16},{16,24},{24,28},{28,20},{20,12},{12,4},{4,0},{10,2},{... | collective-permute-start | bytes 602120 | tf_op jit(solution)/shard_map/ppermute | solution.py:293
  41.2 8.4 %collective-permute-start.16 = (f32[392,128]{1,0:T(8,128)S(1)}, f32[392,128]{1,0:T(8,128)S(1)}, u32[]{:S(2)}, u32[]{:S(2)}) collective-permute-start(f32[392,128]{1,0:T(8,128)S(1)} %add.243), channel_id=1, source_target_pairs={{8,0},{16,8},{24,16},{28,24},{20,28},{12,20},{4,12},{0,4},{2,10},{... | collective-permute-start | bytes 602120 | tf_op jit(solution)/shard_map/ppermute | solution.py:293
  42.8 8.6 %collective-permute-start.14 = (f32[392,128]{1,0:T(8,128)S(1)}, f32[392,128]{1,0:T(8,128)S(1)}, u32[]{:S(2)}, u32[]{:S(2)}) collective-permute-start(f32[392,128]{1,0:T(8,128)S(1)} %add.240), channel_id=1, source_target_pairs={{0,8},{8,16},{16,24},{24,28},{28,20},{20,12},{12,4},{4,0},{10,2},{... | collective-permute-start | bytes 602120 | tf_op jit(solution)/shard_map/ppermute | solution.py:293
  45.4 8.6 %collective-permute-start.12 = (f32[392,128]{1,0:T(8,128)S(1)}, f32[392,128]{1,0:T(8,128)S(1)}, u32[]{:S(2)}, u32[]{:S(2)}) collective-permute-start(f32[392,128]{1,0:T(8,128)S(1)} %add.237), channel_id=1, source_target_pairs={{8,0},{16,8},{24,16},{28,24},{20,28},{12,20},{4,12},{0,4},{2,10},{... | collective-permute-start | bytes 602120 | tf_op jit(solution)/shard_map/ppermute | solution.py:293
  47.1 8.0 %collective-permute-start.10 = (f32[392,128]{1,0:T(8,128)S(1)}, f32[392,128]{1,0:T(8,128)S(1)}, u32[]{:S(2)}, u32[]{:S(2)}) collective-permute-start(f32[392,128]{1,0:T(8,128)S(1)} %add.234), channel_id=1, source_target_pairs={{0,8},{8,16},{16,24},{24,28},{28,20},{20,12},{12,4},{4,0},{10,2},{... | collective-permute-start | bytes 602120 | tf_op jit(solution)/shard_map/ppermute | solution.py:293
  57.6 8.0 %collective-permute-start.24 = (f32[392,128]{1,0:T(8,128)S(1)}, f32[392,128]{1,0:T(8,128)S(1)}, u32[]{:S(2)}, u32[]{:S(2)}) collective-permute-start(f32[392,128]{1,0:T(8,128)S(1)} %add_add_fusion.1.refs_0_), channel_id=1, source_target_pairs={{0,8},{8,16},{16,24},{24,28},{28,20},{20,12},{12,4},{4,0},{10,2},{... | collective-permute-start | bytes 602120 | tf_op jit(solution)/shard_map/ppermute | solution.py:293
  59.7 7.9 %collective-permute-start.18 = (f32[392,128]{1,0:T(8,128)S(1)}, f32[392,128]{1,0:T(8,128)S(1)}, u32[]{:S(2)}, u32[]{:S(2)}) collective-permute-start(f32[392,128]{1,0:T(8,128)S(1)} %add_add_fusion.1.refs_0_), channel_id=1, source_target_pairs={{8,0},{16,8},{24,16},{28,24},{20,28},{12,20},{4,12},{0,4},{2,10},{... | collective-permute-start | bytes 602120 | tf_op jit(solution)/shard_map/ppermute | solution.py:293
  60.0 10.2 %collective-permute-start.19 = (f32[392,128]{1,0:T(8,128)S(1)}, f32[392,128]{1,0:T(8,128)}, u32[]{:S(2)}, u32[]{:S(2)}) collective-permute-start(f32[392,128]{1,0:T(8,128)S(1)} %add_add_fusion.refs_1_), channel_id=1, source_target_pairs={{8,0},{16,8},{24,16},{28,24},{20,28},{12,20},{4,12},{0,4},{2,10},{... | collective-permute-start | bytes 602120 | tf_op jit(solution)/shard_map/ppermute | solution.py:293
  62.0 10.3 %collective-permute-start.27 = (f32[392,128]{1,0:T(8,128)S(1)}, f32[392,128]{1,0:T(8,128)}, u32[]{:S(2)}, u32[]{:S(2)}) collective-permute-start(f32[392,128]{1,0:T(8,128)S(1)} %add_add_fusion.refs_1_), channel_id=1, source_target_pairs={{0,8},{8,16},{16,24},{24,28},{28,20},{20,12},{12,4},{4,0},{10,2},{... | collective-permute-start | bytes 602120 | tf_op jit(solution)/shard_map/ppermute | solution.py:293
  65.6 8.7 %collective-permute-start.25 = (f32[392,128]{1,0:T(8,128)S(1)}, f32[392,128]{1,0:T(8,128)S(1)}, u32[]{:S(2)}, u32[]{:S(2)}) collective-permute-start(f32[392,128]{1,0:T(8,128)S(1)} %collective-permute-done.24.refs_12_), channel_id=1, source_target_pairs={{0,8},{8,16},{16,24},{24,28},{28,20},{20,12},{12,4},{4,0},{10,2},{... | collective-permute-start | bytes 602120 | tf_op jit(solution)/shard_map/ppermute | solution.py:293
  67.6 8.5 %collective-permute-start.20 = (f32[392,128]{1,0:T(8,128)S(1)}, f32[392,128]{1,0:T(8,128)S(1)}, u32[]{:S(2)}, u32[]{:S(2)}) collective-permute-start(f32[392,128]{1,0:T(8,128)S(1)} %collective-permute-done.18.refs_2_), channel_id=1, source_target_pairs={{8,0},{16,8},{24,16},{28,24},{20,28},{12,20},{4,12},{0,4},{2,10},{... | collective-permute-start | bytes 602120 | tf_op jit(solution)/shard_map/ppermute | solution.py:293
  70.2 9.9 %collective-permute-start.21 = (f32[392,128]{1,0:T(8,128)}, f32[392,128]{1,0:T(8,128)S(1)}, u32[]{:S(2)}, u32[]{:S(2)}) collective-permute-start(f32[392,128]{1,0:T(8,128)} %collective-permute-done.19.refs_3_), channel_id=1, source_target_pairs={{8,0},{16,8},{24,16},{28,24},{20,28},{12,20},{4,12},{0,4},{2,10},{... | collective-permute-start | bytes 602120 | tf_op jit(solution)/shard_map/ppermute | solution.py:293
  72.3 8.1 %collective-permute-start.28 = (f32[392,128]{1,0:T(8,128)}, f32[392,128]{1,0:T(8,128)S(1)}, u32[]{:S(2)}, u32[]{:S(2)}) collective-permute-start(f32[392,128]{1,0:T(8,128)} %collective-permute-done.27.refs_13_), channel_id=1, source_target_pairs={{0,8},{8,16},{16,24},{24,28},{28,20},{20,12},{12,4},{4,0},{10,2},{... | collective-permute-start | bytes 602120 | tf_op jit(solution)/shard_map/ppermute | solution.py:293
  74.3 10.2 %collective-permute-start.26 = (f32[392,128]{1,0:T(8,128)S(1)}, f32[392,128]{1,0:T(8,128)S(1)}, u32[]{:S(2)}, u32[]{:S(2)}) collective-permute-start(f32[392,128]{1,0:T(8,128)S(1)} %collective-permute-done.25.refs_10_), channel_id=1, source_target_pairs={{0,8},{8,16},{16,24},{24,28},{28,20},{20,12},{12,4},{4,0},{10,2},{... | collective-permute-start | bytes 602120 | tf_op jit(solution)/shard_map/ppermute | solution.py:293
  76.2 12.0 %collective-permute-start.22 = (f32[392,128]{1,0:T(8,128)S(1)}, f32[392,128]{1,0:T(8,128)S(1)}, u32[]{:S(2)}, u32[]{:S(2)}) collective-permute-start(f32[392,128]{1,0:T(8,128)S(1)} %collective-permute-done.20.refs_4_), channel_id=1, source_target_pairs={{8,0},{16,8},{24,16},{28,24},{20,28},{12,20},{4,12},{0,4},{2,10},{... | collective-permute-start | bytes 602120 | tf_op jit(solution)/shard_map/ppermute | solution.py:293
  80.1 8.6 %collective-permute-start.23 = (f32[392,128]{1,0:T(8,128)S(1)}, f32[392,128]{1,0:T(8,128)S(1)}, u32[]{:S(2)}, u32[]{:S(2)}) collective-permute-start(f32[392,128]{1,0:T(8,128)S(1)} %collective-permute-done.21.refs_5_), channel_id=1, source_target_pairs={{8,0},{16,8},{24,16},{28,24},{20,28},{12,20},{4,12},{0,4},{2,10},{... | collective-permute-start | bytes 602120 | tf_op jit(solution)/shard_map/ppermute | solution.py:293
  84.4 9.7 %collective-permute-start.30 = (f32[392,128]{1,0:T(8,128)S(1)}, f32[392,128]{1,0:T(8,128)S(1)}, u32[]{:S(2)}, u32[]{:S(2)}) collective-permute-start(f32[392,128]{1,0:T(8,128)S(1)} %collective-permute-done.26.refs_8_), channel_id=1, source_target_pairs={{0,8},{8,16},{16,24},{24,28},{28,20},{20,12},{12,4},{4,0},{10,2},{... | collective-permute-start | bytes 602120 | tf_op jit(solution)/shard_map/ppermute | solution.py:293
  95.1 8.0 %collective-permute-start.35 = (f32[392,128]{1,0:T(8,128)S(1)}, f32[392,128]{1,0:T(8,128)S(1)}, u32[]{:S(2)}, u32[]{:S(2)}) collective-permute-start(f32[392,128]{1,0:T(8,128)S(1)} %convolution_add_fusion.1), channel_id=1, source_target_pairs={{0,8},{8,16},{16,24},{24,28},{28,20},{20,12},{12,4},{4,0},{10,2},{... | collective-permute-start | bytes 602120 | tf_op jit(solution)/shard_map/ppermute | solution.py:293
  97.6 8.3 %collective-permute-start.42 = (f32[392,128]{1,0:T(8,128)S(1)}, f32[392,128]{1,0:T(8,128)S(1)}, u32[]{:S(2)}, u32[]{:S(2)}) collective-permute-start(f32[392,128]{1,0:T(8,128)S(1)} %convolution_add_fusion), channel_id=1, source_target_pairs={{0,8},{8,16},{16,24},{24,28},{28,20},{20,12},{12,4},{4,0},{10,2},{... | collective-permute-start | bytes 602120 | tf_op jit(solution)/shard_map/ppermute | solution.py:293
  99.3 8.3 %collective-permute-start.32 = (f32[392,128]{1,0:T(8,128)S(1)}, f32[392,128]{1,0:T(8,128)S(1)}, u32[]{:S(2)}, u32[]{:S(2)}) collective-permute-start(f32[392,128]{1,0:T(8,128)S(1)} %convolution_add_fusion.1), channel_id=1, source_target_pairs={{8,0},{16,8},{24,16},{28,24},{20,28},{12,20},{4,12},{0,4},{2,10},{... | collective-permute-start | bytes 602120 | tf_op jit(solution)/shard_map/ppermute | solution.py:293
  99.9 9.3 %collective-permute-start.39 = (f32[392,128]{1,0:T(8,128)S(1)}, f32[392,128]{1,0:T(8,128)S(1)}, u32[]{:S(2)}, u32[]{:S(2)}) collective-permute-start(f32[392,128]{1,0:T(8,128)S(1)} %convolution_add_fusion), channel_id=1, source_target_pairs={{8,0},{16,8},{24,16},{28,24},{20,28},{12,20},{4,12},{0,4},{2,10},{... | collective-permute-start | bytes 602120 | tf_op jit(solution)/shard_map/ppermute | solution.py:293
  107.5 32.2 %collective-permute-start.48 = (f32[128,200]{1,0:T(8,128)S(1)}, f32[128,200]{1,0:T(8,128)S(1)}, u32[]{:S(2)}, u32[]{:S(2)}) collective-permute-start(f32[128,200]{1,0:T(8,128)S(1)} %add_multiply_fusion), channel_id=1, source_target_pairs={{0,2},{2,0},{4,6},{6,4},{8,10},{10,8},{12,14},{14,12},{16,18},{18,... | collective-permute-start | bytes 307208 | tf_op jit(solution)/shard_map/ppermute | solution.py:293
  109.2 10.5 %collective-permute-start.40 = (f32[392,128]{1,0:T(8,128)S(1)}, f32[392,128]{1,0:T(8,128)S(1)}, u32[]{:S(2)}, u32[]{:S(2)}) collective-permute-start(f32[392,128]{1,0:T(8,128)S(1)} %collective-permute-done.39), channel_id=1, source_target_pairs={{8,0},{16,8},{24,16},{28,24},{20,28},{12,20},{4,12},{0,4},{2,10},{... | collective-permute-start | bytes 602120 | tf_op jit(solution)/shard_map/ppermute | solution.py:293
  110.3 9.4 %collective-permute-start.37 = (f32[392,128]{1,0:T(8,128)S(1)}, f32[392,128]{1,0:T(8,128)S(1)}, u32[]{:S(2)}, u32[]{:S(2)}) collective-permute-start(f32[392,128]{1,0:T(8,128)S(1)} %collective-permute-done.36), channel_id=1, source_target_pairs={{0,8},{8,16},{16,24},{24,28},{28,20},{20,12},{12,4},{4,0},{10,2},{... | collective-permute-start | bytes 602120 | tf_op jit(solution)/shard_map/ppermute | solution.py:293
  112.6 9.9 %collective-permute-start.44 = (f32[392,128]{1,0:T(8,128)S(1)}, f32[392,128]{1,0:T(8,128)S(1)}, u32[]{:S(2)}, u32[]{:S(2)}) collective-permute-start(f32[392,128]{1,0:T(8,128)S(1)} %collective-permute-done.43), channel_id=1, source_target_pairs={{0,8},{8,16},{16,24},{24,28},{28,20},{20,12},{12,4},{4,0},{10,2},{... | collective-permute-start | bytes 602120 | tf_op jit(solution)/shard_map/ppermute | solution.py:293
  115.5 8.2 %collective-permute-start.34 = (f32[392,128]{1,0:T(8,128)S(1)}, f32[392,128]{1,0:T(8,128)S(1)}, u32[]{:S(2)}, u32[]{:S(2)}) collective-permute-start(f32[392,128]{1,0:T(8,128)S(1)} %collective-permute-done.33), channel_id=1, source_target_pairs={{8,0},{16,8},{24,16},{28,24},{20,28},{12,20},{4,12},{0,4},{2,10},{... | collective-permute-start | bytes 602120 | tf_op jit(solution)/shard_map/ppermute | solution.py:293
  (37 other events, 444.3 us)

commit v6 on v5

--- a/solution.py
+++ b/solution.py
@@ -323,7 +323,6 @@
             if s < chips - 1 - far:
                 b = hop(b + c[far + 1 + s], behind)
         totals.append(c[0] + a + b)
-    totals = lax.optimization_barrier(totals)
 
     far_at = chip_at(sign, far) * blk
     far_columns = [lax.dynamic_slice_in_dim(d, far_at, blk, 1) for d in (pair_density, other)]

time: 158 us -> 155 us (0.981)
  starting transfers between devices: 66.1 us -> 63.8 us
    ppermute x50, starting transfers between devices: 56.5 us -> 54.3 us  [hop(): return lax.ppermute(x, 'orb', pairs)]
  transfers between devices with their start and end apart: 57 -> 57, of which waited for: 35 -> 36; matrix products, arithmetic and copies ran while one was open for 3% -> 3% of each run, Pallas kernels for 17% -> 17%
where the time goes in v6:
time: 155 us
  starting transfers between devices  63.8 us (41%)
  waiting for transfers between devices  52 us (34%)
  Pallas kernels  26.2 us (17%)
  local copies, waits for them, and re-layouts  7.19 us (5%)
  matrix products  2.86 us (2%)
  other arithmetic  2.65 us (2%)
    ppermute x50, starting transfers between devices, hop(): return lax.ppermute(x, 'orb', pairs)  54.3 us
    ppermute x50, waiting for transfers between devices, hop(): return lax.ppermute(x, 'orb', pairs)  45.9 us
    pallas_call x2, Pallas kernels, extract(): pl.pallas_call(functools.partial(extract_body, nb, parts), out_shape=out_...  12.5 us
    pallas_call x1, Pallas kernels, q_partial(): pl.pallas_call(functools.partial(q_body, nb, count), out_shape=jax.ShapeD...  9.97 us
    ppermute x7, starting transfers between devices, across(): return lax.ppermute(x, ('orb', 'aux'), table)  9.53 us
    unnamed x24, local copies, waits for them, and re-layouts  6.52 us
    ppermute x7, waiting for transfers between devices, across(): return lax.ppermute(x, ('orb', 'aux'), table)  6.07 us
    pallas_call x1, Pallas kernels, half_partial(): pl.pallas_call(functools.partial(half_body, chips), out_shape=[jax.ShapeD...  3.7 us
  transfers between devices with their start and end apart: 57, of which 36 were waited for; matrix products, arithmetic and copies ran while one was open for 3% of the time, Pallas kernels for 17%

profile of v6, /device:TPU:0, one launch (start us, length us, event | category | flops | bytes accessed | tf_op | source)
XLA Modules:
  0.0 155.3 jit_solution(9461800182312815343)
XLA Ops:
  1.9 7.0 %extract.2 = (f32[56,56,128]{2,1,0:T(8,128)S(1)}, f32[56,56,128]{2,1,0:T(8,128)S(1)}, f32[56,256,128]{2,1,0:T(8,128)}) custom-call(s32[11]{0:T(128)S(1)} %add_add_fusion.4.info, s32[56]{0:T(128)S(1)} %copy-done.6, f32[56,512,128]{2,1,0:T(8,128)} %three.5, s32[8,32]{1,0:T(8,128)S(1)} %bitcast.87), custom_call_target="tpu_custom_call" | custom-call | flops 411041792 | bytes 17891328 | tf_op jit(solution)/shard_map/extract/pallas_call | solution.py:109
  9.6 5.5 %extract.3 = (f32[56,56,128]{2,1,0:T(8,128)S(1)}, f32[56,56,128]{2,1,0:T(8,128)S(1)}) custom-call(s32[11]{0:T(128)S(1)} %add_add_fusion.5.info, s32[56]{0:T(128)S(1)} %copy-done.6, f32[56,512,128]{2,1,0:T(8,128)} %three.5, s32[8,32]{1,0:T(8,128)S(1)} %bitcast.88), custom_call_target="tpu_custom_call" | custom-call | flops 411041792 | bytes 10551296 | tf_op jit(solution)/shard_map/extract/pallas_call | solution.py:109
  15.9 2.4 %slice-done = s8[4194304]{0:T(1024)(128)(4,1)S(1)} async-done(((s8[7340032]{0:T(1024)(128)(4,1)}), s8[4194304]{0:T(1024)(128)(4,1)S(1)}, s32[]{:S(2)}) %slice-start) | async-done | bytes 4194328
  19.7 2.9 %collective-permute-start.3 = (f32[392,128]{1,0:T(8,128)S(1)}, f32[392,128]{1,0:T(8,128)S(1)}, u32[]{:S(2)}, u32[]{:S(2)}) collective-permute-start(f32[392,128]{1,0:T(8,128)S(1)} %get-tuple-element.51), channel_id=1, source_target_pairs={{0,8},{8,16},{16,24},{24,28},{28,20},{20,12},{12,4},{4,0},{10,2},{... | collective-permute-start | bytes 602120 | tf_op jit(solution)/shard_map/ppermute | solution.py:293
  22.6 2.0 %collective-permute-start.5 = (f32[392,128]{1,0:T(8,128)S(1)}, f32[392,128]{1,0:T(8,128)S(1)}, u32[]{:S(2)}, u32[]{:S(2)}) collective-permute-start(f32[392,128]{1,0:T(8,128)S(1)} %get-tuple-element.53), channel_id=1, source_target_pairs={{0,8},{8,16},{16,24},{24,28},{28,20},{20,12},{12,4},{4,0},{10,2},{... | collective-permute-start | bytes 602120 | tf_op jit(solution)/shard_map/ppermute | solution.py:293
  24.6 3.2 %collective-permute-done.3 = f32[392,128]{1,0:T(8,128)S(1)} collective-permute-done((f32[392,128]{1,0:T(8,128)S(1)}, f32[392,128]{1,0:T(8,128)S(1)}, u32[]{:S(2)}, u32[]{:S(2)}) %collective-permute-start.3) | collective-permute-done | bytes 200736 | tf_op jit(solution)/shard_map/ppermute | solution.py:293
  27.9 2.5 %collective-permute-done.4 = f32[392,128]{1,0:T(8,128)S(1)} collective-permute-done((f32[392,128]{1,0:T(8,128)S(1)}, f32[392,128]{1,0:T(8,128)S(1)}, u32[]{:S(2)}, u32[]{:S(2)}) %collective-permute-start.4) | collective-permute-done | bytes 200736 | tf_op jit(solution)/shard_map/ppermute | solution.py:293
  32.5 1.9 %collective-permute-start.8 = (f32[392,128]{1,0:T(8,128)S(1)}, f32[392,128]{1,0:T(8,128)S(1)}, u32[]{:S(2)}, u32[]{:S(2)}) collective-permute-start(f32[392,128]{1,0:T(8,128)S(1)} %add.232), channel_id=1, source_target_pairs={{0,8},{8,16},{16,24},{24,28},{28,20},{20,12},{12,4},{4,0},{10,2},{... | collective-permute-start | bytes 602120 | tf_op jit(solution)/shard_map/ppermute | solution.py:293
  34.4 1.8 %collective-permute-start.13 = (f32[392,128]{1,0:T(8,128)S(1)}, f32[392,128]{1,0:T(8,128)S(1)}, u32[]{:S(2)}, u32[]{:S(2)}) collective-permute-start(f32[392,128]{1,0:T(8,128)S(1)} %add.239), channel_id=1, source_target_pairs={{0,8},{8,16},{16,24},{24,28},{28,20},{20,12},{12,4},{4,0},{10,2},{... | collective-permute-start | bytes 602120 | tf_op jit(solution)/shard_map/ppermute | solution.py:293
  36.6 2.3 %collective-permute-done.8 = f32[392,128]{1,0:T(8,128)S(1)} collective-permute-done((f32[392,128]{1,0:T(8,128)S(1)}, f32[392,128]{1,0:T(8,128)S(1)}, u32[]{:S(2)}, u32[]{:S(2)}) %collective-permute-start.8) | collective-permute-done | bytes 200736 | tf_op jit(solution)/shard_map/ppermute | solution.py:293
  38.9 2.5 %collective-permute-start.9 = (f32[392,128]{1,0:T(8,128)S(1)}, f32[392,128]{1,0:T(8,128)S(1)}, u32[]{:S(2)}, u32[]{:S(2)}) collective-permute-start(f32[392,128]{1,0:T(8,128)S(1)} %add.233), channel_id=1, source_target_pairs={{0,8},{8,16},{16,24},{24,28},{28,20},{20,12},{12,4},{4,0},{10,2},{... | collective-permute-start | bytes 602120 | tf_op jit(solution)/shard_map/ppermute | solution.py:293
  43.2 2.5 %collective-permute-start.14 = (f32[392,128]{1,0:T(8,128)S(1)}, f32[392,128]{1,0:T(8,128)S(1)}, u32[]{:S(2)}, u32[]{:S(2)}) collective-permute-start(f32[392,128]{1,0:T(8,128)S(1)} %add.240), channel_id=1, source_target_pairs={{0,8},{8,16},{16,24},{24,28},{28,20},{20,12},{12,4},{4,0},{10,2},{... | collective-permute-start | bytes 602120 | tf_op jit(solution)/shard_map/ppermute | solution.py:293
  47.5 2.5 %collective-permute-start.10 = (f32[392,128]{1,0:T(8,128)S(1)}, f32[392,128]{1,0:T(8,128)S(1)}, u32[]{:S(2)}, u32[]{:S(2)}) collective-permute-start(f32[392,128]{1,0:T(8,128)S(1)} %add.234), channel_id=1, source_target_pairs={{0,8},{8,16},{16,24},{24,28},{28,20},{20,12},{12,4},{4,0},{10,2},{... | collective-permute-start | bytes 602120 | tf_op jit(solution)/shard_map/ppermute | solution.py:293
  51.8 2.5 %collective-permute-start.15 = (f32[392,128]{1,0:T(8,128)S(1)}, f32[392,128]{1,0:T(8,128)S(1)}, u32[]{:S(2)}, u32[]{:S(2)}) collective-permute-start(f32[392,128]{1,0:T(8,128)S(1)} %add.241), channel_id=1, source_target_pairs={{0,8},{8,16},{16,24},{24,28},{28,20},{20,12},{12,4},{4,0},{10,2},{... | collective-permute-start | bytes 602120 | tf_op jit(solution)/shard_map/ppermute | solution.py:293
  57.0 1.8 %collective-permute-start.24 = (f32[392,128]{1,0:T(8,128)S(1)}, f32[392,128]{1,0:T(8,128)S(1)}, u32[]{:S(2)}, u32[]{:S(2)}) collective-permute-start(f32[392,128]{1,0:T(8,128)S(1)} %add_add_fusion.1.refs_0_), channel_id=1, source_target_pairs={{0,8},{8,16},{16,24},{24,28},{28,20},{20,12},{12,4},{4,0},{10,2},{... | collective-permute-start | bytes 602120 | tf_op jit(solution)/shard_map/ppermute | solution.py:293
  60.5 2.5 %collective-permute-start.27 = (f32[392,128]{1,0:T(8,128)S(1)}, f32[392,128]{1,0:T(8,128)}, u32[]{:S(2)}, u32[]{:S(2)}) collective-permute-start(f32[392,128]{1,0:T(8,128)S(1)} %add_add_fusion.refs_1_), channel_id=1, source_target_pairs={{0,8},{8,16},{16,24},{24,28},{28,20},{20,12},{12,4},{4,0},{10,2},{... | collective-permute-start | bytes 602120 | tf_op jit(solution)/shard_map/ppermute | solution.py:293
  64.7 2.5 %collective-permute-start.25 = (f32[392,128]{1,0:T(8,128)S(1)}, f32[392,128]{1,0:T(8,128)S(1)}, u32[]{:S(2)}, u32[]{:S(2)}) collective-permute-start(f32[392,128]{1,0:T(8,128)S(1)} %collective-permute-done.24.refs_12_), channel_id=1, source_target_pairs={{0,8},{8,16},{16,24},{24,28},{28,20},{20,12},{12,4},{4,0},{10,2},{... | collective-permute-start | bytes 602120 | tf_op jit(solution)/shard_map/ppermute | solution.py:293
  69.0 2.6 %collective-permute-start.28 = (f32[392,128]{1,0:T(8,128)}, f32[392,128]{1,0:T(8,128)S(1)}, u32[]{:S(2)}, u32[]{:S(2)}) collective-permute-start(f32[392,128]{1,0:T(8,128)} %collective-permute-done.27.refs_13_), channel_id=1, source_target_pairs={{0,8},{8,16},{16,24},{24,28},{28,20},{20,12},{12,4},{4,0},{10,2},{... | collective-permute-start | bytes 602120 | tf_op jit(solution)/shard_map/ppermute | solution.py:293
  73.1 2.2 %collective-permute-start.26 = (f32[392,128]{1,0:T(8,128)S(1)}, f32[392,128]{1,0:T(8,128)S(1)}, u32[]{:S(2)}, u32[]{:S(2)}) collective-permute-start(f32[392,128]{1,0:T(8,128)S(1)} %collective-permute-done.25.refs_10_), channel_id=1, source_target_pairs={{0,8},{8,16},{16,24},{24,28},{28,20},{20,12},{12,4},{4,0},{10,2},{... | collective-permute-start | bytes 602120 | tf_op jit(solution)/shard_map/ppermute | solution.py:293
  75.4 2.8 %collective-permute-done.21.refs_5_ = f32[392,128]{1,0:T(8,128)S(1)} collective-permute-done((f32[392,128]{1,0:T(8,128)}, f32[392,128]{1,0:T(8,128)S(1)}, u32[]{:S(2)}, u32[]{:S(2)}) %collective-permute-start.21) | collective-permute-done | bytes 200736 | tf_op jit(solution)/shard_map/ppermute | solution.py:293
  81.3 1.8 %collective-permute-start.30 = (f32[392,128]{1,0:T(8,128)S(1)}, f32[392,128]{1,0:T(8,128)S(1)}, u32[]{:S(2)}, u32[]{:S(2)}) collective-permute-start(f32[392,128]{1,0:T(8,128)S(1)} %collective-permute-done.26.refs_8_), channel_id=1, source_target_pairs={{0,8},{8,16},{16,24},{24,28},{28,20},{20,12},{12,4},{4,0},{10,2},{... | collective-permute-start | bytes 602120 | tf_op jit(solution)/shard_map/ppermute | solution.py:293
  89.4 3.7 %half.1 = (f32[392,128]{1,0:T(8,128)S(1)}, f32[392,128]{1,0:T(8,128)S(1)}) custom-call(s32[11]{0:T(128)S(1)} %add_add_fusion.5.info, f32[196,3136]{1,0:T(8,128)S(1)} %copy-done.1, f32[196,3136]{1,0:T(8,128)S(1)} %copy-done.3, f32[392,128]{1,0:T(8,128)S(1)} %add_add_fusion.1.refs_0_, f32[392,128]{1,0:T(8,128)S(1)} %add_add_fusion.refs_1_, ...), custom_call_target="tpu_custom_call" | custom-call | flops 1888223232 | bytes 8128512 | tf_op jit(solution)/shard_map/half/pallas_call | solution.py:243
  98.5 1.9 %collective-permute-done.35 = f32[392,128]{1,0:T(8,128)S(1)} collective-permute-done((f32[392,128]{1,0:T(8,128)S(1)}, f32[392,128]{1,0:T(8,128)S(1)}, u32[]{:S(2)}, u32[]{:S(2)}) %collective-permute-start.35) | collective-permute-done | bytes 200736 | tf_op jit(solution)/shard_map/ppermute | solution.py:293
  107.2 2.5 %collective-permute-done.43 = f32[392,128]{1,0:T(8,128)S(1)} collective-permute-done((f32[392,128]{1,0:T(8,128)S(1)}, f32[392,128]{1,0:T(8,128)S(1)}, u32[]{:S(2)}, u32[]{:S(2)}) %collective-permute-start.43) | collective-permute-done | bytes 200736 | tf_op jit(solution)/shard_map/ppermute | solution.py:293
  112.4 1.7 %collective-permute-done.40 = f32[392,128]{1,0:T(8,128)S(1)} collective-permute-done((f32[392,128]{1,0:T(8,128)S(1)}, f32[392,128]{1,0:T(8,128)S(1)}, u32[]{:S(2)}, u32[]{:S(2)}) %collective-permute-start.40) | collective-permute-done | bytes 200736 | tf_op jit(solution)/shard_map/ppermute | solution.py:293
  116.2 2.5 %collective-permute-done.44 = f32[392,128]{1,0:T(8,128)S(1)} collective-permute-done((f32[392,128]{1,0:T(8,128)S(1)}, f32[392,128]{1,0:T(8,128)S(1)}, u32[]{:S(2)}, u32[]{:S(2)}) %collective-permute-start.44) | collective-permute-done | bytes 200736 | tf_op jit(solution)/shard_map/ppermute | solution.py:293
  119.5 2.1 %collective-permute-done.41 = f32[392,128]{1,0:T(8,128)S(1)} collective-permute-done((f32[392,128]{1,0:T(8,128)S(1)}, f32[392,128]{1,0:T(8,128)S(1)}, u32[]{:S(2)}, u32[]{:S(2)}) %collective-permute-start.41) | collective-permute-done | bytes 200736 | tf_op jit(solution)/shard_map/ppermute | solution.py:293
  123.3 2.1 %collective-permute-done.45 = f32[392,128]{1,0:T(8,128)S(1)} collective-permute-done((f32[392,128]{1,0:T(8,128)S(1)}, f32[392,128]{1,0:T(8,128)S(1)}, u32[]{:S(2)}, u32[]{:S(2)}) %collective-permute-start.45) | collective-permute-done | bytes 200736 | tf_op jit(solution)/shard_map/ppermute | solution.py:293
  125.4 10.0 %qpartial.1 = f32[64,256]{1,0:T(8,128)S(1)} custom-call(s32[11]{0:T(128)S(1)} %add_add_fusion.5.info, f32[56,512,128]{2,1,0:T(8,128)} %three.5, s32[8,32]{1,0:T(8,128)S(1)} %bitcast.89, f32[56,256,128]{2,1,0:T(8,128)} %collective-permute-done.7.sib, f32[7,56,128]{2,1,0:T(8,128)S(1)} %bitcast.70, f32[7,56,128]{2,1,0:T(8,128)S(1)} %bitcast.75, ...), custom_call_target="tpu_custom_call" | custom-call | flops 1233125376 | bytes 17891328 | tf_op jit(solution)/shard_map/qpartial/pallas_call | solution.py:176
  137.5 2.7 %collective-permute-start.52 = (f32[112,128]{1,0:T(8,128)S(1)}, f32[112,128]{1,0:T(8,128)S(1)}, u32[]{:S(2)}, u32[]{:S(2)}) collective-permute-start(f32[112,128]{1,0:T(8,128)S(1)} %add.264), channel_id=1, source_target_pairs={{0,5},{1,4},{2,7},{3,6},{4,1},{5,0},{6,3},{7,2},{8,13},{9,12},{10,... | collective-permute-start | bytes 172040 | tf_op jit(solution)/shard_map/ppermute | solution.py:358
  142.6 1.8 %collective-permute-done.51 = f32[112,128]{1,0:T(8,128)S(1)} collective-permute-done((f32[112,128]{1,0:T(8,128)S(1)}, f32[112,128]{1,0:T(8,128)S(1)}, u32[]{:S(2)}, u32[]{:S(2)}) %collective-permute-start.51) | collective-permute-done | bytes 57376 | tf_op jit(solution)/shard_map/ppermute | solution.py:358
  144.9 2.1 %collective-permute-start.55 = (f32[112,128]{1,0:T(8,128)S(1)}, f32[112,128]{1,0:T(8,128)S(1)}, u32[]{:S(2)}, u32[]{:S(2)}) collective-permute-start(f32[112,128]{1,0:T(8,128)S(1)} %add_add_fusion.3), channel_id=1, source_target_pairs={{0,24},{1,25},{2,26},{3,27},{4,28},{5,29},{6,30},{7,31},{8,16},{9,... | collective-permute-start | bytes 172040 | tf_op jit(solution)/shard_map/ppermute | solution.py:358
  (165 shorter events, 63.8 us)
Async XLA Ops:
  0.0 15.8 %collective-permute-start.2 = (f32[196,3136]{1,0:T(8,128)}, f32[196,3136]{1,0:T(8,128)S(1)}, u32[]{:S(2)}, u32[]{:S(2)}) collective-permute-start(f32[196,3136]{1,0:T(8,128)} %own.1), channel_id=1, source_target_pairs={{0,2},{2,0},{4,6},{6,4},{8,10},{10,8},{12,14},{14,12},{16,18},{18,... | collective-permute-start | bytes 7375880 | tf_op jit(solution)/shard_map/ppermute | solution.py:293
  19.3 13.2 %collective-permute-start.7 = (f32[56,256,128]{2,1,0:T(8,128)S(1)}, f32[56,256,128]{2,1,0:T(8,128)}, u32[]{:S(2)}, u32[]{:S(2)}) collective-permute-start(f32[56,256,128]{2,1,0:T(8,128)S(1)} %bitcast.93), channel_id=1, source_target_pairs={{0,2},{2,0},{4,6},{6,4},{8,10},{10,8},{12,14},{14,12},{16,18},{18,... | collective-permute-start | bytes 22020104 | tf_op jit(solution)/shard_map/ppermute | solution.py:293
  19.7 8.2 %collective-permute-start.3 = (f32[392,128]{1,0:T(8,128)S(1)}, f32[392,128]{1,0:T(8,128)S(1)}, u32[]{:S(2)}, u32[]{:S(2)}) collective-permute-start(f32[392,128]{1,0:T(8,128)S(1)} %get-tuple-element.51), channel_id=1, source_target_pairs={{0,8},{8,16},{16,24},{24,28},{28,20},{20,12},{12,4},{4,0},{10,2},{... | collective-permute-start | bytes 602120 | tf_op jit(solution)/shard_map/ppermute | solution.py:293
  22.6 7.8 %collective-permute-start.4 = (f32[392,128]{1,0:T(8,128)S(1)}, f32[392,128]{1,0:T(8,128)S(1)}, u32[]{:S(2)}, u32[]{:S(2)}) collective-permute-start(f32[392,128]{1,0:T(8,128)S(1)} %get-tuple-element.52), channel_id=1, source_target_pairs={{8,0},{16,8},{24,16},{28,24},{20,28},{12,20},{4,12},{0,4},{2,10},{... | collective-permute-start | bytes 602120 | tf_op jit(solution)/shard_map/ppermute | solution.py:293
  22.6 9.2 %collective-permute-start.5 = (f32[392,128]{1,0:T(8,128)S(1)}, f32[392,128]{1,0:T(8,128)S(1)}, u32[]{:S(2)}, u32[]{:S(2)}) collective-permute-start(f32[392,128]{1,0:T(8,128)S(1)} %get-tuple-element.53), channel_id=1, source_target_pairs={{0,8},{8,16},{16,24},{24,28},{28,20},{20,12},{12,4},{4,0},{10,2},{... | collective-permute-start | bytes 602120 | tf_op jit(solution)/shard_map/ppermute | solution.py:293
  24.6 7.9 %collective-permute-start.6 = (f32[392,128]{1,0:T(8,128)S(1)}, f32[392,128]{1,0:T(8,128)S(1)}, u32[]{:S(2)}, u32[]{:S(2)}) collective-permute-start(f32[392,128]{1,0:T(8,128)S(1)} %get-tuple-element.54), channel_id=1, source_target_pairs={{8,0},{16,8},{24,16},{28,24},{20,28},{12,20},{4,12},{0,4},{2,10},{... | collective-permute-start | bytes 602120 | tf_op jit(solution)/shard_map/ppermute | solution.py:293
  34.4 8.8 %collective-permute-start.13 = (f32[392,128]{1,0:T(8,128)S(1)}, f32[392,128]{1,0:T(8,128)S(1)}, u32[]{:S(2)}, u32[]{:S(2)}) collective-permute-start(f32[392,128]{1,0:T(8,128)S(1)} %add.239), channel_id=1, source_target_pairs={{0,8},{8,16},{16,24},{24,28},{28,20},{20,12},{12,4},{4,0},{10,2},{... | collective-permute-start | bytes 602120 | tf_op jit(solution)/shard_map/ppermute | solution.py:293
  36.2 9.6 %collective-permute-start.11 = (f32[392,128]{1,0:T(8,128)S(1)}, f32[392,128]{1,0:T(8,128)S(1)}, u32[]{:S(2)}, u32[]{:S(2)}) collective-permute-start(f32[392,128]{1,0:T(8,128)S(1)} %add.236), channel_id=1, source_target_pairs={{8,0},{16,8},{24,16},{28,24},{20,28},{12,20},{4,12},{0,4},{2,10},{... | collective-permute-start | bytes 602120 | tf_op jit(solution)/shard_map/ppermute | solution.py:293
  38.9 8.6 %collective-permute-start.9 = (f32[392,128]{1,0:T(8,128)S(1)}, f32[392,128]{1,0:T(8,128)S(1)}, u32[]{:S(2)}, u32[]{:S(2)}) collective-permute-start(f32[392,128]{1,0:T(8,128)S(1)} %add.233), channel_id=1, source_target_pairs={{0,8},{8,16},{16,24},{24,28},{28,20},{20,12},{12,4},{4,0},{10,2},{... | collective-permute-start | bytes 602120 | tf_op jit(solution)/shard_map/ppermute | solution.py:293
  41.5 8.6 %collective-permute-start.16 = (f32[392,128]{1,0:T(8,128)S(1)}, f32[392,128]{1,0:T(8,128)S(1)}, u32[]{:S(2)}, u32[]{:S(2)}) collective-permute-start(f32[392,128]{1,0:T(8,128)S(1)} %add.243), channel_id=1, source_target_pairs={{8,0},{16,8},{24,16},{28,24},{20,28},{12,20},{4,12},{0,4},{2,10},{... | collective-permute-start | bytes 602120 | tf_op jit(solution)/shard_map/ppermute | solution.py:293
  43.2 8.6 %collective-permute-start.14 = (f32[392,128]{1,0:T(8,128)S(1)}, f32[392,128]{1,0:T(8,128)S(1)}, u32[]{:S(2)}, u32[]{:S(2)}) collective-permute-start(f32[392,128]{1,0:T(8,128)S(1)} %add.240), channel_id=1, source_target_pairs={{0,8},{8,16},{16,24},{24,28},{28,20},{20,12},{12,4},{4,0},{10,2},{... | collective-permute-start | bytes 602120 | tf_op jit(solution)/shard_map/ppermute | solution.py:293
  45.8 8.5 %collective-permute-start.12 = (f32[392,128]{1,0:T(8,128)S(1)}, f32[392,128]{1,0:T(8,128)S(1)}, u32[]{:S(2)}, u32[]{:S(2)}) collective-permute-start(f32[392,128]{1,0:T(8,128)S(1)} %add.237), channel_id=1, source_target_pairs={{8,0},{16,8},{24,16},{28,24},{20,28},{12,20},{4,12},{0,4},{2,10},{... | collective-permute-start | bytes 602120 | tf_op jit(solution)/shard_map/ppermute | solution.py:293
  47.5 8.6 %collective-permute-start.10 = (f32[392,128]{1,0:T(8,128)S(1)}, f32[392,128]{1,0:T(8,128)S(1)}, u32[]{:S(2)}, u32[]{:S(2)}) collective-permute-start(f32[392,128]{1,0:T(8,128)S(1)} %add.234), channel_id=1, source_target_pairs={{0,8},{8,16},{16,24},{24,28},{28,20},{20,12},{12,4},{4,0},{10,2},{... | collective-permute-start | bytes 602120 | tf_op jit(solution)/shard_map/ppermute | solution.py:293
  50.1 8.7 %collective-permute-start.17 = (f32[392,128]{1,0:T(8,128)S(1)}, f32[392,128]{1,0:T(8,128)S(1)}, u32[]{:S(2)}, u32[]{:S(2)}) collective-permute-start(f32[392,128]{1,0:T(8,128)S(1)} %add.244), channel_id=1, source_target_pairs={{8,0},{16,8},{24,16},{28,24},{20,28},{12,20},{4,12},{0,4},{2,10},{... | collective-permute-start | bytes 602120 | tf_op jit(solution)/shard_map/ppermute | solution.py:293
  51.8 8.6 %collective-permute-start.15 = (f32[392,128]{1,0:T(8,128)S(1)}, f32[392,128]{1,0:T(8,128)S(1)}, u32[]{:S(2)}, u32[]{:S(2)}) collective-permute-start(f32[392,128]{1,0:T(8,128)S(1)} %add.241), channel_id=1, source_target_pairs={{0,8},{8,16},{16,24},{24,28},{28,20},{20,12},{12,4},{4,0},{10,2},{... | collective-permute-start | bytes 602120 | tf_op jit(solution)/shard_map/ppermute | solution.py:293
  56.1 11.0 %collective-permute-start.18 = (f32[392,128]{1,0:T(8,128)S(1)}, f32[392,128]{1,0:T(8,128)S(1)}, u32[]{:S(2)}, u32[]{:S(2)}) collective-permute-start(f32[392,128]{1,0:T(8,128)S(1)} %add_add_fusion.1.refs_0_), channel_id=1, source_target_pairs={{8,0},{16,8},{24,16},{28,24},{20,28},{12,20},{4,12},{0,4},{2,10},{... | collective-permute-start | bytes 602120 | tf_op jit(solution)/shard_map/ppermute | solution.py:293
  60.4 8.5 %collective-permute-start.19 = (f32[392,128]{1,0:T(8,128)S(1)}, f32[392,128]{1,0:T(8,128)}, u32[]{:S(2)}, u32[]{:S(2)}) collective-permute-start(f32[392,128]{1,0:T(8,128)S(1)} %add_add_fusion.refs_1_), channel_id=1, source_target_pairs={{8,0},{16,8},{24,16},{28,24},{20,28},{12,20},{4,12},{0,4},{2,10},{... | collective-permute-start | bytes 602120 | tf_op jit(solution)/shard_map/ppermute | solution.py:293
  60.5 8.5 %collective-permute-start.27 = (f32[392,128]{1,0:T(8,128)S(1)}, f32[392,128]{1,0:T(8,128)}, u32[]{:S(2)}, u32[]{:S(2)}) collective-permute-start(f32[392,128]{1,0:T(8,128)S(1)} %add_add_fusion.refs_1_), channel_id=1, source_target_pairs={{0,8},{8,16},{16,24},{24,28},{28,20},{20,12},{12,4},{4,0},{10,2},{... | collective-permute-start | bytes 602120 | tf_op jit(solution)/shard_map/ppermute | solution.py:293
  64.7 8.4 %collective-permute-start.25 = (f32[392,128]{1,0:T(8,128)S(1)}, f32[392,128]{1,0:T(8,128)S(1)}, u32[]{:S(2)}, u32[]{:S(2)}) collective-permute-start(f32[392,128]{1,0:T(8,128)S(1)} %collective-permute-done.24.refs_12_), channel_id=1, source_target_pairs={{0,8},{8,16},{16,24},{24,28},{28,20},{20,12},{12,4},{4,0},{10,2},{... | collective-permute-start | bytes 602120 | tf_op jit(solution)/shard_map/ppermute | solution.py:293
  67.2 8.2 %collective-permute-start.20 = (f32[392,128]{1,0:T(8,128)S(1)}, f32[392,128]{1,0:T(8,128)S(1)}, u32[]{:S(2)}, u32[]{:S(2)}) collective-permute-start(f32[392,128]{1,0:T(8,128)S(1)} %collective-permute-done.18.refs_2_), channel_id=1, source_target_pairs={{8,0},{16,8},{24,16},{28,24},{20,28},{12,20},{4,12},{0,4},{2,10},{... | collective-permute-start | bytes 602120 | tf_op jit(solution)/shard_map/ppermute | solution.py:293
  68.9 9.3 %collective-permute-start.21 = (f32[392,128]{1,0:T(8,128)}, f32[392,128]{1,0:T(8,128)S(1)}, u32[]{:S(2)}, u32[]{:S(2)}) collective-permute-start(f32[392,128]{1,0:T(8,128)} %collective-permute-done.19.refs_3_), channel_id=1, source_target_pairs={{8,0},{16,8},{24,16},{28,24},{20,28},{12,20},{4,12},{0,4},{2,10},{... | collective-permute-start | bytes 602120 | tf_op jit(solution)/shard_map/ppermute | solution.py:293
  69.0 10.4 %collective-permute-start.28 = (f32[392,128]{1,0:T(8,128)}, f32[392,128]{1,0:T(8,128)S(1)}, u32[]{:S(2)}, u32[]{:S(2)}) collective-permute-start(f32[392,128]{1,0:T(8,128)} %collective-permute-done.27.refs_13_), channel_id=1, source_target_pairs={{0,8},{8,16},{16,24},{24,28},{28,20},{20,12},{12,4},{4,0},{10,2},{... | collective-permute-start | bytes 602120 | tf_op jit(solution)/shard_map/ppermute | solution.py:293
  73.1 8.2 %collective-permute-start.26 = (f32[392,128]{1,0:T(8,128)S(1)}, f32[392,128]{1,0:T(8,128)S(1)}, u32[]{:S(2)}, u32[]{:S(2)}) collective-permute-start(f32[392,128]{1,0:T(8,128)S(1)} %collective-permute-done.25.refs_10_), channel_id=1, source_target_pairs={{0,8},{8,16},{16,24},{24,28},{28,20},{20,12},{12,4},{4,0},{10,2},{... | collective-permute-start | bytes 602120 | tf_op jit(solution)/shard_map/ppermute | solution.py:293
  75.4 11.0 %collective-permute-start.22 = (f32[392,128]{1,0:T(8,128)S(1)}, f32[392,128]{1,0:T(8,128)S(1)}, u32[]{:S(2)}, u32[]{:S(2)}) collective-permute-start(f32[392,128]{1,0:T(8,128)S(1)} %collective-permute-done.20.refs_4_), channel_id=1, source_target_pairs={{8,0},{16,8},{24,16},{28,24},{20,28},{12,20},{4,12},{0,4},{2,10},{... | collective-permute-start | bytes 602120 | tf_op jit(solution)/shard_map/ppermute | solution.py:293
  78.3 9.4 %collective-permute-start.23 = (f32[392,128]{1,0:T(8,128)S(1)}, f32[392,128]{1,0:T(8,128)S(1)}, u32[]{:S(2)}, u32[]{:S(2)}) collective-permute-start(f32[392,128]{1,0:T(8,128)S(1)} %collective-permute-done.21.refs_5_), channel_id=1, source_target_pairs={{8,0},{16,8},{24,16},{28,24},{20,28},{12,20},{4,12},{0,4},{2,10},{... | collective-permute-start | bytes 602120 | tf_op jit(solution)/shard_map/ppermute | solution.py:293
  81.3 11.8 %collective-permute-start.30 = (f32[392,128]{1,0:T(8,128)S(1)}, f32[392,128]{1,0:T(8,128)S(1)}, u32[]{:S(2)}, u32[]{:S(2)}) collective-permute-start(f32[392,128]{1,0:T(8,128)S(1)} %collective-permute-done.26.refs_8_), channel_id=1, source_target_pairs={{0,8},{8,16},{16,24},{24,28},{28,20},{20,12},{12,4},{4,0},{10,2},{... | collective-permute-start | bytes 602120 | tf_op jit(solution)/shard_map/ppermute | solution.py:293
  85.1 8.5 %collective-permute-start.31 = (f32[392,128]{1,0:T(8,128)S(1)}, f32[392,128]{1,0:T(8,128)S(1)}, u32[]{:S(2)}, u32[]{:S(2)}) collective-permute-start(f32[392,128]{1,0:T(8,128)S(1)} %collective-permute-done.29.refs_9_), channel_id=1, source_target_pairs={{0,8},{8,16},{16,24},{24,28},{28,20},{20,12},{12,4},{4,0},{10,2},{... | collective-permute-start | bytes 602120 | tf_op jit(solution)/shard_map/ppermute | solution.py:293
  103.6 32.6 %collective-permute-start.48 = (f32[128,200]{1,0:T(8,128)S(1)}, f32[128,200]{1,0:T(8,128)S(1)}, u32[]{:S(2)}, u32[]{:S(2)}) collective-permute-start(f32[128,200]{1,0:T(8,128)S(1)} %add_multiply_fusion), channel_id=1, source_target_pairs={{0,2},{2,0},{4,6},{6,4},{8,10},{10,8},{12,14},{14,12},{16,18},{18,... | collective-permute-start | bytes 307208 | tf_op jit(solution)/shard_map/ppermute | solution.py:293
  105.0 9.2 %collective-permute-start.40 = (f32[392,128]{1,0:T(8,128)S(1)}, f32[392,128]{1,0:T(8,128)S(1)}, u32[]{:S(2)}, u32[]{:S(2)}) collective-permute-start(f32[392,128]{1,0:T(8,128)S(1)} %collective-permute-done.39), channel_id=1, source_target_pairs={{8,0},{16,8},{24,16},{28,24},{20,28},{12,20},{4,12},{0,4},{2,10},{... | collective-permute-start | bytes 602120 | tf_op jit(solution)/shard_map/ppermute | solution.py:293
  106.4 9.3 %collective-permute-start.37 = (f32[392,128]{1,0:T(8,128)S(1)}, f32[392,128]{1,0:T(8,128)S(1)}, u32[]{:S(2)}, u32[]{:S(2)}) collective-permute-start(f32[392,128]{1,0:T(8,128)S(1)} %collective-permute-done.36), channel_id=1, source_target_pairs={{0,8},{8,16},{16,24},{24,28},{28,20},{20,12},{12,4},{4,0},{10,2},{... | collective-permute-start | bytes 602120 | tf_op jit(solution)/shard_map/ppermute | solution.py:293
  109.6 9.0 %collective-permute-start.44 = (f32[392,128]{1,0:T(8,128)S(1)}, f32[392,128]{1,0:T(8,128)S(1)}, u32[]{:S(2)}, u32[]{:S(2)}) collective-permute-start(f32[392,128]{1,0:T(8,128)S(1)} %collective-permute-done.43), channel_id=1, source_target_pairs={{0,8},{8,16},{16,24},{24,28},{28,20},{20,12},{12,4},{4,0},{10,2},{... | collective-permute-start | bytes 602120 | tf_op jit(solution)/shard_map/ppermute | solution.py:293
  111.1 8.4 %collective-permute-start.34 = (f32[392,128]{1,0:T(8,128)S(1)}, f32[392,128]{1,0:T(8,128)S(1)}, u32[]{:S(2)}, u32[]{:S(2)}) collective-permute-start(f32[392,128]{1,0:T(8,128)S(1)} %collective-permute-done.33), channel_id=1, source_target_pairs={{8,0},{16,8},{24,16},{28,24},{20,28},{12,20},{4,12},{0,4},{2,10},{... | collective-permute-start | bytes 602120 | tf_op jit(solution)/shard_map/ppermute | solution.py:293
  (37 other events, 425.2 us)

commit v7 on v6

--- a/solution.py
+++ b/solution.py
@@ -346,7 +346,6 @@
     near_blocks = [gathered[k][j] for j in range(chips) if j != far for k in range(2)]
     halves = half_partial(pair_density, other, near_blocks, mine, chips)
     halves = [h + jnp.dot(density_far, gathered[k][far], precision=HIGH) for k, h in enumerate(halves)]
-    halves = lax.optimization_barrier(halves)
     q = q_partial(three_index, shells, sib_three, [gather(x) for x in halves], mine)
     q = q.reshape(chips, TILE, 2 * rows)[:, :nb].reshape(act, 2 * rows)
 

time: 155 us -> 155 us (level)
  no operation moved by 1% of the time
where the time goes in v7:
time: 155 us
  starting transfers between devices  63 us (41%)
  waiting for transfers between devices  52.4 us (34%)
  Pallas kernels  26.2 us (17%)
  local copies, waits for them, and re-layouts  7.19 us (5%)
  matrix products  2.85 us (2%)
  other arithmetic  2.65 us (2%)
    ppermute x50, starting transfers between devices, hop(): return lax.ppermute(x, 'orb', pairs)  53.5 us
    ppermute x50, waiting for transfers between devices, hop(): return lax.ppermute(x, 'orb', pairs)  46.5 us
    pallas_call x2, Pallas kernels, extract(): pl.pallas_call(functools.partial(extract_body, nb, parts), out_shape=out_...  12.5 us
    pallas_call x1, Pallas kernels, q_partial(): pl.pallas_call(functools.partial(q_body, nb, count), out_shape=jax.ShapeD...  9.97 us
    ppermute x7, starting transfers between devices, across(): return lax.ppermute(x, ('orb', 'aux'), table)  9.52 us
    unnamed x24, local copies, waits for them, and re-layouts  6.52 us
    ppermute x7, waiting for transfers between devices, across(): return lax.ppermute(x, ('orb', 'aux'), table)  5.86 us
    pallas_call x1, Pallas kernels, half_partial(): pl.pallas_call(functools.partial(half_body, chips), out_shape=[jax.ShapeD...  3.69 us
  transfers between devices with their start and end apart: 57, of which 36 were waited for; matrix products, arithmetic and copies ran while one was open for 3% of the time, Pallas kernels for 17%

profile of v7, /device:TPU:0, one launch (start us, length us, event | category | flops | bytes accessed | tf_op | source)
XLA Modules:
  0.0 154.8 jit_solution(8556298758445222647)
XLA Ops:
  1.9 7.0 %extract.2 = (f32[56,56,128]{2,1,0:T(8,128)S(1)}, f32[56,56,128]{2,1,0:T(8,128)S(1)}, f32[56,256,128]{2,1,0:T(8,128)}) custom-call(s32[11]{0:T(128)S(1)} %add_add_fusion.4.info, s32[56]{0:T(128)S(1)} %copy-done.6, f32[56,512,128]{2,1,0:T(8,128)} %three.5, s32[8,32]{1,0:T(8,128)S(1)} %bitcast.87), custom_call_target="tpu_custom_call" | custom-call | flops 411041792 | bytes 17891328 | tf_op jit(solution)/shard_map/extract/pallas_call | solution.py:109
  9.6 5.5 %extract.3 = (f32[56,56,128]{2,1,0:T(8,128)S(1)}, f32[56,56,128]{2,1,0:T(8,128)S(1)}) custom-call(s32[11]{0:T(128)S(1)} %add_add_fusion.5.info, s32[56]{0:T(128)S(1)} %copy-done.6, f32[56,512,128]{2,1,0:T(8,128)} %three.5, s32[8,32]{1,0:T(8,128)S(1)} %bitcast.88), custom_call_target="tpu_custom_call" | custom-call | flops 411041792 | bytes 10551296 | tf_op jit(solution)/shard_map/extract/pallas_call | solution.py:109
  15.9 2.4 %slice-done = s8[4194304]{0:T(1024)(128)(4,1)S(1)} async-done(((s8[7340032]{0:T(1024)(128)(4,1)}), s8[4194304]{0:T(1024)(128)(4,1)S(1)}, s32[]{:S(2)}) %slice-start) | async-done | bytes 4194328
  19.7 3.5 %collective-permute-start.3 = (f32[392,128]{1,0:T(8,128)S(1)}, f32[392,128]{1,0:T(8,128)S(1)}, u32[]{:S(2)}, u32[]{:S(2)}) collective-permute-start(f32[392,128]{1,0:T(8,128)S(1)} %get-tuple-element.49), channel_id=1, source_target_pairs={{0,8},{8,16},{16,24},{24,28},{28,20},{20,12},{12,4},{4,0},{10,2},{... | collective-permute-start | bytes 602120 | tf_op jit(solution)/shard_map/ppermute | solution.py:293
  23.1 2.0 %collective-permute-start.5 = (f32[392,128]{1,0:T(8,128)S(1)}, f32[392,128]{1,0:T(8,128)S(1)}, u32[]{:S(2)}, u32[]{:S(2)}) collective-permute-start(f32[392,128]{1,0:T(8,128)S(1)} %get-tuple-element.51), channel_id=1, source_target_pairs={{0,8},{8,16},{16,24},{24,28},{28,20},{20,12},{12,4},{4,0},{10,2},{... | collective-permute-start | bytes 602120 | tf_op jit(solution)/shard_map/ppermute | solution.py:293
  25.2 3.3 %collective-permute-done.3 = f32[392,128]{1,0:T(8,128)S(1)} collective-permute-done((f32[392,128]{1,0:T(8,128)S(1)}, f32[392,128]{1,0:T(8,128)S(1)}, u32[]{:S(2)}, u32[]{:S(2)}) %collective-permute-start.3) | collective-permute-done | bytes 200736 | tf_op jit(solution)/shard_map/ppermute | solution.py:293
  28.5 2.0 %collective-permute-done.4 = f32[392,128]{1,0:T(8,128)S(1)} collective-permute-done((f32[392,128]{1,0:T(8,128)S(1)}, f32[392,128]{1,0:T(8,128)S(1)}, u32[]{:S(2)}, u32[]{:S(2)}) %collective-permute-start.4) | collective-permute-done | bytes 200736 | tf_op jit(solution)/shard_map/ppermute | solution.py:293
  32.7 2.0 %collective-permute-start.8 = (f32[392,128]{1,0:T(8,128)S(1)}, f32[392,128]{1,0:T(8,128)S(1)}, u32[]{:S(2)}, u32[]{:S(2)}) collective-permute-start(f32[392,128]{1,0:T(8,128)S(1)} %add.232), channel_id=1, source_target_pairs={{0,8},{8,16},{16,24},{24,28},{28,20},{20,12},{12,4},{4,0},{10,2},{... | collective-permute-start | bytes 602120 | tf_op jit(solution)/shard_map/ppermute | solution.py:293
  36.8 2.6 %collective-permute-done.8 = f32[392,128]{1,0:T(8,128)S(1)} collective-permute-done((f32[392,128]{1,0:T(8,128)S(1)}, f32[392,128]{1,0:T(8,128)S(1)}, u32[]{:S(2)}, u32[]{:S(2)}) %collective-permute-start.8) | collective-permute-done | bytes 200736 | tf_op jit(solution)/shard_map/ppermute | solution.py:293
  39.4 2.5 %collective-permute-start.9 = (f32[392,128]{1,0:T(8,128)S(1)}, f32[392,128]{1,0:T(8,128)S(1)}, u32[]{:S(2)}, u32[]{:S(2)}) collective-permute-start(f32[392,128]{1,0:T(8,128)S(1)} %add.233), channel_id=1, source_target_pairs={{0,8},{8,16},{16,24},{24,28},{28,20},{20,12},{12,4},{4,0},{10,2},{... | collective-permute-start | bytes 602120 | tf_op jit(solution)/shard_map/ppermute | solution.py:293
  43.7 2.5 %collective-permute-start.14 = (f32[392,128]{1,0:T(8,128)S(1)}, f32[392,128]{1,0:T(8,128)S(1)}, u32[]{:S(2)}, u32[]{:S(2)}) collective-permute-start(f32[392,128]{1,0:T(8,128)S(1)} %add.240), channel_id=1, source_target_pairs={{0,8},{8,16},{16,24},{24,28},{28,20},{20,12},{12,4},{4,0},{10,2},{... | collective-permute-start | bytes 602120 | tf_op jit(solution)/shard_map/ppermute | solution.py:293
  48.0 2.5 %collective-permute-start.10 = (f32[392,128]{1,0:T(8,128)S(1)}, f32[392,128]{1,0:T(8,128)S(1)}, u32[]{:S(2)}, u32[]{:S(2)}) collective-permute-start(f32[392,128]{1,0:T(8,128)S(1)} %add.234), channel_id=1, source_target_pairs={{0,8},{8,16},{16,24},{24,28},{28,20},{20,12},{12,4},{4,0},{10,2},{... | collective-permute-start | bytes 602120 | tf_op jit(solution)/shard_map/ppermute | solution.py:293
  52.3 2.5 %collective-permute-start.15 = (f32[392,128]{1,0:T(8,128)S(1)}, f32[392,128]{1,0:T(8,128)S(1)}, u32[]{:S(2)}, u32[]{:S(2)}) collective-permute-start(f32[392,128]{1,0:T(8,128)S(1)} %add.241), channel_id=1, source_target_pairs={{0,8},{8,16},{16,24},{24,28},{28,20},{20,12},{12,4},{4,0},{10,2},{... | collective-permute-start | bytes 602120 | tf_op jit(solution)/shard_map/ppermute | solution.py:293
  60.8 2.5 %collective-permute-start.27 = (f32[392,128]{1,0:T(8,128)S(1)}, f32[392,128]{1,0:T(8,128)}, u32[]{:S(2)}, u32[]{:S(2)}) collective-permute-start(f32[392,128]{1,0:T(8,128)S(1)} %add_add_fusion.refs_1_), channel_id=1, source_target_pairs={{0,8},{8,16},{16,24},{24,28},{28,20},{20,12},{12,4},{4,0},{10,2},{... | collective-permute-start | bytes 602120 | tf_op jit(solution)/shard_map/ppermute | solution.py:293
  63.3 2.1 %collective-permute-done.24.refs_12_ = f32[392,128]{1,0:T(8,128)S(1)} collective-permute-done((f32[392,128]{1,0:T(8,128)S(1)}, f32[392,128]{1,0:T(8,128)S(1)}, u32[]{:S(2)}, u32[]{:S(2)}) %collective-permute-start.24) | collective-permute-done | bytes 200736 | tf_op jit(solution)/shard_map/ppermute | solution.py:293
  65.4 2.0 %collective-permute-start.25 = (f32[392,128]{1,0:T(8,128)S(1)}, f32[392,128]{1,0:T(8,128)S(1)}, u32[]{:S(2)}, u32[]{:S(2)}) collective-permute-start(f32[392,128]{1,0:T(8,128)S(1)} %collective-permute-done.24.refs_12_), channel_id=1, source_target_pairs={{0,8},{8,16},{16,24},{24,28},{28,20},{20,12},{12,4},{4,0},{10,2},{... | collective-permute-start | bytes 602120 | tf_op jit(solution)/shard_map/ppermute | solution.py:293
  67.5 1.7 %collective-permute-done.19.refs_3_ = f32[392,128]{1,0:T(8,128)} collective-permute-done((f32[392,128]{1,0:T(8,128)S(1)}, f32[392,128]{1,0:T(8,128)}, u32[]{:S(2)}, u32[]{:S(2)}) %collective-permute-start.19) | collective-permute-done | bytes 200736 | tf_op jit(solution)/shard_map/ppermute | solution.py:293
  69.8 2.0 %collective-permute-start.28 = (f32[392,128]{1,0:T(8,128)}, f32[392,128]{1,0:T(8,128)S(1)}, u32[]{:S(2)}, u32[]{:S(2)}) collective-permute-start(f32[392,128]{1,0:T(8,128)} %collective-permute-done.27.refs_13_), channel_id=1, source_target_pairs={{0,8},{8,16},{16,24},{24,28},{28,20},{20,12},{12,4},{4,0},{10,2},{... | collective-permute-start | bytes 602120 | tf_op jit(solution)/shard_map/ppermute | solution.py:293
  71.9 1.9 %collective-permute-done.25.refs_10_ = f32[392,128]{1,0:T(8,128)S(1)} collective-permute-done((f32[392,128]{1,0:T(8,128)S(1)}, f32[392,128]{1,0:T(8,128)S(1)}, u32[]{:S(2)}, u32[]{:S(2)}) %collective-permute-start.25) | collective-permute-done | bytes 200736 | tf_op jit(solution)/shard_map/ppermute | solution.py:293
  73.8 2.2 %collective-permute-start.26 = (f32[392,128]{1,0:T(8,128)S(1)}, f32[392,128]{1,0:T(8,128)S(1)}, u32[]{:S(2)}, u32[]{:S(2)}) collective-permute-start(f32[392,128]{1,0:T(8,128)S(1)} %collective-permute-done.25.refs_10_), channel_id=1, source_target_pairs={{0,8},{8,16},{16,24},{24,28},{28,20},{20,12},{12,4},{4,0},{10,2},{... | collective-permute-start | bytes 602120 | tf_op jit(solution)/shard_map/ppermute | solution.py:293
  76.1 2.8 %collective-permute-done.21.refs_5_ = f32[392,128]{1,0:T(8,128)S(1)} collective-permute-done((f32[392,128]{1,0:T(8,128)}, f32[392,128]{1,0:T(8,128)S(1)}, u32[]{:S(2)}, u32[]{:S(2)}) %collective-permute-start.21) | collective-permute-done | bytes 200736 | tf_op jit(solution)/shard_map/ppermute | solution.py:293
  90.0 3.7 %half.1 = (f32[392,128]{1,0:T(8,128)S(1)}, f32[392,128]{1,0:T(8,128)S(1)}) custom-call(s32[11]{0:T(128)S(1)} %add_add_fusion.5.info, f32[196,3136]{1,0:T(8,128)S(1)} %copy-done.1, f32[196,3136]{1,0:T(8,128)S(1)} %copy-done.3, f32[392,128]{1,0:T(8,128)S(1)} %add_add_fusion.1.refs_0_, f32[392,128]{1,0:T(8,128)S(1)} %add_add_fusion.refs_1_, ...), custom_call_target="tpu_custom_call" | custom-call | flops 1888223232 | bytes 8128512 | tf_op jit(solution)/shard_map/half/pallas_call | solution.py:243
  107.6 1.8 %collective-permute-done.43 = f32[392,128]{1,0:T(8,128)S(1)} collective-permute-done((f32[392,128]{1,0:T(8,128)S(1)}, f32[392,128]{1,0:T(8,128)S(1)}, u32[]{:S(2)}, u32[]{:S(2)}) %collective-permute-start.43) | collective-permute-done | bytes 200736 | tf_op jit(solution)/shard_map/ppermute | solution.py:293
  109.9 1.8 %collective-permute-start.33 = (f32[392,128]{1,0:T(8,128)S(1)}, f32[392,128]{1,0:T(8,128)S(1)}, u32[]{:S(2)}, u32[]{:S(2)}) collective-permute-start(f32[392,128]{1,0:T(8,128)S(1)} %collective-permute-done.32), channel_id=1, source_target_pairs={{8,0},{16,8},{24,16},{28,24},{20,28},{12,20},{4,12},{0,4},{2,10},{... | collective-permute-start | bytes 602120 | tf_op jit(solution)/shard_map/ppermute | solution.py:293
  111.7 1.8 %collective-permute-done.40 = f32[392,128]{1,0:T(8,128)S(1)} collective-permute-done((f32[392,128]{1,0:T(8,128)S(1)}, f32[392,128]{1,0:T(8,128)S(1)}, u32[]{:S(2)}, u32[]{:S(2)}) %collective-permute-start.40) | collective-permute-done | bytes 200736 | tf_op jit(solution)/shard_map/ppermute | solution.py:293
  115.5 2.6 %collective-permute-done.44 = f32[392,128]{1,0:T(8,128)S(1)} collective-permute-done((f32[392,128]{1,0:T(8,128)S(1)}, f32[392,128]{1,0:T(8,128)S(1)}, u32[]{:S(2)}, u32[]{:S(2)}) %collective-permute-start.44) | collective-permute-done | bytes 200736 | tf_op jit(solution)/shard_map/ppermute | solution.py:293
  119.8 2.3 %collective-permute-done.41 = f32[392,128]{1,0:T(8,128)S(1)} collective-permute-done((f32[392,128]{1,0:T(8,128)S(1)}, f32[392,128]{1,0:T(8,128)S(1)}, u32[]{:S(2)}, u32[]{:S(2)}) %collective-permute-start.41) | collective-permute-done | bytes 200736 | tf_op jit(solution)/shard_map/ppermute | solution.py:293
  122.9 2.1 %collective-permute-done.45 = f32[392,128]{1,0:T(8,128)S(1)} collective-permute-done((f32[392,128]{1,0:T(8,128)S(1)}, f32[392,128]{1,0:T(8,128)S(1)}, u32[]{:S(2)}, u32[]{:S(2)}) %collective-permute-start.45) | collective-permute-done | bytes 200736 | tf_op jit(solution)/shard_map/ppermute | solution.py:293
  125.0 10.0 %qpartial.1 = f32[64,256]{1,0:T(8,128)S(1)} custom-call(s32[11]{0:T(128)S(1)} %add_add_fusion.5.info, f32[56,512,128]{2,1,0:T(8,128)} %three.5, s32[8,32]{1,0:T(8,128)S(1)} %bitcast.89, f32[56,256,128]{2,1,0:T(8,128)} %collective-permute-done.7.sib, f32[7,56,128]{2,1,0:T(8,128)S(1)} %bitcast.70, f32[7,56,128]{2,1,0:T(8,128)S(1)} %bitcast.75, ...), custom_call_target="tpu_custom_call" | custom-call | flops 1233125376 | bytes 17891328 | tf_op jit(solution)/shard_map/qpartial/pallas_call | solution.py:176
  137.1 2.5 %collective-permute-start.52 = (f32[112,128]{1,0:T(8,128)S(1)}, f32[112,128]{1,0:T(8,128)S(1)}, u32[]{:S(2)}, u32[]{:S(2)}) collective-permute-start(f32[112,128]{1,0:T(8,128)S(1)} %add.264), channel_id=1, source_target_pairs={{0,5},{1,4},{2,7},{3,6},{4,1},{5,0},{6,3},{7,2},{8,13},{9,12},{10,... | collective-permute-start | bytes 172040 | tf_op jit(solution)/shard_map/ppermute | solution.py:357
  144.3 2.9 %collective-permute-start.55 = (f32[112,128]{1,0:T(8,128)S(1)}, f32[112,128]{1,0:T(8,128)S(1)}, u32[]{:S(2)}, u32[]{:S(2)}) collective-permute-start(f32[112,128]{1,0:T(8,128)S(1)} %add_add_fusion.3), channel_id=1, source_target_pairs={{0,24},{1,25},{2,26},{3,27},{4,28},{5,29},{6,30},{7,31},{8,16},{9,... | collective-permute-start | bytes 172040 | tf_op jit(solution)/shard_map/ppermute | solution.py:357
  150.5 1.9 %collective-permute-done.54 = f32[112,128]{1,0:T(8,128)S(1)} collective-permute-done((f32[112,128]{1,0:T(8,128)S(1)}, f32[112,128]{1,0:T(8,128)S(1)}, u32[]{:S(2)}, u32[]{:S(2)}) %collective-permute-start.54) | collective-permute-done | bytes 57376 | tf_op jit(solution)/shard_map/ppermute | solution.py:357
  (165 shorter events, 63.2 us)
Async XLA Ops:
  0.0 15.8 %collective-permute-start.2 = (f32[196,3136]{1,0:T(8,128)}, f32[196,3136]{1,0:T(8,128)S(1)}, u32[]{:S(2)}, u32[]{:S(2)}) collective-permute-start(f32[196,3136]{1,0:T(8,128)} %own.1), channel_id=1, source_target_pairs={{0,2},{2,0},{4,6},{6,4},{8,10},{10,8},{12,14},{14,12},{16,18},{18,... | collective-permute-start | bytes 7375880 | tf_op jit(solution)/shard_map/ppermute | solution.py:293
  19.3 13.4 %collective-permute-start.7 = (f32[56,256,128]{2,1,0:T(8,128)S(1)}, f32[56,256,128]{2,1,0:T(8,128)}, u32[]{:S(2)}, u32[]{:S(2)}) collective-permute-start(f32[56,256,128]{2,1,0:T(8,128)S(1)} %bitcast.93), channel_id=1, source_target_pairs={{0,2},{2,0},{4,6},{6,4},{8,10},{10,8},{12,14},{14,12},{16,18},{18,... | collective-permute-start | bytes 22020104 | tf_op jit(solution)/shard_map/ppermute | solution.py:293
  19.7 8.8 %collective-permute-start.3 = (f32[392,128]{1,0:T(8,128)S(1)}, f32[392,128]{1,0:T(8,128)S(1)}, u32[]{:S(2)}, u32[]{:S(2)}) collective-permute-start(f32[392,128]{1,0:T(8,128)S(1)} %get-tuple-element.49), channel_id=1, source_target_pairs={{0,8},{8,16},{16,24},{24,28},{28,20},{20,12},{12,4},{4,0},{10,2},{... | collective-permute-start | bytes 602120 | tf_op jit(solution)/shard_map/ppermute | solution.py:293
  23.1 8.8 %collective-permute-start.5 = (f32[392,128]{1,0:T(8,128)S(1)}, f32[392,128]{1,0:T(8,128)S(1)}, u32[]{:S(2)}, u32[]{:S(2)}) collective-permute-start(f32[392,128]{1,0:T(8,128)S(1)} %get-tuple-element.51), channel_id=1, source_target_pairs={{0,8},{8,16},{16,24},{24,28},{28,20},{20,12},{12,4},{4,0},{10,2},{... | collective-permute-start | bytes 602120 | tf_op jit(solution)/shard_map/ppermute | solution.py:293
  34.7 9.0 %collective-permute-start.13 = (f32[392,128]{1,0:T(8,128)S(1)}, f32[392,128]{1,0:T(8,128)S(1)}, u32[]{:S(2)}, u32[]{:S(2)}) collective-permute-start(f32[392,128]{1,0:T(8,128)S(1)} %add.239), channel_id=1, source_target_pairs={{0,8},{8,16},{16,24},{24,28},{28,20},{20,12},{12,4},{4,0},{10,2},{... | collective-permute-start | bytes 602120 | tf_op jit(solution)/shard_map/ppermute | solution.py:293
  36.3 9.9 %collective-permute-start.11 = (f32[392,128]{1,0:T(8,128)S(1)}, f32[392,128]{1,0:T(8,128)S(1)}, u32[]{:S(2)}, u32[]{:S(2)}) collective-permute-start(f32[392,128]{1,0:T(8,128)S(1)} %add.236), channel_id=1, source_target_pairs={{8,0},{16,8},{24,16},{28,24},{20,28},{12,20},{4,12},{0,4},{2,10},{... | collective-permute-start | bytes 602120 | tf_op jit(solution)/shard_map/ppermute | solution.py:293
  39.4 8.6 %collective-permute-start.9 = (f32[392,128]{1,0:T(8,128)S(1)}, f32[392,128]{1,0:T(8,128)S(1)}, u32[]{:S(2)}, u32[]{:S(2)}) collective-permute-start(f32[392,128]{1,0:T(8,128)S(1)} %add.233), channel_id=1, source_target_pairs={{0,8},{8,16},{16,24},{24,28},{28,20},{20,12},{12,4},{4,0},{10,2},{... | collective-permute-start | bytes 602120 | tf_op jit(solution)/shard_map/ppermute | solution.py:293
  42.0 8.6 %collective-permute-start.16 = (f32[392,128]{1,0:T(8,128)S(1)}, f32[392,128]{1,0:T(8,128)S(1)}, u32[]{:S(2)}, u32[]{:S(2)}) collective-permute-start(f32[392,128]{1,0:T(8,128)S(1)} %add.243), channel_id=1, source_target_pairs={{8,0},{16,8},{24,16},{28,24},{20,28},{12,20},{4,12},{0,4},{2,10},{... | collective-permute-start | bytes 602120 | tf_op jit(solution)/shard_map/ppermute | solution.py:293
  43.7 8.6 %collective-permute-start.14 = (f32[392,128]{1,0:T(8,128)S(1)}, f32[392,128]{1,0:T(8,128)S(1)}, u32[]{:S(2)}, u32[]{:S(2)}) collective-permute-start(f32[392,128]{1,0:T(8,128)S(1)} %add.240), channel_id=1, source_target_pairs={{0,8},{8,16},{16,24},{24,28},{28,20},{20,12},{12,4},{4,0},{10,2},{... | collective-permute-start | bytes 602120 | tf_op jit(solution)/shard_map/ppermute | solution.py:293
  46.3 8.5 %collective-permute-start.12 = (f32[392,128]{1,0:T(8,128)S(1)}, f32[392,128]{1,0:T(8,128)S(1)}, u32[]{:S(2)}, u32[]{:S(2)}) collective-permute-start(f32[392,128]{1,0:T(8,128)S(1)} %add.237), channel_id=1, source_target_pairs={{8,0},{16,8},{24,16},{28,24},{20,28},{12,20},{4,12},{0,4},{2,10},{... | collective-permute-start | bytes 602120 | tf_op jit(solution)/shard_map/ppermute | solution.py:293
  48.0 8.4 %collective-permute-start.10 = (f32[392,128]{1,0:T(8,128)S(1)}, f32[392,128]{1,0:T(8,128)S(1)}, u32[]{:S(2)}, u32[]{:S(2)}) collective-permute-start(f32[392,128]{1,0:T(8,128)S(1)} %add.234), channel_id=1, source_target_pairs={{0,8},{8,16},{16,24},{24,28},{28,20},{20,12},{12,4},{4,0},{10,2},{... | collective-permute-start | bytes 602120 | tf_op jit(solution)/shard_map/ppermute | solution.py:293
  50.6 8.4 %collective-permute-start.17 = (f32[392,128]{1,0:T(8,128)S(1)}, f32[392,128]{1,0:T(8,128)S(1)}, u32[]{:S(2)}, u32[]{:S(2)}) collective-permute-start(f32[392,128]{1,0:T(8,128)S(1)} %add.244), channel_id=1, source_target_pairs={{8,0},{16,8},{24,16},{28,24},{20,28},{12,20},{4,12},{0,4},{2,10},{... | collective-permute-start | bytes 602120 | tf_op jit(solution)/shard_map/ppermute | solution.py:293
  52.3 8.4 %collective-permute-start.15 = (f32[392,128]{1,0:T(8,128)S(1)}, f32[392,128]{1,0:T(8,128)S(1)}, u32[]{:S(2)}, u32[]{:S(2)}) collective-permute-start(f32[392,128]{1,0:T(8,128)S(1)} %add.241), channel_id=1, source_target_pairs={{0,8},{8,16},{16,24},{24,28},{28,20},{20,12},{12,4},{4,0},{10,2},{... | collective-permute-start | bytes 602120 | tf_op jit(solution)/shard_map/ppermute | solution.py:293
  56.4 11.0 %collective-permute-start.18 = (f32[392,128]{1,0:T(8,128)S(1)}, f32[392,128]{1,0:T(8,128)S(1)}, u32[]{:S(2)}, u32[]{:S(2)}) collective-permute-start(f32[392,128]{1,0:T(8,128)S(1)} %add_add_fusion.1.refs_0_), channel_id=1, source_target_pairs={{8,0},{16,8},{24,16},{28,24},{20,28},{12,20},{4,12},{0,4},{2,10},{... | collective-permute-start | bytes 602120 | tf_op jit(solution)/shard_map/ppermute | solution.py:293
  57.5 7.9 %collective-permute-start.24 = (f32[392,128]{1,0:T(8,128)S(1)}, f32[392,128]{1,0:T(8,128)S(1)}, u32[]{:S(2)}, u32[]{:S(2)}) collective-permute-start(f32[392,128]{1,0:T(8,128)S(1)} %add_add_fusion.1.refs_0_), channel_id=1, source_target_pairs={{0,8},{8,16},{16,24},{24,28},{28,20},{20,12},{12,4},{4,0},{10,2},{... | collective-permute-start | bytes 602120 | tf_op jit(solution)/shard_map/ppermute | solution.py:293
  60.7 8.5 %collective-permute-start.19 = (f32[392,128]{1,0:T(8,128)S(1)}, f32[392,128]{1,0:T(8,128)}, u32[]{:S(2)}, u32[]{:S(2)}) collective-permute-start(f32[392,128]{1,0:T(8,128)S(1)} %add_add_fusion.refs_1_), channel_id=1, source_target_pairs={{8,0},{16,8},{24,16},{28,24},{20,28},{12,20},{4,12},{0,4},{2,10},{... | collective-permute-start | bytes 602120 | tf_op jit(solution)/shard_map/ppermute | solution.py:293
  60.8 9.0 %collective-permute-start.27 = (f32[392,128]{1,0:T(8,128)S(1)}, f32[392,128]{1,0:T(8,128)}, u32[]{:S(2)}, u32[]{:S(2)}) collective-permute-start(f32[392,128]{1,0:T(8,128)S(1)} %add_add_fusion.refs_1_), channel_id=1, source_target_pairs={{0,8},{8,16},{16,24},{24,28},{28,20},{20,12},{12,4},{4,0},{10,2},{... | collective-permute-start | bytes 602120 | tf_op jit(solution)/shard_map/ppermute | solution.py:293
  65.4 8.4 %collective-permute-start.25 = (f32[392,128]{1,0:T(8,128)S(1)}, f32[392,128]{1,0:T(8,128)S(1)}, u32[]{:S(2)}, u32[]{:S(2)}) collective-permute-start(f32[392,128]{1,0:T(8,128)S(1)} %collective-permute-done.24.refs_12_), channel_id=1, source_target_pairs={{0,8},{8,16},{16,24},{24,28},{28,20},{20,12},{12,4},{4,0},{10,2},{... | collective-permute-start | bytes 602120 | tf_op jit(solution)/shard_map/ppermute | solution.py:293
  67.5 8.7 %collective-permute-start.20 = (f32[392,128]{1,0:T(8,128)S(1)}, f32[392,128]{1,0:T(8,128)S(1)}, u32[]{:S(2)}, u32[]{:S(2)}) collective-permute-start(f32[392,128]{1,0:T(8,128)S(1)} %collective-permute-done.18.refs_2_), channel_id=1, source_target_pairs={{8,0},{16,8},{24,16},{28,24},{20,28},{12,20},{4,12},{0,4},{2,10},{... | collective-permute-start | bytes 602120 | tf_op jit(solution)/shard_map/ppermute | solution.py:293
  69.2 9.8 %collective-permute-start.21 = (f32[392,128]{1,0:T(8,128)}, f32[392,128]{1,0:T(8,128)S(1)}, u32[]{:S(2)}, u32[]{:S(2)}) collective-permute-start(f32[392,128]{1,0:T(8,128)} %collective-permute-done.19.refs_3_), channel_id=1, source_target_pairs={{8,0},{16,8},{24,16},{28,24},{20,28},{12,20},{4,12},{0,4},{2,10},{... | collective-permute-start | bytes 602120 | tf_op jit(solution)/shard_map/ppermute | solution.py:293
  69.8 9.9 %collective-permute-start.28 = (f32[392,128]{1,0:T(8,128)}, f32[392,128]{1,0:T(8,128)S(1)}, u32[]{:S(2)}, u32[]{:S(2)}) collective-permute-start(f32[392,128]{1,0:T(8,128)} %collective-permute-done.27.refs_13_), channel_id=1, source_target_pairs={{0,8},{8,16},{16,24},{24,28},{28,20},{20,12},{12,4},{4,0},{10,2},{... | collective-permute-start | bytes 602120 | tf_op jit(solution)/shard_map/ppermute | solution.py:293
  73.8 7.9 %collective-permute-start.26 = (f32[392,128]{1,0:T(8,128)S(1)}, f32[392,128]{1,0:T(8,128)S(1)}, u32[]{:S(2)}, u32[]{:S(2)}) collective-permute-start(f32[392,128]{1,0:T(8,128)S(1)} %collective-permute-done.25.refs_10_), channel_id=1, source_target_pairs={{0,8},{8,16},{16,24},{24,28},{28,20},{20,12},{12,4},{4,0},{10,2},{... | collective-permute-start | bytes 602120 | tf_op jit(solution)/shard_map/ppermute | solution.py:293
  76.1 10.6 %collective-permute-start.22 = (f32[392,128]{1,0:T(8,128)S(1)}, f32[392,128]{1,0:T(8,128)S(1)}, u32[]{:S(2)}, u32[]{:S(2)}) collective-permute-start(f32[392,128]{1,0:T(8,128)S(1)} %collective-permute-done.20.refs_4_), channel_id=1, source_target_pairs={{8,0},{16,8},{24,16},{28,24},{20,28},{12,20},{4,12},{0,4},{2,10},{... | collective-permute-start | bytes 602120 | tf_op jit(solution)/shard_map/ppermute | solution.py:293
  79.0 9.2 %collective-permute-start.23 = (f32[392,128]{1,0:T(8,128)S(1)}, f32[392,128]{1,0:T(8,128)S(1)}, u32[]{:S(2)}, u32[]{:S(2)}) collective-permute-start(f32[392,128]{1,0:T(8,128)S(1)} %collective-permute-done.21.refs_5_), channel_id=1, source_target_pairs={{8,0},{16,8},{24,16},{28,24},{20,28},{12,20},{4,12},{0,4},{2,10},{... | collective-permute-start | bytes 602120 | tf_op jit(solution)/shard_map/ppermute | solution.py:293
  81.7 12.0 %collective-permute-start.30 = (f32[392,128]{1,0:T(8,128)S(1)}, f32[392,128]{1,0:T(8,128)S(1)}, u32[]{:S(2)}, u32[]{:S(2)}) collective-permute-start(f32[392,128]{1,0:T(8,128)S(1)} %collective-permute-done.26.refs_8_), channel_id=1, source_target_pairs={{0,8},{8,16},{16,24},{24,28},{28,20},{20,12},{12,4},{4,0},{10,2},{... | collective-permute-start | bytes 602120 | tf_op jit(solution)/shard_map/ppermute | solution.py:293
  85.4 9.8 %collective-permute-start.38 = (f32[392,128]{1,0:T(8,128)S(1)}, f32[392,128]{1,0:T(8,128)S(1)}, u32[]{:S(2)}, u32[]{:S(2)}) collective-permute-start(f32[392,128]{1,0:T(8,128)S(1)} %collective-permute-done.29.refs_9_), channel_id=1, source_target_pairs={{0,8},{8,16},{16,24},{24,28},{28,20},{20,12},{12,4},{4,0},{10,2},{... | collective-permute-start | bytes 602120 | tf_op jit(solution)/shard_map/ppermute | solution.py:293
  103.1 32.7 %collective-permute-start.48 = (f32[128,200]{1,0:T(8,128)S(1)}, f32[128,200]{1,0:T(8,128)S(1)}, u32[]{:S(2)}, u32[]{:S(2)}) collective-permute-start(f32[128,200]{1,0:T(8,128)S(1)} %add_multiply_fusion), channel_id=1, source_target_pairs={{0,2},{2,0},{4,6},{6,4},{8,10},{10,8},{12,14},{14,12},{16,18},{18,... | collective-permute-start | bytes 307208 | tf_op jit(solution)/shard_map/ppermute | solution.py:293
  105.5 8.0 %collective-permute-start.40 = (f32[392,128]{1,0:T(8,128)S(1)}, f32[392,128]{1,0:T(8,128)S(1)}, u32[]{:S(2)}, u32[]{:S(2)}) collective-permute-start(f32[392,128]{1,0:T(8,128)S(1)} %collective-permute-done.39), channel_id=1, source_target_pairs={{8,0},{16,8},{24,16},{28,24},{20,28},{12,20},{4,12},{0,4},{2,10},{... | collective-permute-start | bytes 602120 | tf_op jit(solution)/shard_map/ppermute | solution.py:293
  105.9 9.1 %collective-permute-start.36 = (f32[392,128]{1,0:T(8,128)S(1)}, f32[392,128]{1,0:T(8,128)S(1)}, u32[]{:S(2)}, u32[]{:S(2)}) collective-permute-start(f32[392,128]{1,0:T(8,128)S(1)} %collective-permute-done.35), channel_id=1, source_target_pairs={{0,8},{8,16},{16,24},{24,28},{28,20},{20,12},{12,4},{4,0},{10,2},{... | collective-permute-start | bytes 602120 | tf_op jit(solution)/shard_map/ppermute | solution.py:293
  109.4 8.8 %collective-permute-start.44 = (f32[392,128]{1,0:T(8,128)S(1)}, f32[392,128]{1,0:T(8,128)S(1)}, u32[]{:S(2)}, u32[]{:S(2)}) collective-permute-start(f32[392,128]{1,0:T(8,128)S(1)} %collective-permute-done.43), channel_id=1, source_target_pairs={{0,8},{8,16},{16,24},{24,28},{28,20},{20,12},{12,4},{4,0},{10,2},{... | collective-permute-start | bytes 602120 | tf_op jit(solution)/shard_map/ppermute | solution.py:293
  109.9 9.9 %collective-permute-start.33 = (f32[392,128]{1,0:T(8,128)S(1)}, f32[392,128]{1,0:T(8,128)S(1)}, u32[]{:S(2)}, u32[]{:S(2)}) collective-permute-start(f32[392,128]{1,0:T(8,128)S(1)} %collective-permute-done.32), channel_id=1, source_target_pairs={{8,0},{16,8},{24,16},{28,24},{20,28},{12,20},{4,12},{0,4},{2,10},{... | collective-permute-start | bytes 602120 | tf_op jit(solution)/shard_map/ppermute | solution.py:293
  113.5 8.6 %collective-permute-start.41 = (f32[392,128]{1,0:T(8,128)S(1)}, f32[392,128]{1,0:T(8,128)S(1)}, u32[]{:S(2)}, u32[]{:S(2)}) collective-permute-start(f32[392,128]{1,0:T(8,128)S(1)} %collective-permute-done.40), channel_id=1, source_target_pairs={{8,0},{16,8},{24,16},{28,24},{20,28},{12,20},{4,12},{0,4},{2,10},{... | collective-permute-start | bytes 602120 | tf_op jit(solution)/shard_map/ppermute | solution.py:293
  (37 other events, 420.7 us)
